TPU v7x, 32 devices: a whole 2x2x4 slice. The times are simulated.
32 devices in a mesh: pair: 2 (over x), src: 16 (over z, y, core).
Axes of the slice: x: 2, y: 2, z: 4, core: 2. Of those that a mesh axis runs over, the one named last changes fastest.
Arguments:
- source_feat: bfloat16 [1024, 256], P(('pair', 'src')), parts along dimension 0, may hold values from -6 to 6
- target_feat: bfloat16 [1024, 64, 256], P(('pair', 'src')), parts along dimension 0, may hold values from -6 to 6
- conv_weight: bfloat16 [64, 64], replicated, may hold values from -0.75 to 0.75
- conv_bias: float32 [64], replicated, may hold values from -3 to 3
- proj_weight: bfloat16 [64, 64], replicated, may hold values from -0.75 to 0.75
Outputs:
- cost_tokens: bfloat16 [1024, 32768], P(('pair', 'src')), parts along dimension 0
There are 2 independent parts, one for each index of `pair`. A program takes and returns all parts, laid end to end along the dimension named above; an argument that names none is the same for every part. Nothing has to cross between parts.
All inputs are finite; a program needn't handle non-finite values.
Results may differ from a plain program's by a relative error of at most 0.0051.
Values may be sent and summed in bfloat16 or wider, within the bound.
No kernel may reach another device: no remote copies, remote signals or barrier semaphores. Data moves between devices by JAX's collectives and lax.ppermute only.
A program may use at most 128 MiB of HBM per device.

v0:
```python
import jax
import jax.numpy as jnp
from jax import lax
from jax.sharding import PartitionSpec as P


def per_device(source_feat, target_feat, conv_weight, conv_bias, proj_weight):
    chans = target_feat.shape[2]
    cells = target_feat.shape[1]
    patched = target_feat.reshape(-1, chans)
    scale = chans ** (-0.5)

    def embed_cost(cost):
        count = cost.shape[0]
        flat = cost.reshape(-1, cells)
        embedded = jnp.dot(flat, conv_weight, preferred_element_type=jnp.float32) + conv_bias
        hidden = jax.nn.gelu(embedded, approximate=False).astype(jnp.bfloat16)
        result = embedded + jnp.dot(hidden, proj_weight, preferred_element_type=jnp.float32)
        return result.astype(jnp.bfloat16).reshape(count, -1)

    cost = lax.dot_general(
        lax.all_gather(source_feat, "src", axis=0, tiled=True),
        patched,
        (((1,), (1,)), ((), ())),
        preferred_element_type=jnp.float32,
    )
    local_rows = embed_cost((cost * scale).astype(jnp.bfloat16))
    return lax.all_to_all(local_rows, "src", split_axis=0, concat_axis=1, tiled=True)


def solution(mesh):
    in_specs = (P(("pair", "src"), None), P(("pair", "src"), None, None), P(), P(), P())
    out_specs = P(("pair", "src"), None)
    return jax.shard_map(
        per_device, mesh=mesh, in_specs=in_specs, out_specs=out_specs, check_vma=False
    )
```

profile of v0, /device:TPU:0, one launch (start us, length us, event | category | flops | bytes accessed | tf_op | source)
XLA Modules:
  0.0 104.0 jit_solution(13310065887691339308)
XLA Ops:
  0.0 0.0 copy-start
  0.0 24.2 %all_gather.3 = bf16[512,256]{1,0:T(8,128)(2,1)S(1)} all-gather(bf16[32,256]{1,0:T(8,128)(2,1)} %param.5), channel_id=1, replica_groups=mesh['pair'=2,'src'=16] {'src'}, dimensions={0}, use_global_device_ids=true | all-gather | bytes 278528 | tf_op jit(solution)/shard_map/all_gather | solution.py:22
  24.2 0.0 copy-done
  24.2 0.0 copy-start.1
  24.2 0.0 copy-start.2
  24.2 0.7 multiply_convert_fusion
  24.9 5.3 %reshape.13 = bf16[16384,64]{1,0:T(8,128)(2,1)} reshape(bf16[512,2048]{1,0:T(8,128)(2,1)S(1)} %multiply_convert_fusion) | data formatting | bytes 4194304 | tf_op jit(solution)/shard_map/reshape | solution.py:15
  30.3 0.0 copy-done.1
  30.3 0.0 copy-done.2
  30.3 0.0 copy-start.3
  30.3 3.8 %convolution_add_fusion.1 = f32[16384,64]{0,1:T(8,128)S(1)} fusion(bf16[16384,64]{1,0:T(8,128)(2,1)} %reshape.13, bf16[64,64]{1,0:T(8,128)(2,1)S(1)} %copy-done.1, f32[64]{0:T(128)S(1)} %copy-done.2), kind=kOutput, calls=%fused_computation.1 | convolution fusion | flops 135266304 | bytes 6299904 | tf_op jit(solution)/shard_map/dot_general | solution.py:16
  34.1 0.0 copy-done.3
  34.1 9.6 %fusion = bf16[16384,64]{0,1:T(8,128)(2,1)S(1)} fusion(f32[16384,64]{0,1:T(8,128)S(1)} %convolution_add_fusion.1, bf16[64,64]{1,0:T(8,128)(2,1)S(1)} %copy-done.3), kind=kOutput, calls=%fused_computation.2 | convolution fusion | flops 204472320 | bytes 6299648 | tf_op jit(solution)/shard_map/dot_general | solution.py:18
  43.7 3.2 %copy.7 = bf16[16384,64]{1,0:T(8,128)(2,1)} copy(bf16[16384,64]{0,1:T(8,128)(2,1)S(1)} %fusion) | data formatting | bytes 4194304 | tf_op jit(solution)/shard_map/convert_element_type | solution.py:19
  46.9 5.8 %all_to_all.14 = bf16[16,32,2048]{2,1,0:T(8,128)(2,1)S(1)} reshape(bf16[16384,64]{1,0:T(8,128)(2,1)} %copy.7) | data formatting | bytes 4194304 | tf_op jit(solution)/shard_map/all_to_all | solution.py:28
  52.7 49.9 %all_to_all.19 = bf16[16,32,2048]{2,1,0:T(8,128)(2,1)S(1)} all-to-all(bf16[16,32,2048]{2,1,0:T(8,128)(2,1)S(1)} %all_to_all.14), channel_id=1, replica_groups=mesh['pair'=2,'src'=16] {'src'}, dimensions={0} | all-to-all | bytes 4194304 | tf_op jit(solution)/shard_map/all_to_all | solution.py:28
  102.6 1.5 %copy.9 = bf16[16,4,8,2048]{3,2,0,1:T(8,128)(2,1)} copy(bf16[16,4,8,2048]{3,2,1,0:T(8,128)(2,1)S(1)} %bitcast.10) | data formatting | bytes 4194304 | tf_op jit(solution)/shard_map/all_to_all | solution.py:28
Async XLA Ops:
  0.0 24.2 %copy-start = (bf16[32,64,256]{2,1,0:T(8,128)(2,1)S(1)}, bf16[32,64,256]{2,1,0:T(8,128)(2,1)}, u32[]{:S(2)}) copy-start(bf16[32,64,256]{2,1,0:T(8,128)(2,1)} %param.6) | copy-start | bytes 3145732
  24.2 6.1 %copy-start.1 = (bf16[64,64]{1,0:T(8,128)(2,1)S(1)}, bf16[64,64]{1,0:T(8,128)(2,1)}, u32[]{:S(2)}) copy-start(bf16[64,64]{1,0:T(8,128)(2,1)} %param.7) | copy-start | bytes 24580
  24.2 6.1 %copy-start.2 = (f32[64]{0:T(128)S(1)}, f32[64]{0:T(128)}, u32[]{:S(2)}) copy-start(f32[64]{0:T(128)} %param.8) | copy-start | bytes 772
  30.3 3.8 %copy-start.3 = (bf16[64,64]{1,0:T(8,128)(2,1)S(1)}, bf16[64,64]{1,0:T(8,128)(2,1)}, u32[]{:S(2)}) copy-start(bf16[64,64]{1,0:T(8,128)(2,1)} %param.9) | copy-start | bytes 24580
where the time goes:
time: 105 us; the launch traced here: 104 us
  blocking collectives  74.1 us (71%)
  local copies, waits for them, and re-layouts  15.7 us (15%)
  matrix products  14.2 us (14%)
    all_to_all x1, blocking collectives, per_device(): lax.all_to_all(local_rows, 'src', split_axis=0, concat_axis=1, tiled=True)  49.9 us
    all_gather x1, blocking collectives, per_device(): lax.all_gather(source_feat, 'src', axis=0, tiled=True)  24.2 us
    dot_general x1, matrix products, embed_cost(): jnp.dot(hidden, proj_weight, preferred_element_type=jnp.float32)  9.61 us
    all_to_all x2, local copies, waits for them, and re-layouts, per_device(): lax.all_to_all(local_rows, 'src', split_axis=0, concat_axis=1, tiled=True)  7.21 us
    reshape x1, local copies, waits for them, and re-layouts, embed_cost(): flat = cost.reshape(-1, cells)  5.34 us
    dot_general x1, matrix products, embed_cost(): jnp.dot(flat, conv_weight, preferred_element_type=jnp.float32) + conv_bias  3.82 us
    convert_element_type x1, local copies, waits for them, and re-layouts, embed_cost(): return result.astype(jnp.bfloat16).reshape(count, -1)  3.17 us

commit v1 on v0

v1 whole, which is shorter than its diff:
```python
import functools

import jax
import jax.numpy as jnp
from jax import lax
from jax.experimental import pallas as pl
from jax.experimental.pallas import tpu as pltpu
from jax.sharding import PartitionSpec as P

WIDE = 256
COVER = 40
PARAMS = pltpu.CompilerParams(vmem_limit_bytes=20 << 20)
SMALL = pltpu.CompilerParams(vmem_limit_bytes=4 << 20)
SWAP_NUM, SWAP_DEN = 1, 2


def gelu(x):
    return x * (lax.erf(x * 0.7071067811865476) * 0.5 + 0.5)


def block_tokens(source, target, w_ref, b_ref, p_ref, scale):
    cost = lax.dot_general(
        source, target, (((1,), (1,)), ((), ())), preferred_element_type=jnp.float32
    )
    cost = (cost * scale).astype(jnp.bfloat16)
    embedded = jnp.dot(cost, w_ref[...], preferred_element_type=jnp.float32) + b_ref[...]
    hidden = gelu(embedded).astype(jnp.bfloat16)
    out = embedded + jnp.dot(hidden, p_ref[...], preferred_element_type=jnp.float32)
    return out.astype(jnp.bfloat16)


def widen_kernel(w_ref, b_ref, p_ref, ww_ref, wb_ref, wp_ref):
    cells, emb = w_ref.shape
    ww_ref[...] = jnp.zeros_like(ww_ref)
    wp_ref[...] = jnp.zeros_like(wp_ref)
    for i in range(WIDE // cells):
        ww_ref[i * cells:(i + 1) * cells, i * emb:(i + 1) * emb] = w_ref[...]
        wp_ref[i * emb:(i + 1) * emb, i * emb:(i + 1) * emb] = p_ref[...]
        wb_ref[:, i * emb:(i + 1) * emb] = b_ref[...]


def widen(conv_weight, conv_bias, proj_weight):
    return pl.pallas_call(
        widen_kernel,
        out_shape=[
            jax.ShapeDtypeStruct((WIDE, WIDE), conv_weight.dtype),
            jax.ShapeDtypeStruct((1, WIDE), conv_bias.dtype),
            jax.ShapeDtypeStruct((WIDE, WIDE), proj_weight.dtype),
        ],
        compiler_params=SMALL,
    )(conv_weight, conv_bias[None, :], proj_weight)


def far_kernel(src_ref, tgt_ref, w_ref, b_ref, p_ref, out_ref, *, scale):
    out_ref[...] = block_tokens(src_ref[...], tgt_ref[...], w_ref, b_ref, p_ref, scale)


def cost_of(px, cols, chans):
    return pl.CostEstimate(
        flops=COVER * 2 * px * cols * (chans + 2 * WIDE),
        bytes_accessed=2 * px * cols + 2 * cols * chans,
        transcendentals=px * cols,
    )


def direct_tokens(source, patched, first, wide, scale):
    px, chans = source.shape
    cols = patched.shape[0] - first
    skip = first // WIDE
    return pl.pallas_call(
        functools.partial(far_kernel, scale=scale),
        grid=(cols // WIDE,),
        in_specs=[
            pl.BlockSpec((px, chans), lambda i: (0, 0)),
            pl.BlockSpec((WIDE, chans), lambda i: (i + skip, 0)),
            pl.BlockSpec((WIDE, WIDE), lambda i: (0, 0)),
            pl.BlockSpec((1, WIDE), lambda i: (0, 0)),
            pl.BlockSpec((WIDE, WIDE), lambda i: (0, 0)),
        ],
        out_specs=pl.BlockSpec((px, WIDE), lambda i: (0, i)),
        out_shape=jax.ShapeDtypeStruct((px, cols), jnp.bfloat16),
        compiler_params=PARAMS,
        cost_estimate=cost_of(px, cols, chans),
    )(source, patched, *wide)


def near_kernel(src_ref, own_ref, got_ref, w_ref, b_ref, p_ref, *rest, scale, s_dev, own_steps):
    outs, rows_ref = rest[:-1], rest[-1]
    group = len(outs)
    step = pl.program_id(0)

    @pl.when(step == 0)
    def _():
        me = lax.axis_index("src")
        lane = lax.rem(me, group)
        base = me - lane
        for k in range(group):
            to = base + lax.rem(lane + k, group)
            rows_ref[k * s_dev:(k + 1) * s_dev, :] = src_ref[
                pl.ds(pl.multiple_of(to * s_dev, s_dev), s_dev), :
            ]

    target = jnp.where(step < own_steps, own_ref[...], got_ref[...])
    tok = block_tokens(rows_ref[...], target, w_ref, b_ref, p_ref, scale)
    for k in range(group):
        outs[k][...] = tok[k * s_dev:(k + 1) * s_dev, :]


def near_tokens(source, patched, got, s_dev, group, wide, scale):
    px, chans = source.shape
    rows = got.shape[0]
    steps = rows // WIDE
    return pl.pallas_call(
        functools.partial(near_kernel, scale=scale, s_dev=s_dev, own_steps=steps),
        grid=(2 * steps,),
        in_specs=[
            pl.BlockSpec((px, chans), lambda i: (0, 0)),
            pl.BlockSpec((WIDE, chans), lambda i: (jnp.minimum(i, steps - 1), 0)),
            pl.BlockSpec((WIDE, chans), lambda i: (jnp.maximum(i - steps, 0), 0)),
            pl.BlockSpec((WIDE, WIDE), lambda i: (0, 0)),
            pl.BlockSpec((1, WIDE), lambda i: (0, 0)),
            pl.BlockSpec((WIDE, WIDE), lambda i: (0, 0)),
        ],
        out_specs=[pl.BlockSpec((s_dev, WIDE), lambda i: (0, i))] * group,
        out_shape=[jax.ShapeDtypeStruct((s_dev, 2 * rows), jnp.bfloat16)] * group,
        scratch_shapes=[pltpu.VMEM((group * s_dev, chans), source.dtype)],
        compiler_params=PARAMS,
        cost_estimate=cost_of(group * s_dev, 2 * rows, chans),
    )(source, patched, got, *wide)


def place_near_kernel(*refs, cols, stride):
    parts, out_ref, sems = refs[:-2], refs[-2], refs[-1]
    group = len(parts)
    me = lax.axis_index("src")
    lane = lax.rem(me, group)
    base = me - lane
    other = lax.rem(base + group, 2 * group)
    copies = []
    for k, part in enumerate(parts):
        frm = lax.rem(lane + group - k, group)
        for side, start in ((0, base + frm), (1, other + frm)):
            at = pl.multiple_of(start * stride, 128)
            copies.append(pltpu.make_async_copy(
                part.at[:, side * cols:(side + 1) * cols],
                out_ref.at[:, pl.ds(at, cols)],
                sems.at[2 * k + side],
            ))
    for copy in copies:
        copy.start()
    for copy in copies:
        copy.wait()


def place_near(parts, cols, stride, width):
    s_dev = parts[0].shape[0]
    any_spec = pl.BlockSpec(memory_space=pl.ANY)
    return pl.pallas_call(
        functools.partial(place_near_kernel, cols=cols, stride=stride),
        in_specs=[any_spec] * len(parts),
        out_specs=any_spec,
        out_shape=jax.ShapeDtypeStruct((s_dev, width), jnp.bfloat16),
        scratch_shapes=[pltpu.SemaphoreType.DMA((2 * len(parts),))],
        compiler_params=SMALL,
        cost_estimate=pl.CostEstimate(flops=0, bytes_accessed=4 * s_dev * width, transcendentals=0),
    )(*parts)


def place_direct_kernel(part_ref, held_ref, out_ref, sems, *, first, stride):
    n, _, cols = part_ref.shape
    copies = [
        pltpu.make_async_copy(
            part_ref.at[i],
            out_ref.at[:, i * stride + first:i * stride + first + cols],
            sems.at[i],
        )
        for i in range(n)
    ]
    for copy in copies:
        copy.start()
    for copy in copies:
        copy.wait()


def place_direct(part, held, first, stride):
    n, s_dev, cols = part.shape
    any_spec = pl.BlockSpec(memory_space=pl.ANY)
    return pl.pallas_call(
        functools.partial(place_direct_kernel, first=first, stride=stride),
        in_specs=[any_spec] * 2,
        out_specs=any_spec,
        out_shape=jax.ShapeDtypeStruct(held.shape, held.dtype),
        scratch_shapes=[pltpu.SemaphoreType.DMA((n,))],
        input_output_aliases={1: 0},
        compiler_params=SMALL,
        cost_estimate=pl.CostEstimate(flops=0, bytes_accessed=4 * n * s_dev * cols, transcendentals=0),
    )(part, held)


def per_device(source_feat, target_feat, conv_weight, conv_bias, proj_weight):
    patches, cells, chans = target_feat.shape
    emb = conv_weight.shape[1]
    s_dev = source_feat.shape[0]
    scale = chans ** (-0.5)
    n = lax.axis_size("src")
    group = n // 2
    patched = target_feat.reshape(-1, chans)
    swapped = patches * SWAP_NUM // SWAP_DEN * cells
    stride = patches * emb
    first = swapped // cells * emb

    got = lax.ppermute(patched[:swapped], "src", [(i, (i + group) % n) for i in range(n)])
    source = lax.all_to_all(
        jnp.broadcast_to(source_feat[None], (n, s_dev, chans)), "src", 0, 0, tiled=True
    ).reshape(n * s_dev, chans)
    wide = widen(conv_weight, conv_bias, proj_weight)

    direct = direct_tokens(source, patched, swapped, wide, scale).reshape(n, s_dev, -1)
    direct = lax.all_to_all(direct, "src", 0, 0, tiled=True)

    near = near_tokens(source, patched, got, s_dev, group, wide, scale)
    parts = [near[0]]
    for k in range(1, group):
        ring = [(i, i // group * group + (i + k) % group) for i in range(n)]
        parts.append(lax.ppermute(near[k], "src", ring))
    held = place_near(parts, first, stride, n * stride)
    return place_direct(direct, held, first, stride)


def solution(mesh):
    in_specs = (P(("pair", "src"), None), P(("pair", "src"), None, None), P(), P(), P())
    out_specs = P(("pair", "src"), None)
    return jax.shard_map(
        per_device, mesh=mesh, in_specs=in_specs, out_specs=out_specs, check_vma=False
    )
```

time: 105 us -> 71.5 us (0.68)
  blocking collectives: 74.1 us -> 0 us
  starting transfers between devices: 0 us -> 34 us
  waiting for transfers between devices: 0 us -> 19.5 us
  matrix products: 14.2 us -> 0 us
  Pallas kernels: 0 us -> 10.1 us
  local copies, waits for them, and re-layouts: 15.7 us -> 6.65 us
    all_to_all x1 -> x0, blocking collectives: 49.9 us -> none  [per_device(): lax.all_to_all(local_rows, 'src', split_axis=0, concat_axis=1, tiled=True)]
    all_gather x1 -> x0, blocking collectives: 24.2 us -> none  [per_device(): lax.all_gather(source_feat, 'src', axis=0, tiled=True)]
    all_to_all x0 -> x2, starting transfers between devices: none -> 21.4 us  [the longest x1 14 us: per_device(): direct = lax.all_to_all(direct, 'src', 0, 0, tiled=True)]
    ppermute x0 -> x8, waiting for transfers between devices: none -> 15.9 us  [the longest x7 12.8 us: per_device(): parts.append(lax.ppermute(near[k], 'src', ring))]
    dot_general x3 -> x0, matrix products: 14.2 us -> none  [the longest x1 9.61 us: embed_cost(): jnp.dot(hidden, proj_weight, preferred_element_type=jnp.float32)]
    ppermute x0 -> x8, starting transfers between devices: none -> 12.6 us  [the longest x7 9.78 us: per_device(): parts.append(lax.ppermute(near[k], 'src', ring))]
    pallas_call x0 -> x5, Pallas kernels: none -> 10.1 us  [the longest x1 4.5 us: near_tokens(): pl.pallas_call(functools.partial(near_kernel, scale=scale, s_dev=s_dev, o...]
    all_to_all x2 -> x0, local copies, waits for them, and re-layouts: 7.21 us -> none  [per_device(): lax.all_to_all(local_rows, 'src', split_axis=0, concat_axis=1, tiled=True)]
  transfers between devices with their start and end apart: 0 -> 10, of which waited for: 0 -> 6; matrix products, arithmetic and copies ran while one was open for 0% -> 3% of each run, Pallas kernels for 0% -> 13%
where the time goes in v1:
time: 71.5 us; the launch traced here: 70.3 us
  starting transfers between devices  34 us (48%)
  waiting for transfers between devices  19.5 us (27%)
  Pallas kernels  10.1 us (14%)
  local copies, waits for them, and re-layouts  6.65 us (9%)
    all_to_all x1, starting transfers between devices, per_device(): direct = lax.all_to_all(direct, 'src', 0, 0, tiled=True)  14 us
    ppermute x7, waiting for transfers between devices, per_device(): parts.append(lax.ppermute(near[k], 'src', ring))  12.8 us
    ppermute x7, starting transfers between devices, per_device(): parts.append(lax.ppermute(near[k], 'src', ring))  9.78 us
    all_to_all x1, starting transfers between devices, per_device(): lax.all_to_all(jnp.broadcast_to(source_feat[None], (n, s_dev, chans)), 's...  7.39 us
    pallas_call x1, Pallas kernels, near_tokens(): pl.pallas_call(functools.partial(near_kernel, scale=scale, s_dev=s_dev, o...  4.5 us
    all_to_all x1, waiting for transfers between devices, per_device(): lax.all_to_all(jnp.broadcast_to(source_feat[None], (n, s_dev, chans)), 's...  3.61 us
    unnamed x10, local copies, waits for them, and re-layouts  3.32 us
    pallas_call x1, Pallas kernels, direct_tokens(): pl.pallas_call(functools.partial(far_kernel, scale=scale), grid=(cols //...  3.28 us
  transfers between devices with their start and end apart: 10, of which 6 were waited for; matrix products, arithmetic and copies ran while one was open for 3% of the time, Pallas kernels for 13%

profile of v1, /device:TPU:0, one launch (start us, length us, event | category | flops | bytes accessed | tf_op | source)
XLA Modules:
  0.0 70.3 jit_solution(10713093334863151421)
XLA Ops:
  0.0 1.4 %broadcast_in_dim.4 = bf16[16,32,256]{2,1,0:T(8,128)(2,1)} broadcast(bf16[32,256]{1,0:T(8,128)(2,1)} %param.5), dimensions={1,2} | broadcast | bytes 278528 | tf_op jit(solution)/shard_map/broadcast_in_dim | solution.py:214
  1.4 7.4 %all-to-all-start = ((bf16[16,32,256]{2,1,0:T(8,128)(2,1)}), bf16[16,32,256]{2,1,0:T(8,128)(2,1)S(1)}, u32[]{:S(2)}, u32[]{:S(2)}) async-start(bf16[16,32,256]{2,1,0:T(8,128)(2,1)} %broadcast_in_dim.4), calls=%async_computation | async-start | bytes 524288 | tf_op jit(solution)/shard_map/all_to_all | solution.py:213
  8.8 1.9 %slice.6 = bf16[16,64,256]{2,1,0:T(8,128)(2,1)} slice(bf16[32,64,256]{2,1,0:T(8,128)(2,1)} %param.6), slice={[0:16], [0:64], [0:256]} | slice | bytes 1048576 | tf_op jit(solution)/shard_map/slice | solution.py:212
  10.7 2.8 %collective-permute-start = (bf16[1024,256]{1,0:T(8,128)(2,1)}, bf16[1024,256]{1,0:T(8,128)(2,1)S(1)}, u32[]{:S(2)}, u32[]{:S(2)}) collective-permute-start(bf16[1024,256]{1,0:T(8,128)(2,1)} %bitcast.4), channel_id=1, source_target_pairs={{0,8},{1,9},{2,10},{3,11},{4,12},{5,13},{6,14},{7,15},{8,0},{9,1},... | collective-permute-start | bytes 1572872 | tf_op jit(solution)/shard_map/ppermute | solution.py:212
  13.6 0.0 copy-start.2
  13.6 0.7 %copy-done.2 = bf16[64,64]{1,0:T(8,128)(2,1)S(1)} copy-done((bf16[64,64]{1,0:T(8,128)(2,1)S(1)}, bf16[64,64]{1,0:T(8,128)(2,1)}, u32[]{:S(2)}) %copy-start.2) | copy-done | bytes 8216
  14.3 0.0 copy-start.3
  14.3 0.7 %copy-done.3 = bf16[64,64]{1,0:T(8,128)(2,1)S(1)} copy-done((bf16[64,64]{1,0:T(8,128)(2,1)S(1)}, bf16[64,64]{1,0:T(8,128)(2,1)}, u32[]{:S(2)}) %copy-start.3) | copy-done | bytes 8216
  15.0 0.0 copy-start.4
  15.0 0.7 copy-done.4
  15.6 0.1 shard_map.55
  15.7 3.6 %all-to-all-done = bf16[16,32,256]{2,1,0:T(8,128)(2,1)S(1)} async-done(((bf16[16,32,256]{2,1,0:T(8,128)(2,1)}), bf16[16,32,256]{2,1,0:T(8,128)(2,1)S(1)}, u32[]{:S(2)}, u32[]{:S(2)}) %all-to-all-start) | async-done | bytes 262176 | tf_op jit(solution)/shard_map/all_to_all | solution.py:213
  19.4 0.0 copy-start
  19.4 1.2 %copy-done = bf16[32,64,256]{2,1,0:T(8,128)(2,1)S(1)} copy-done((bf16[32,64,256]{2,1,0:T(8,128)(2,1)S(1)}, bf16[32,64,256]{2,1,0:T(8,128)(2,1)}, u32[]{:S(2)}) %copy-start) | copy-done | bytes 1048600
  20.6 3.3 %shard_map.56 = bf16[512,1024]{1,0:T(8,128)(2,1)} custom-call(bf16[512,256]{1,0:T(8,128)(2,1)S(1)} %bitcast.7, bf16[2048,256]{1,0:T(8,128)(2,1)S(1)} %bitcast.5, bf16[256,256]{1,0:T(8,128)(2,1)S(1)} %get-tuple-element.16.w_ref, f32[1,256]{1,0:T(1,128)S(1)} %get-tuple-element.17.b_ref, bf16[256,256]{1,0:T(8,128)(2,1)S(1)} %get-tuple-element.18.p_ref), custom_call_target="tpu_custom_call" | custom-call | flops 32212254720 | bytes 1572864 | tf_op jit(solution)/shard_map/pallas_call | solution.py:70
  23.9 0.0 copy-start.1
  23.9 14.0 %all-to-all-start.1 = ((bf16[16,32,1024]{2,1,0:T(8,128)(2,1)}), bf16[16,32,1024]{2,1,0:T(8,128)(2,1)S(1)}, u32[]{:S(2)}, u32[]{:S(2)}) async-start(bf16[16,32,1024]{2,1,0:T(8,128)(2,1)} %bitcast.3), calls=%async_computation.1 | async-start | bytes 2097152 | tf_op jit(solution)/shard_map/all_to_all | solution.py:219
  37.9 3.1 %collective-permute-done.got_ref = bf16[1024,256]{1,0:T(8,128)(2,1)S(1)} collective-permute-done((bf16[1024,256]{1,0:T(8,128)(2,1)}, bf16[1024,256]{1,0:T(8,128)(2,1)S(1)}, u32[]{:S(2)}, u32[]{:S(2)}) %collective-permute-start) | collective-permute-done | bytes 524320 | tf_op jit(solution)/shard_map/ppermute | solution.py:212
  41.0 0.0 copy-done.1
  41.0 4.5 %shard_map.57 = (bf16[32,2048]{1,0:T(8,128)(2,1)S(1)}, bf16[32,2048]{1,0:T(8,128)(2,1)S(1)}, bf16[32,2048]{1,0:T(8,128)(2,1)S(1)}, bf16[32,2048]{1,0:T(8,128)(2,...) custom-call(bf16[512,256]{1,0:T(8,128)(2,1)S(1)} %bitcast.8, ...), custom_call_target="tpu_custom_call" | custom-call | flops 32212254720 | bytes 2097152 | tf_op jit(solution)/shard_map/pallas_call | solution.py:113
  45.5 0.1 collective-permute-start.1
  45.5 1.5 %collective-permute-start.2 = (bf16[32,2048]{1,0:T(8,128)(2,1)S(1)}, bf16[32,2048]{1,0:T(8,128)(2,1)S(1)}, u32[]{:S(2)}, u32[]{:S(2)}) collective-permute-start(bf16[32,2048]{1,0:T(8,128)(2,1)S(1)} %get-tuple-element.21), channel_id=1, source_target_pairs={{0,2},{1,3},{2,4},{3,5},{4,6},{5,7},{6,0},{7,1},{8,10},{9,11},{10,... | collective-permute-start | bytes 393224 | tf_op jit(solution)/shard_map/ppermute | solution.py:225
  47.1 0.0 collective-permute-start.3
  47.1 2.9 %collective-permute-start.4 = (bf16[32,2048]{1,0:T(8,128)(2,1)S(1)}, bf16[32,2048]{1,0:T(8,128)(2,1)S(1)}, u32[]{:S(2)}, u32[]{:S(2)}) collective-permute-start(bf16[32,2048]{1,0:T(8,128)(2,1)S(1)} %get-tuple-element.23), channel_id=1, source_target_pairs={{0,4},{1,5},{2,6},{3,7},{4,0},{5,1},{6,2},{7,3},{8,12},{9,13},{10,... | collective-permute-start | bytes 393224 | tf_op jit(solution)/shard_map/ppermute | solution.py:225
  49.9 0.0 collective-permute-start.5
  49.9 7.0 %collective-permute-done.1.refs_1_ = bf16[32,2048]{1,0:T(8,128)(2,1)S(1)} collective-permute-done((bf16[32,2048]{1,0:T(8,128)(2,1)S(1)}, bf16[32,2048]{1,0:T(8,128)(2,1)S(1)}, u32[]{:S(2)}, u32[]{:S(2)}) %collective-permute-start.1) | collective-permute-done | bytes 131104 | tf_op jit(solution)/shard_map/ppermute | solution.py:225
  56.9 0.0 collective-permute-start.6
  56.9 0.9 %collective-permute-done.2.refs_2_ = bf16[32,2048]{1,0:T(8,128)(2,1)S(1)} collective-permute-done((bf16[32,2048]{1,0:T(8,128)(2,1)S(1)}, bf16[32,2048]{1,0:T(8,128)(2,1)S(1)}, u32[]{:S(2)}, u32[]{:S(2)}) %collective-permute-start.2) | collective-permute-done | bytes 131104 | tf_op jit(solution)/shard_map/ppermute | solution.py:225
  57.9 5.3 %collective-permute-start.7 = (bf16[32,2048]{1,0:T(8,128)(2,1)S(1)}, bf16[32,2048]{1,0:T(8,128)(2,1)S(1)}, u32[]{:S(2)}, u32[]{:S(2)}) collective-permute-start(bf16[32,2048]{1,0:T(8,128)(2,1)S(1)} %get-tuple-element.26), channel_id=1, source_target_pairs={{0,7},{1,0},{2,1},{3,2},{4,3},{5,4},{6,5},{7,6},{8,15},{9,8},{10,9... | collective-permute-start | bytes 393224 | tf_op jit(solution)/shard_map/ppermute | solution.py:225
  63.2 0.0 collective-permute-done.3.refs_3_
  63.2 0.0 collective-permute-done.4.refs_4_
  63.2 0.0 collective-permute-done.5.refs_5_
  63.2 2.6 %collective-permute-done.6.refs_6_ = bf16[32,2048]{1,0:T(8,128)(2,1)S(1)} collective-permute-done((bf16[32,2048]{1,0:T(8,128)(2,1)S(1)}, bf16[32,2048]{1,0:T(8,128)(2,1)S(1)}, u32[]{:S(2)}, u32[]{:S(2)}) %collective-permute-start.6) | collective-permute-done | bytes 131104 | tf_op jit(solution)/shard_map/ppermute | solution.py:225
  65.8 2.2 %collective-permute-done.7.refs_7_ = bf16[32,2048]{1,0:T(8,128)(2,1)S(1)} collective-permute-done((bf16[32,2048]{1,0:T(8,128)(2,1)S(1)}, bf16[32,2048]{1,0:T(8,128)(2,1)S(1)}, u32[]{:S(2)}, u32[]{:S(2)}) %collective-permute-start.7) | collective-permute-done | bytes 131104 | tf_op jit(solution)/shard_map/ppermute | solution.py:225
  68.1 1.1 %shard_map.58.held_ref = bf16[32,32768]{1,0:T(8,128)(2,1)} custom-call(bf16[32,2048]{1,0:T(8,128)(2,1)S(1)} %get-tuple-element.19.refs_0_, bf16[32,2048]{1,0:T(8,128)(2,1)S(1)} %collective-permute-done.1.refs_1_, bf16[32,2048]{1,0:T(8,128)(2,1)S(1)} %collective-permute-done.2.refs_2_, bf16[32,2048]{1,0:T(8,128)(2,1)S(1)} %collective-permute-done.3.refs_3_, ...), custom_call_target="tpu_custom_call" | custom-call | bytes 4194304 | tf_op jit(solution)/shard_map/pallas_call | solution.py:158
  69.2 0.0 all-to-all-done.1.part_ref
  69.2 1.1 %shard_map.59 = bf16[32,32768]{1,0:T(8,128)(2,1)} custom-call(bf16[16,32,1024]{2,1,0:T(8,128)(2,1)S(1)} %all-to-all-done.1.part_ref, bf16[32,32768]{1,0:T(8,128)(2,1)} %shard_map.58.held_ref), custom_call_target="tpu_custom_call", output_to_operand_aliasing={{}: (1, {})} | custom-call | bytes 2097152 | tf_op jit(solution)/shard_map/pallas_call | solution.py:188
Async XLA Ops:
  1.4 17.9 %all-to-all-start = ((bf16[16,32,256]{2,1,0:T(8,128)(2,1)}), bf16[16,32,256]{2,1,0:T(8,128)(2,1)S(1)}, u32[]{:S(2)}, u32[]{:S(2)}) async-start(bf16[16,32,256]{2,1,0:T(8,128)(2,1)} %broadcast_in_dim.4), calls=%async_computation | async-start | bytes 524288 | tf_op jit(solution)/shard_map/all_to_all | solution.py:213
  10.7 30.2 %collective-permute-start = (bf16[1024,256]{1,0:T(8,128)(2,1)}, bf16[1024,256]{1,0:T(8,128)(2,1)S(1)}, u32[]{:S(2)}, u32[]{:S(2)}) collective-permute-start(bf16[1024,256]{1,0:T(8,128)(2,1)} %bitcast.4), channel_id=1, source_target_pairs={{0,8},{1,9},{2,10},{3,11},{4,12},{5,13},{6,14},{7,15},{8,0},{9,1},... | collective-permute-start | bytes 1572872 | tf_op jit(solution)/shard_map/ppermute | solution.py:212
  13.6 0.7 %copy-start.2 = (bf16[64,64]{1,0:T(8,128)(2,1)S(1)}, bf16[64,64]{1,0:T(8,128)(2,1)}, u32[]{:S(2)}) copy-start(bf16[64,64]{1,0:T(8,128)(2,1)} %w_ref.1) | copy-start | bytes 24580
  14.3 0.7 %copy-start.3 = (bf16[64,64]{1,0:T(8,128)(2,1)S(1)}, bf16[64,64]{1,0:T(8,128)(2,1)}, u32[]{:S(2)}) copy-start(bf16[64,64]{1,0:T(8,128)(2,1)} %p_ref.1) | copy-start | bytes 24580
  15.0 0.7 copy-start.4
  19.4 1.2 %copy-start = (bf16[32,64,256]{2,1,0:T(8,128)(2,1)S(1)}, bf16[32,64,256]{2,1,0:T(8,128)(2,1)}, u32[]{:S(2)}) copy-start(bf16[32,64,256]{2,1,0:T(8,128)(2,1)} %param.6) | copy-start | bytes 3145732
  23.9 17.1 %copy-start.1 = (bf16[32,64,256]{2,1,0:T(8,128)(2,1)S(1)}, bf16[32,64,256]{2,1,0:T(8,128)(2,1)}, u32[]{:S(2)}) copy-start(bf16[32,64,256]{2,1,0:T(8,128)(2,1)} %param.6) | copy-start | bytes 3145732
  23.9 45.3 %all-to-all-start.1 = ((bf16[16,32,1024]{2,1,0:T(8,128)(2,1)}), bf16[16,32,1024]{2,1,0:T(8,128)(2,1)S(1)}, u32[]{:S(2)}, u32[]{:S(2)}) async-start(bf16[16,32,1024]{2,1,0:T(8,128)(2,1)} %bitcast.3), calls=%async_computation.1 | async-start | bytes 2097152 | tf_op jit(solution)/shard_map/all_to_all | solution.py:219
  45.5 11.4 %collective-permute-start.1 = (bf16[32,2048]{1,0:T(8,128)(2,1)S(1)}, bf16[32,2048]{1,0:T(8,128)(2,1)S(1)}, u32[]{:S(2)}, u32[]{:S(2)}) collective-permute-start(bf16[32,2048]{1,0:T(8,128)(2,1)S(1)} %get-tuple-element.20), channel_id=1, source_target_pairs={{0,1},{1,2},{2,3},{3,4},{4,5},{5,6},{6,7},{7,0},{8,9},{9,10},{10,1... | collective-permute-start | bytes 393224 | tf_op jit(solution)/shard_map/ppermute | solution.py:225
  45.5 12.3 %collective-permute-start.2 = (bf16[32,2048]{1,0:T(8,128)(2,1)S(1)}, bf16[32,2048]{1,0:T(8,128)(2,1)S(1)}, u32[]{:S(2)}, u32[]{:S(2)}) collective-permute-start(bf16[32,2048]{1,0:T(8,128)(2,1)S(1)} %get-tuple-element.21), channel_id=1, source_target_pairs={{0,2},{1,3},{2,4},{3,5},{4,6},{5,7},{6,0},{7,1},{8,10},{9,11},{10,... | collective-permute-start | bytes 393224 | tf_op jit(solution)/shard_map/ppermute | solution.py:225
  47.1 16.1 %collective-permute-start.3 = (bf16[32,2048]{1,0:T(8,128)(2,1)S(1)}, bf16[32,2048]{1,0:T(8,128)(2,1)S(1)}, u32[]{:S(2)}, u32[]{:S(2)}) collective-permute-start(bf16[32,2048]{1,0:T(8,128)(2,1)S(1)} %get-tuple-element.22), channel_id=1, source_target_pairs={{0,3},{1,4},{2,5},{3,6},{4,7},{5,0},{6,1},{7,2},{8,11},{9,12},{10,... | collective-permute-start | bytes 393224 | tf_op jit(solution)/shard_map/ppermute | solution.py:225
  47.1 16.1 %collective-permute-start.4 = (bf16[32,2048]{1,0:T(8,128)(2,1)S(1)}, bf16[32,2048]{1,0:T(8,128)(2,1)S(1)}, u32[]{:S(2)}, u32[]{:S(2)}) collective-permute-start(bf16[32,2048]{1,0:T(8,128)(2,1)S(1)} %get-tuple-element.23), channel_id=1, source_target_pairs={{0,4},{1,5},{2,6},{3,7},{4,0},{5,1},{6,2},{7,3},{8,12},{9,13},{10,... | collective-permute-start | bytes 393224 | tf_op jit(solution)/shard_map/ppermute | solution.py:225
  49.9 13.3 %collective-permute-start.5 = (bf16[32,2048]{1,0:T(8,128)(2,1)S(1)}, bf16[32,2048]{1,0:T(8,128)(2,1)S(1)}, u32[]{:S(2)}, u32[]{:S(2)}) collective-permute-start(bf16[32,2048]{1,0:T(8,128)(2,1)S(1)} %get-tuple-element.24), channel_id=1, source_target_pairs={{0,5},{1,6},{2,7},{3,0},{4,1},{5,2},{6,3},{7,4},{8,13},{9,14},{10,... | collective-permute-start | bytes 393224 | tf_op jit(solution)/shard_map/ppermute | solution.py:225
  56.9 8.9 %collective-permute-start.6 = (bf16[32,2048]{1,0:T(8,128)(2,1)S(1)}, bf16[32,2048]{1,0:T(8,128)(2,1)S(1)}, u32[]{:S(2)}, u32[]{:S(2)}) collective-permute-start(bf16[32,2048]{1,0:T(8,128)(2,1)S(1)} %get-tuple-element.25), channel_id=1, source_target_pairs={{0,6},{1,7},{2,0},{3,1},{4,2},{5,3},{6,4},{7,5},{8,14},{9,15},{10,... | collective-permute-start | bytes 393224 | tf_op jit(solution)/shard_map/ppermute | solution.py:225
  57.9 10.2 %collective-permute-start.7 = (bf16[32,2048]{1,0:T(8,128)(2,1)S(1)}, bf16[32,2048]{1,0:T(8,128)(2,1)S(1)}, u32[]{:S(2)}, u32[]{:S(2)}) collective-permute-start(bf16[32,2048]{1,0:T(8,128)(2,1)S(1)} %get-tuple-element.26), channel_id=1, source_target_pairs={{0,7},{1,0},{2,1},{3,2},{4,3},{5,4},{6,5},{7,6},{8,15},{9,8},{10,9... | collective-permute-start | bytes 393224 | tf_op jit(solution)/shard_map/ppermute | solution.py:225

commit v2 on v0

v2 whole, which is shorter than its diff:
```python
import functools

import jax
import jax.numpy as jnp
from jax import lax
from jax.experimental import pallas as pl
from jax.experimental.pallas import tpu as pltpu
from jax.sharding import PartitionSpec as P

WIDE = 256
INNER = 4
SWAP_NUM, SWAP_DEN = 3, 8
COVER = 40
PARAMS = pltpu.CompilerParams(vmem_limit_bytes=20 << 20)
SMALL = pltpu.CompilerParams(vmem_limit_bytes=4 << 20)
ANY = pl.BlockSpec(memory_space=pl.ANY)
HBM = pl.BlockSpec(memory_space=pltpu.HBM)
VMEM = pl.BlockSpec(memory_space=pltpu.VMEM)


def gelu(x):
    return x * (lax.erf(x * 0.7071067811865476) * 0.5 + 0.5)


def block_tokens(source, target, w_ref, b_ref, p_ref, scale):
    cost = lax.dot_general(
        source, target, (((1,), (1,)), ((), ())), preferred_element_type=jnp.float32
    )
    cost = (cost * scale).astype(jnp.bfloat16)
    embedded = jnp.dot(cost, w_ref[...], preferred_element_type=jnp.float32) + b_ref[...]
    hidden = gelu(embedded).astype(jnp.bfloat16)
    out = embedded + jnp.dot(hidden, p_ref[...], preferred_element_type=jnp.float32)
    return out.astype(jnp.bfloat16)


def prepare_kernel(tgt_ref, w_in, b_in, p_in, cross_ref, rest_ref, ww_ref, wb_ref, wp_ref,
                   w_ref, b_ref, p_ref, sems):
    swapped, total = cross_ref.shape[0], tgt_ref.shape[0]
    small = [
        pltpu.make_async_copy(w_in, w_ref, sems.at[0]),
        pltpu.make_async_copy(b_in, b_ref, sems.at[1]),
        pltpu.make_async_copy(p_in, p_ref, sems.at[2]),
    ]
    large = [
        pltpu.make_async_copy(tgt_ref.at[0:swapped, :], cross_ref, sems.at[3]),
        pltpu.make_async_copy(tgt_ref.at[swapped:total, :], rest_ref, sems.at[4]),
    ]
    for copy in small + large:
        copy.start()
    ww_ref[...] = jnp.zeros_like(ww_ref)
    wp_ref[...] = jnp.zeros_like(wp_ref)
    for copy in small:
        copy.wait()
    cells, emb = w_ref.shape
    for i in range(WIDE // cells):
        ww_ref[i * cells:(i + 1) * cells, i * emb:(i + 1) * emb] = w_ref[...]
        wp_ref[i * emb:(i + 1) * emb, i * emb:(i + 1) * emb] = p_ref[...]
        wb_ref[:, i * emb:(i + 1) * emb] = b_ref[...]
    for copy in large:
        copy.wait()


def prepare(patched, swapped, conv_weight, conv_bias, proj_weight):
    rows, chans = patched.shape
    bias = conv_bias[None, :]
    return pl.pallas_call(
        prepare_kernel,
        in_specs=[HBM] * 4,
        out_specs=[VMEM] * 5,
        out_shape=[
            jax.ShapeDtypeStruct((swapped, chans), patched.dtype),
            jax.ShapeDtypeStruct((rows - swapped, chans), patched.dtype),
            jax.ShapeDtypeStruct((WIDE, WIDE), conv_weight.dtype),
            jax.ShapeDtypeStruct((1, WIDE), conv_bias.dtype),
            jax.ShapeDtypeStruct((WIDE, WIDE), proj_weight.dtype),
        ],
        scratch_shapes=[
            pltpu.VMEM(conv_weight.shape, conv_weight.dtype),
            pltpu.VMEM(bias.shape, bias.dtype),
            pltpu.VMEM(proj_weight.shape, proj_weight.dtype),
            pltpu.SemaphoreType.DMA((5,)),
        ],
        compiler_params=SMALL,
    )(*[pltpu.with_memory_space_constraint(x, pltpu.HBM) for x in (patched, conv_weight, bias, proj_weight)])


def cost_of(px, cols, chans):
    return pl.CostEstimate(
        flops=COVER * 2 * px * cols * (chans + 2 * WIDE),
        bytes_accessed=2 * px * cols + 2 * cols * chans,
        transcendentals=px * cols,
    )


def direct_kernel(src_ref, tgt_ref, w_ref, b_ref, p_ref, out_ref, rows_ref, *, scale):
    inner, outer, s_dev, _ = src_ref.shape

    @pl.when(pl.program_id(0) == 0)
    def _():
        mine = lax.axis_index("src") // inner
        for k in range(outer):
            for j in range(inner):
                at = pl.multiple_of(((mine ^ k) * inner + j) * s_dev, s_dev)
                rows_ref[pl.ds(at, s_dev), :] = src_ref[j, k]

    out_ref[...] = block_tokens(rows_ref[...], tgt_ref[...], w_ref, b_ref, p_ref, scale)


def direct_tokens(source, rest, wide, scale):
    inner, outer, s_dev, chans = source.shape
    px = inner * outer * s_dev
    cols = rest.shape[0]
    return pl.pallas_call(
        functools.partial(direct_kernel, scale=scale),
        grid=(cols // WIDE,),
        in_specs=[
            pl.BlockSpec(source.shape, lambda i: (0, 0, 0, 0)),
            pl.BlockSpec((WIDE, chans), lambda i: (i, 0)),
            pl.BlockSpec((WIDE, WIDE), lambda i: (0, 0)),
            pl.BlockSpec((1, WIDE), lambda i: (0, 0)),
            pl.BlockSpec((WIDE, WIDE), lambda i: (0, 0)),
        ],
        out_specs=pl.BlockSpec((px, WIDE), lambda i: (0, i)),
        out_shape=jax.ShapeDtypeStruct((px, cols), jnp.bfloat16),
        scratch_shapes=[pltpu.VMEM((px, chans), source.dtype)],
        compiler_params=PARAMS,
        cost_estimate=cost_of(px, cols, chans),
    )(source, rest, *wide)


def near_kernel(src_ref, tgt_ref, w_ref, b_ref, p_ref, *rest, scale, group):
    outs, rows_ref = rest[-1 - group:-1], rest[-1]
    inner, _, s_dev, _ = src_ref.shape

    @pl.when(pl.program_id(0) == 0)
    def _():
        lane = lax.rem(lax.axis_index("src"), inner)
        for k in range(group):
            rows_ref[k * s_dev:(k + 1) * s_dev, :] = src_ref[lane ^ (k % inner), k // inner]

    tok = block_tokens(rows_ref[...], tgt_ref[...], w_ref, b_ref, p_ref, scale)
    for k in range(group):
        outs[k][...] = tok[k * s_dev:(k + 1) * s_dev, :]


def near_tokens(source, target, held, group, wide, scale):
    _, _, s_dev, chans = source.shape
    rows = target.shape[0]
    steps = rows // WIDE
    skip = steps if held else 0
    return pl.pallas_call(
        functools.partial(near_kernel, scale=scale, group=group),
        grid=(steps,),
        in_specs=[
            pl.BlockSpec(source.shape, lambda i: (0, 0, 0, 0)),
            pl.BlockSpec((WIDE, chans), lambda i: (i, 0)),
            pl.BlockSpec((WIDE, WIDE), lambda i: (0, 0)),
            pl.BlockSpec((1, WIDE), lambda i: (0, 0)),
            pl.BlockSpec((WIDE, WIDE), lambda i: (0, 0)),
        ] + [ANY] * len(held),
        out_specs=[pl.BlockSpec((s_dev, WIDE), lambda i: (0, i + skip))] * group,
        out_shape=[jax.ShapeDtypeStruct((s_dev, 2 * rows), jnp.bfloat16)] * group,
        scratch_shapes=[pltpu.VMEM((group * s_dev, chans), source.dtype)],
        input_output_aliases={5 + k: k for k in range(len(held))},
        compiler_params=PARAMS,
        cost_estimate=cost_of(group * s_dev, rows, chans),
    )(source, target, *wide, *held)


def place_kernel(direct_ref, *refs):
    parts, out_ref, sems = refs[:-2], refs[-2], refs[-1]
    group = len(parts)
    n, _, tail = direct_ref.shape
    first = parts[0].shape[1] // 2
    stride = first + tail
    me = lax.axis_index("src")
    copies = [
        pltpu.make_async_copy(
            direct_ref.at[i], out_ref.at[:, i * stride + first:(i + 1) * stride], sems.at[i]
        )
        for i in range(n)
    ]
    for k, part in enumerate(parts):
        near = me ^ k
        for side, frm in ((0, near), (1, near ^ group)):
            at = pl.multiple_of(frm * stride, 128)
            copies.append(pltpu.make_async_copy(
                part.at[:, side * first:(side + 1) * first],
                out_ref.at[:, pl.ds(at, first)],
                sems.at[n + 2 * k + side],
            ))
    for copy in copies:
        copy.start()
    for copy in copies:
        copy.wait()


def place(direct, parts):
    n, s_dev, tail = direct.shape
    width = n * (tail + parts[0].shape[1] // 2)
    return pl.pallas_call(
        place_kernel,
        in_specs=[ANY] * (1 + len(parts)),
        out_specs=ANY,
        out_shape=jax.ShapeDtypeStruct((s_dev, width), jnp.bfloat16),
        scratch_shapes=[pltpu.SemaphoreType.DMA((n + 2 * len(parts),))],
        compiler_params=SMALL,
        cost_estimate=pl.CostEstimate(flops=0, bytes_accessed=4 * s_dev * width, transcendentals=0),
    )(direct, *parts)


def per_device(source_feat, target_feat, conv_weight, conv_bias, proj_weight):
    patches, cells, chans = target_feat.shape
    s_dev = source_feat.shape[0]
    scale = chans ** (-0.5)
    n = lax.axis_size("src")
    group, outer = n // 2, n // INNER
    swapped = patches * SWAP_NUM // SWAP_DEN * cells

    def exchange(x, bits):
        return lax.ppermute(x, "src", [(i, i ^ bits) for i in range(n)])

    crossed, rest, *wide = prepare(
        target_feat.reshape(-1, chans), swapped, conv_weight, conv_bias, proj_weight
    )
    got = exchange(crossed, group)
    column = jnp.stack([source_feat] + [exchange(source_feat, k * INNER) for k in range(1, outer)])
    rows = [list(range(i, i + INNER)) for i in range(0, n, INNER)]
    source = lax.all_gather(column, "src", axis=0, axis_index_groups=rows)

    direct = direct_tokens(source, rest, wide, scale).reshape(n, s_dev, -1)
    direct = lax.all_to_all(direct, "src", 0, 0, tiled=True)

    near = near_tokens(source, crossed, [], group, wide, scale)
    near = near_tokens(source, got, near, group, wide, scale)
    parts = [near[0]] + [exchange(near[k], k) for k in range(1, group)]
    return place(direct, parts)


def solution(mesh):
    in_specs = (P(("pair", "src"), None), P(("pair", "src"), None, None), P(), P(), P())
    out_specs = P(("pair", "src"), None)
    return jax.shard_map(
        per_device, mesh=mesh, in_specs=in_specs, out_specs=out_specs, check_vma=False
    )
```

time: 105 us -> 60 us (0.57)
  blocking collectives: 74.1 us -> 5.79 us
  waiting for transfers between devices: 0 us -> 24.4 us
  starting transfers between devices: 0 us -> 18.2 us
  local copies, waits for them, and re-layouts: 15.7 us -> 0 us
  matrix products: 14.2 us -> 0 us
  Pallas kernels: 0 us -> 10.2 us
    all_to_all x1 -> x0, blocking collectives: 49.9 us -> none  [per_device(): lax.all_to_all(local_rows, 'src', split_axis=0, concat_axis=1, tiled=True)]
    ppermute x0 -> x11, waiting for transfers between devices: none -> 24.4 us  [exchange(): return lax.ppermute(x, 'src', [(i, i ^ bits) for i in range(n)])]
    all_gather x1, blocking collectives: 24.2 us -> 5.79 us  [per_device(): source = lax.all_gather(column, 'src', axis=0, axis_index_groups=rows)]
    ppermute x0 -> x11, starting transfers between devices: none -> 14.5 us  [exchange(): return lax.ppermute(x, 'src', [(i, i ^ bits) for i in range(n)])]
    dot_general x3 -> x0, matrix products: 14.2 us -> none  [the longest x1 9.61 us: embed_cost(): jnp.dot(hidden, proj_weight, preferred_element_type=jnp.float32)]
    pallas_call x0 -> x5, Pallas kernels: none -> 10.2 us  [the longest x1 3.92 us: direct_tokens(): pl.pallas_call(functools.partial(direct_kernel, scale=scale), grid=(cols...]
    all_to_all x2 -> x0, local copies, waits for them, and re-layouts: 7.21 us -> none  [per_device(): lax.all_to_all(local_rows, 'src', split_axis=0, concat_axis=1, tiled=True)]
    reshape x1 -> x0, local copies, waits for them, and re-layouts: 5.34 us -> none  [embed_cost(): flat = cost.reshape(-1, cells)]
  transfers between devices with their start and end apart: 0 -> 12, of which waited for: 0 -> 8; matrix products, arithmetic and copies ran while one was open for 0% -> 1% of each run, Pallas kernels for 0% -> 15%
where the time goes in v2:
time: 60 us; the launch traced here: 59.3 us
  waiting for transfers between devices  24.4 us (41%)
  starting transfers between devices  18.2 us (30%)
  Pallas kernels  10.2 us (17%)
  blocking collectives  5.79 us (10%)
  other arithmetic  0.73 us (1%)
    ppermute x11, waiting for transfers between devices, exchange(): return lax.ppermute(x, 'src', [(i, i ^ bits) for i in range(n)])  24.4 us
    ppermute x11, starting transfers between devices, exchange(): return lax.ppermute(x, 'src', [(i, i ^ bits) for i in range(n)])  14.5 us
    all_gather x1, blocking collectives, per_device(): source = lax.all_gather(column, 'src', axis=0, axis_index_groups=rows)  5.79 us
    pallas_call x1, Pallas kernels, direct_tokens(): pl.pallas_call(functools.partial(direct_kernel, scale=scale), grid=(cols...  3.92 us
    all_to_all x1, starting transfers between devices, per_device(): direct = lax.all_to_all(direct, 'src', 0, 0, tiled=True)  3.7 us
    pallas_call x2, Pallas kernels, near_tokens(): pl.pallas_call(functools.partial(near_kernel, scale=scale, group=group),...  3.38 us
    pallas_call x1, Pallas kernels, place(): pl.pallas_call(place_kernel, in_specs=[ANY] * (1 + len(parts)), out_specs...  1.57 us
    pallas_call x1, Pallas kernels, prepare(): pl.pallas_call(prepare_kernel, in_specs=[HBM] * 4, out_specs=[VMEM] * 5,...  1.3 us
  transfers between devices with their start and end apart: 12, of which 8 were waited for; matrix products, arithmetic and copies ran while one was open for 1% of the time, Pallas kernels for 15%

profile of v2, /device:TPU:0, one launch (start us, length us, event | category | flops | bytes accessed | tf_op | source)
XLA Modules:
  0.0 59.3 jit_solution(38360688736460956)
XLA Ops:
  0.0 3.0 %collective-permute-start = (bf16[32,256]{1,0:T(8,128)(2,1)}, bf16[32,256]{1,0:T(8,128)(2,1)S(1)}, u32[]{:S(2)}, u32[]{:S(2)}) collective-permute-start(bf16[32,256]{1,0:T(8,128)(2,1)} %param.5), channel_id=1, source_target_pairs={{0,4},{1,5},{2,6},{3,7},{4,0},{5,1},{6,2},{7,3},{8,12},{9,13},{10,... | collective-permute-start | bytes 49160 | tf_op jit(solution)/shard_map/ppermute | solution.py:221
  3.0 2.5 %collective-permute-start.2 = (bf16[32,256]{1,0:T(8,128)(2,1)}, bf16[32,256]{1,0:T(8,128)(2,1)S(1)}, u32[]{:S(2)}, u32[]{:S(2)}) collective-permute-start(bf16[32,256]{1,0:T(8,128)(2,1)} %param.5), channel_id=1, source_target_pairs={{0,12},{1,13},{2,14},{3,15},{4,8},{5,9},{6,10},{7,11},{8,4},{9,5},... | collective-permute-start | bytes 49160 | tf_op jit(solution)/shard_map/ppermute | solution.py:221
  5.5 0.1 collective-permute-start.1
  5.6 1.3 %shard_map.55 = (bf16[768,256]{1,0:T(8,128)(2,1)S(1)}, bf16[1280,256]{1,0:T(8,128)(2,1)S(1)}, bf16[256,256]{1,0:T(8,128)(2,1)S(1)}, f32[1,256]{1,0:T(1,128)S(1)}, bf16[256,256]{1,0:T(8,128)(2,1)S(1)}) custom-call(bf16[2048,256]{1,0:T(8,128)(2,1)} %bitcast.11, bf16[64,64]{1,0:T(8,128)(2,1)} %w_in.1, f32[1,64]{1,0:T(1,128)} %bitcast.16, bf16[64,64]{1,0:T(8,128)(2,1)} %p_in.1), custom_call_target="tpu_custom_call" | custom-call | tf_op jit(solution)/shard_map/pallas_call | solution.py:66
  6.9 2.9 %collective-permute-start.3 = (bf16[768,256]{1,0:T(8,128)(2,1)S(1)}, bf16[768,256]{1,0:T(8,128)(2,1)S(1)}, u32[]{:S(2)}, u32[]{:S(2)}) collective-permute-start(bf16[768,256]{1,0:T(8,128)(2,1)S(1)} %get-tuple-element.30.tgt_ref), channel_id=1, source_target_pairs={{0,8},{1,9},{2,10},{3,11},{4,12},{5,13},{6,14},{7,15},{8,0},{9,1},... | collective-permute-start | bytes 1179656 | tf_op jit(solution)/shard_map/ppermute | solution.py:221
  9.8 0.0 collective-permute-done
  9.8 0.0 collective-permute-done.2
  9.8 0.8 %collective-permute-done.1 = bf16[32,256]{1,0:T(8,128)(2,1)S(1)} collective-permute-done((bf16[32,256]{1,0:T(8,128)(2,1)}, bf16[32,256]{1,0:T(8,128)(2,1)S(1)}, u32[]{:S(2)}, u32[]{:S(2)}) %collective-permute-start.1) | collective-permute-done | bytes 16416 | tf_op jit(solution)/shard_map/ppermute | solution.py:221
  10.6 0.7 %pad_maximum_fusion = bf16[4,32,256]{2,1,0:T(8,128)(2,1)S(1)} fusion(bf16[1,32,256]{2,1,0:T(8,128)(2,1)S(1)} %bitcast.14, bf16[1,32,256]{2,1,0:T(8,128)(2,1)S(1)} %bitcast.15, bf16[1,32,256]{2,1,0:T(8,128)(2,1)S(1)} %bitcast.13, bf16[1,32,256]{2,1,0:T(8,128)(2,1)} %bitcast.12), kind=kLoop, calls=%fused_computation | loop fusion | flops 98304 | bytes 131072 | tf_op jit(solution)/shard_map/stack | solution.py:227
  11.3 5.8 %all-gather = bf16[16,32,256]{2,1,0:T(8,128)(2,1)S(1)} all-gather(bf16[4,32,256]{2,1,0:T(8,128)(2,1)S(1)} %pad_maximum_fusion), channel_id=2, replica_groups={{0,1,2,3},{4,5,6,7},{8,9,10,11},{12,13,14,15},{16,17,18,19},{20,21,22,2..., dimensions={0}, use_global_device_ids=true | all-gather | bytes 327680 | tf_op jit(solution)/shard_map/all_gather | solution.py:229
  17.1 3.9 %shard_map.56 = bf16[512,1280]{1,0:T(8,128)(2,1)} custom-call(bf16[4,4,32,256]{3,2,1,0:T(8,128)(2,1)S(1)} %bitcast.8, bf16[1280,256]{1,0:T(8,128)(2,1)S(1)} %get-tuple-element.26.tgt_ref, bf16[256,256]{1,0:T(8,128)(2,1)S(1)} %get-tuple-element.27.w_ref, f32[1,256]{1,0:T(1,128)S(1)} %get-tuple-element.28.b_ref, bf16[256,256]{1,0:T(8,128)(2,1)S(1)} %get-tuple-element.29.p_ref), custom_call_target="tpu_custom_call" | custom-call | flops 40265318400 | bytes 1966080 | tf_op jit(solution)/shard_map/pallas_call | solution.py:113
  21.1 3.7 %all-to-all-start = ((bf16[16,32,1280]{2,1,0:T(8,128)(2,1)}), bf16[16,32,1280]{2,1,0:T(8,128)(2,1)S(1)}, u32[]{:S(2)}, u32[]{:S(2)}) async-start(bf16[16,32,1280]{2,1,0:T(8,128)(2,1)} %bitcast.7), calls=%async_computation | async-start | bytes 2621440 | tf_op jit(solution)/shard_map/all_to_all | solution.py:232
  24.8 1.7 %shard_map.57 = (bf16[32,1536]{1,0:T(8,128)(2,1)S(1)}, bf16[32,1536]{1,0:T(8,128)(2,1)S(1)}, bf16[32,1536]{1,0:T(8,128)(2,1)S(1)}, bf16[32,1536]{1,0:T(8,128)(2,...) custom-call(bf16[4,4,32,256]{3,2,1,0:T(8,128)(2,1)S(1)} %bitcast.9, ...), custom_call_target="tpu_custom_call" | custom-call | flops 12079595520 | bytes 786432 | tf_op jit(solution)/shard_map/pallas_call | solution.py:151
  26.5 0.5 collective-permute-done.3.tgt_ref
  27.0 1.7 %shard_map.58 = (bf16[32,1536]{1,0:T(8,128)(2,1)S(1)}, bf16[32,1536]{1,0:T(8,128)(2,1)S(1)}, bf16[32,1536]{1,0:T(8,128)(2,1)S(1)}, bf16[32,1536]{1,0:T(8,128)(2,...) custom-call(bf16[4,4,32,256]{3,2,1,0:T(8,128)(2,1)S(1)} %bitcast.10,, ...), custom_call_target="tpu_custom_call", output_to_operand_aliasing={{0}: (5, {}), {1}: (6, {}), {2}: (7, {}), {3}: (8, {}), {4}... | custom-call | flops 12079595520 | bytes 786432 | tf_op jit(solution)/shard_map/pallas_call | solution.py:151
  28.6 0.1 collective-permute-start.4
  28.7 1.6 %collective-permute-start.5 = (bf16[32,1536]{1,0:T(8,128)(2,1)S(1)}, bf16[32,1536]{1,0:T(8,128)(2,1)S(1)}, u32[]{:S(2)}, u32[]{:S(2)}) collective-permute-start(bf16[32,1536]{1,0:T(8,128)(2,1)S(1)} %get-tuple-element.41), channel_id=1, source_target_pairs={{0,2},{1,3},{2,0},{3,1},{4,6},{5,7},{6,4},{7,5},{8,10},{9,11},{10,... | collective-permute-start | bytes 294920 | tf_op jit(solution)/shard_map/ppermute | solution.py:221
  30.3 0.3 collective-permute-start.6
  30.6 1.4 %collective-permute-start.7 = (bf16[32,1536]{1,0:T(8,128)(2,1)S(1)}, bf16[32,1536]{1,0:T(8,128)(2,1)S(1)}, u32[]{:S(2)}, u32[]{:S(2)}) collective-permute-start(bf16[32,1536]{1,0:T(8,128)(2,1)S(1)} %get-tuple-element.43), channel_id=1, source_target_pairs={{0,4},{1,5},{2,6},{3,7},{4,0},{5,1},{6,2},{7,3},{8,12},{9,13},{10,... | collective-permute-start | bytes 294920 | tf_op jit(solution)/shard_map/ppermute | solution.py:221
  31.9 0.3 collective-permute-start.8
  32.3 0.0 collective-permute-done.4.refs_1_
  32.3 2.4 %collective-permute-start.9 = (bf16[32,1536]{1,0:T(8,128)(2,1)S(1)}, bf16[32,1536]{1,0:T(8,128)(2,1)S(1)}, u32[]{:S(2)}, u32[]{:S(2)}) collective-permute-start(bf16[32,1536]{1,0:T(8,128)(2,1)S(1)} %get-tuple-element.45), channel_id=1, source_target_pairs={{0,6},{1,7},{2,4},{3,5},{4,2},{5,3},{6,0},{7,1},{8,14},{9,15},{10,... | collective-permute-start | bytes 294920 | tf_op jit(solution)/shard_map/ppermute | solution.py:221
  34.6 4.0 %collective-permute-done.5.refs_2_ = bf16[32,1536]{1,0:T(8,128)(2,1)S(1)} collective-permute-done((bf16[32,1536]{1,0:T(8,128)(2,1)S(1)}, bf16[32,1536]{1,0:T(8,128)(2,1)S(1)}, u32[]{:S(2)}, u32[]{:S(2)}) %collective-permute-start.5) | collective-permute-done | bytes 98336 | tf_op jit(solution)/shard_map/ppermute | solution.py:221
  38.7 0.0 collective-permute-start.10
  38.7 3.3 %collective-permute-done.6.refs_3_ = bf16[32,1536]{1,0:T(8,128)(2,1)S(1)} collective-permute-done((bf16[32,1536]{1,0:T(8,128)(2,1)S(1)}, bf16[32,1536]{1,0:T(8,128)(2,1)S(1)}, u32[]{:S(2)}, u32[]{:S(2)}) %collective-permute-start.6) | collective-permute-done | bytes 98336 | tf_op jit(solution)/shard_map/ppermute | solution.py:221
  42.0 7.4 %collective-permute-done.7.refs_4_ = bf16[32,1536]{1,0:T(8,128)(2,1)S(1)} collective-permute-done((bf16[32,1536]{1,0:T(8,128)(2,1)S(1)}, bf16[32,1536]{1,0:T(8,128)(2,1)S(1)}, u32[]{:S(2)}, u32[]{:S(2)}) %collective-permute-start.7) | collective-permute-done | bytes 98336 | tf_op jit(solution)/shard_map/ppermute | solution.py:221
  49.4 2.1 %collective-permute-done.8.refs_5_ = bf16[32,1536]{1,0:T(8,128)(2,1)S(1)} collective-permute-done((bf16[32,1536]{1,0:T(8,128)(2,1)S(1)}, bf16[32,1536]{1,0:T(8,128)(2,1)S(1)}, u32[]{:S(2)}, u32[]{:S(2)}) %collective-permute-start.8) | collective-permute-done | bytes 98336 | tf_op jit(solution)/shard_map/ppermute | solution.py:221
  51.5 5.1 %collective-permute-done.9.refs_6_ = bf16[32,1536]{1,0:T(8,128)(2,1)S(1)} collective-permute-done((bf16[32,1536]{1,0:T(8,128)(2,1)S(1)}, bf16[32,1536]{1,0:T(8,128)(2,1)S(1)}, u32[]{:S(2)}, u32[]{:S(2)}) %collective-permute-start.9) | collective-permute-done | bytes 98336 | tf_op jit(solution)/shard_map/ppermute | solution.py:221
  56.6 1.2 %collective-permute-done.10.refs_7_ = bf16[32,1536]{1,0:T(8,128)(2,1)S(1)} collective-permute-done((bf16[32,1536]{1,0:T(8,128)(2,1)S(1)}, bf16[32,1536]{1,0:T(8,128)(2,1)S(1)}, u32[]{:S(2)}, u32[]{:S(2)}) %collective-permute-start.10) | collective-permute-done | bytes 98336 | tf_op jit(solution)/shard_map/ppermute | solution.py:221
  57.8 0.0 all-to-all-done.direct_ref
  57.8 1.6 %shard_map.59 = bf16[32,32768]{1,0:T(8,128)(2,1)} custom-call(bf16[16,32,1280]{2,1,0:T(8,128)(2,1)S(1)} %all-to-all-done.direct_ref, bf16[32,1536]{1,0:T(8,128)(2,1)S(1)} %get-tuple-element.39.refs_0_, bf16[32,1536]{1,0:T(8,128)(2,1)S(1)} %collective-permute-done.4.refs_1_, bf16[32,1536]{1,0:T(8,128)(2,1)S(1)} %collective-permute-done.5.refs_2_, ...), custom_call_target="tpu_custom_call" | custom-call | bytes 4194304 | tf_op jit(solution)/shard_map/pallas_call | solution.py:201
Async XLA Ops:
  0.0 9.8 %collective-permute-start = (bf16[32,256]{1,0:T(8,128)(2,1)}, bf16[32,256]{1,0:T(8,128)(2,1)S(1)}, u32[]{:S(2)}, u32[]{:S(2)}) collective-permute-start(bf16[32,256]{1,0:T(8,128)(2,1)} %param.5), channel_id=1, source_target_pairs={{0,4},{1,5},{2,6},{3,7},{4,0},{5,1},{6,2},{7,3},{8,12},{9,13},{10,... | collective-permute-start | bytes 49160 | tf_op jit(solution)/shard_map/ppermute | solution.py:221
  3.0 6.8 %collective-permute-start.2 = (bf16[32,256]{1,0:T(8,128)(2,1)}, bf16[32,256]{1,0:T(8,128)(2,1)S(1)}, u32[]{:S(2)}, u32[]{:S(2)}) collective-permute-start(bf16[32,256]{1,0:T(8,128)(2,1)} %param.5), channel_id=1, source_target_pairs={{0,12},{1,13},{2,14},{3,15},{4,8},{5,9},{6,10},{7,11},{8,4},{9,5},... | collective-permute-start | bytes 49160 | tf_op jit(solution)/shard_map/ppermute | solution.py:221
  5.5 5.1 %collective-permute-start.1 = (bf16[32,256]{1,0:T(8,128)(2,1)}, bf16[32,256]{1,0:T(8,128)(2,1)S(1)}, u32[]{:S(2)}, u32[]{:S(2)}) collective-permute-start(bf16[32,256]{1,0:T(8,128)(2,1)} %param.5), channel_id=1, source_target_pairs={{0,8},{1,9},{2,10},{3,11},{4,12},{5,13},{6,14},{7,15},{8,0},{9,1},... | collective-permute-start | bytes 49160 | tf_op jit(solution)/shard_map/ppermute | solution.py:221
  6.9 20.0 %collective-permute-start.3 = (bf16[768,256]{1,0:T(8,128)(2,1)S(1)}, bf16[768,256]{1,0:T(8,128)(2,1)S(1)}, u32[]{:S(2)}, u32[]{:S(2)}) collective-permute-start(bf16[768,256]{1,0:T(8,128)(2,1)S(1)} %get-tuple-element.30.tgt_ref), channel_id=1, source_target_pairs={{0,8},{1,9},{2,10},{3,11},{4,12},{5,13},{6,14},{7,15},{8,0},{9,1},... | collective-permute-start | bytes 1179656 | tf_op jit(solution)/shard_map/ppermute | solution.py:221
  21.1 36.7 %all-to-all-start = ((bf16[16,32,1280]{2,1,0:T(8,128)(2,1)}), bf16[16,32,1280]{2,1,0:T(8,128)(2,1)S(1)}, u32[]{:S(2)}, u32[]{:S(2)}) async-start(bf16[16,32,1280]{2,1,0:T(8,128)(2,1)} %bitcast.7), calls=%async_computation | async-start | bytes 2621440 | tf_op jit(solution)/shard_map/all_to_all | solution.py:232
  28.6 3.6 %collective-permute-start.4 = (bf16[32,1536]{1,0:T(8,128)(2,1)S(1)}, bf16[32,1536]{1,0:T(8,128)(2,1)S(1)}, u32[]{:S(2)}, u32[]{:S(2)}) collective-permute-start(bf16[32,1536]{1,0:T(8,128)(2,1)S(1)} %get-tuple-element.40), channel_id=1, source_target_pairs={{0,1},{1,0},{2,3},{3,2},{4,5},{5,4},{6,7},{7,6},{8,9},{9,8},{10,11... | collective-permute-start | bytes 294920 | tf_op jit(solution)/shard_map/ppermute | solution.py:221
  28.7 10.0 %collective-permute-start.5 = (bf16[32,1536]{1,0:T(8,128)(2,1)S(1)}, bf16[32,1536]{1,0:T(8,128)(2,1)S(1)}, u32[]{:S(2)}, u32[]{:S(2)}) collective-permute-start(bf16[32,1536]{1,0:T(8,128)(2,1)S(1)} %get-tuple-element.41), channel_id=1, source_target_pairs={{0,2},{1,3},{2,0},{3,1},{4,6},{5,7},{6,4},{7,5},{8,10},{9,11},{10,... | collective-permute-start | bytes 294920 | tf_op jit(solution)/shard_map/ppermute | solution.py:221
  30.3 11.7 %collective-permute-start.6 = (bf16[32,1536]{1,0:T(8,128)(2,1)S(1)}, bf16[32,1536]{1,0:T(8,128)(2,1)S(1)}, u32[]{:S(2)}, u32[]{:S(2)}) collective-permute-start(bf16[32,1536]{1,0:T(8,128)(2,1)S(1)} %get-tuple-element.42), channel_id=1, source_target_pairs={{0,3},{1,2},{2,1},{3,0},{4,7},{5,6},{6,5},{7,4},{8,11},{9,10},{10,... | collective-permute-start | bytes 294920 | tf_op jit(solution)/shard_map/ppermute | solution.py:221
  30.6 18.8 %collective-permute-start.7 = (bf16[32,1536]{1,0:T(8,128)(2,1)S(1)}, bf16[32,1536]{1,0:T(8,128)(2,1)S(1)}, u32[]{:S(2)}, u32[]{:S(2)}) collective-permute-start(bf16[32,1536]{1,0:T(8,128)(2,1)S(1)} %get-tuple-element.43), channel_id=1, source_target_pairs={{0,4},{1,5},{2,6},{3,7},{4,0},{5,1},{6,2},{7,3},{8,12},{9,13},{10,... | collective-permute-start | bytes 294920 | tf_op jit(solution)/shard_map/ppermute | solution.py:221
  31.9 19.6 %collective-permute-start.8 = (bf16[32,1536]{1,0:T(8,128)(2,1)S(1)}, bf16[32,1536]{1,0:T(8,128)(2,1)S(1)}, u32[]{:S(2)}, u32[]{:S(2)}) collective-permute-start(bf16[32,1536]{1,0:T(8,128)(2,1)S(1)} %get-tuple-element.44), channel_id=1, source_target_pairs={{0,5},{1,4},{2,7},{3,6},{4,1},{5,0},{6,3},{7,2},{8,13},{9,12},{10,... | collective-permute-start | bytes 294920 | tf_op jit(solution)/shard_map/ppermute | solution.py:221
  32.3 24.3 %collective-permute-start.9 = (bf16[32,1536]{1,0:T(8,128)(2,1)S(1)}, bf16[32,1536]{1,0:T(8,128)(2,1)S(1)}, u32[]{:S(2)}, u32[]{:S(2)}) collective-permute-start(bf16[32,1536]{1,0:T(8,128)(2,1)S(1)} %get-tuple-element.45), channel_id=1, source_target_pairs={{0,6},{1,7},{2,4},{3,5},{4,2},{5,3},{6,0},{7,1},{8,14},{9,15},{10,... | collective-permute-start | bytes 294920 | tf_op jit(solution)/shard_map/ppermute | solution.py:221
  38.7 19.1 %collective-permute-start.10 = (bf16[32,1536]{1,0:T(8,128)(2,1)S(1)}, bf16[32,1536]{1,0:T(8,128)(2,1)S(1)}, u32[]{:S(2)}, u32[]{:S(2)}) collective-permute-start(bf16[32,1536]{1,0:T(8,128)(2,1)S(1)} %get-tuple-element.46), channel_id=1, source_target_pairs={{0,7},{1,6},{2,5},{3,4},{4,3},{5,2},{6,1},{7,0},{8,15},{9,14},{10,... | collective-permute-start | bytes 294920 | tf_op jit(solution)/shard_map/ppermute | solution.py:221

commit v3 on v2

--- a/solution.py
+++ b/solution.py
@@ -18,19 +18,31 @@
 VMEM = pl.BlockSpec(memory_space=pltpu.VMEM)
 
 
+def partners(group):
+    return list(range(group))[::-1]
+
+
 def gelu(x):
     return x * (lax.erf(x * 0.7071067811865476) * 0.5 + 0.5)
 
 
-def block_tokens(source, target, w_ref, b_ref, p_ref, scale):
-    cost = lax.dot_general(
-        source, target, (((1,), (1,)), ((), ())), preferred_element_type=jnp.float32
-    )
-    cost = (cost * scale).astype(jnp.bfloat16)
-    embedded = jnp.dot(cost, w_ref[...], preferred_element_type=jnp.float32) + b_ref[...]
-    hidden = gelu(embedded).astype(jnp.bfloat16)
-    out = embedded + jnp.dot(hidden, p_ref[...], preferred_element_type=jnp.float32)
-    return out.astype(jnp.bfloat16)
+def pipeline_tokens(source, target_ref, w_ref, b_ref, p_ref, scale, store):
+    blocks = target_ref.shape[0] // WIDE
+    cost, embedded, hidden = {}, {}, {}
+    for i in range(blocks + 2):
+        if i < blocks:
+            product = lax.dot_general(
+                source, target_ref[i * WIDE:(i + 1) * WIDE, :], (((1,), (1,)), ((), ())),
+                preferred_element_type=jnp.float32,
+            )
+            cost[i] = (product * scale).astype(jnp.bfloat16)
+        if 0 <= i - 1 < blocks:
+            embed = jnp.dot(cost.pop(i - 1), w_ref[...], preferred_element_type=jnp.float32)
+            embedded[i - 1] = embed + b_ref[...]
+            hidden[i - 1] = gelu(embedded[i - 1]).astype(jnp.bfloat16)
+        if 0 <= i - 2:
+            mixed = jnp.dot(hidden.pop(i - 2), p_ref[...], preferred_element_type=jnp.float32)
+            store(i - 2, (embedded.pop(i - 2) + mixed).astype(jnp.bfloat16))
 
 
 def prepare_kernel(tgt_ref, w_in, b_in, p_in, cross_ref, rest_ref, ww_ref, wb_ref, wp_ref,
@@ -92,102 +104,122 @@
     )
 
 
-def direct_kernel(src_ref, tgt_ref, w_ref, b_ref, p_ref, out_ref, rows_ref, *, scale):
-    inner, outer, s_dev, _ = src_ref.shape
-
-    @pl.when(pl.program_id(0) == 0)
-    def _():
-        mine = lax.axis_index("src") // inner
-        for k in range(outer):
-            for j in range(inner):
-                at = pl.multiple_of(((mine ^ k) * inner + j) * s_dev, s_dev)
-                rows_ref[pl.ds(at, s_dev), :] = src_ref[j, k]
-
-    out_ref[...] = block_tokens(rows_ref[...], tgt_ref[...], w_ref, b_ref, p_ref, scale)
+def direct_kernel(src_ref, tgt_ref, w_ref, b_ref, p_ref, out_ref, *, scale):
+    inner, outer, s_dev, chans = src_ref.shape
+    height = out_ref.shape[0] // s_dev
+    mine = lax.axis_index("src") // inner
+    begin = pl.program_id(0) * height
+    rows = []
+    for r in range(height):
+        place = begin + r
+        rows.append(src_ref[lax.rem(place, inner), mine ^ (place // inner)])
+
+    def store(i, tok):
+        out_ref[:, i * WIDE:(i + 1) * WIDE] = tok
+
+    pipeline_tokens(jnp.concatenate(rows), tgt_ref, w_ref, b_ref, p_ref, scale, store)
 
 
 def direct_tokens(source, rest, wide, scale):
     inner, outer, s_dev, chans = source.shape
     px = inner * outer * s_dev
+    height = min(px, 512)
     cols = rest.shape[0]
     return pl.pallas_call(
         functools.partial(direct_kernel, scale=scale),
-        grid=(cols // WIDE,),
+        grid=(px // height,),
         in_specs=[
             pl.BlockSpec(source.shape, lambda i: (0, 0, 0, 0)),
-            pl.BlockSpec((WIDE, chans), lambda i: (i, 0)),
+            pl.BlockSpec((cols, chans), lambda i: (0, 0)),
             pl.BlockSpec((WIDE, WIDE), lambda i: (0, 0)),
             pl.BlockSpec((1, WIDE), lambda i: (0, 0)),
             pl.BlockSpec((WIDE, WIDE), lambda i: (0, 0)),
         ],
-        out_specs=pl.BlockSpec((px, WIDE), lambda i: (0, i)),
+        out_specs=pl.BlockSpec((height, cols), lambda i: (i, 0)),
         out_shape=jax.ShapeDtypeStruct((px, cols), jnp.bfloat16),
-        scratch_shapes=[pltpu.VMEM((px, chans), source.dtype)],
         compiler_params=PARAMS,
         cost_estimate=cost_of(px, cols, chans),
     )(source, rest, *wide)
 
 
 def near_kernel(src_ref, tgt_ref, w_ref, b_ref, p_ref, *rest, scale, group):
-    outs, rows_ref = rest[-1 - group:-1], rest[-1]
+    outs = rest[-group:]
     inner, _, s_dev, _ = src_ref.shape
-
-    @pl.when(pl.program_id(0) == 0)
-    def _():
-        lane = lax.rem(lax.axis_index("src"), inner)
+    lane = lax.rem(lax.axis_index("src"), inner)
+    rows = [src_ref[lane ^ (k % inner), k // inner] for k in partners(group)]
+
+    def store(i, tok):
         for k in range(group):
-            rows_ref[k * s_dev:(k + 1) * s_dev, :] = src_ref[lane ^ (k % inner), k // inner]
-
-    tok = block_tokens(rows_ref[...], tgt_ref[...], w_ref, b_ref, p_ref, scale)
-    for k in range(group):
-        outs[k][...] = tok[k * s_dev:(k + 1) * s_dev, :]
+            outs[k][:, i * WIDE:(i + 1) * WIDE] = tok[k * s_dev:(k + 1) * s_dev, :]
+
+    pipeline_tokens(jnp.concatenate(rows), tgt_ref, w_ref, b_ref, p_ref, scale, store)
 
 
 def near_tokens(source, target, held, group, wide, scale):
     _, _, s_dev, chans = source.shape
     rows = target.shape[0]
-    steps = rows // WIDE
-    skip = steps if held else 0
+    side = 1 if held else 0
     return pl.pallas_call(
         functools.partial(near_kernel, scale=scale, group=group),
-        grid=(steps,),
+        grid=(1,),
         in_specs=[
             pl.BlockSpec(source.shape, lambda i: (0, 0, 0, 0)),
-            pl.BlockSpec((WIDE, chans), lambda i: (i, 0)),
+            pl.BlockSpec((rows, chans), lambda i: (0, 0)),
             pl.BlockSpec((WIDE, WIDE), lambda i: (0, 0)),
             pl.BlockSpec((1, WIDE), lambda i: (0, 0)),
             pl.BlockSpec((WIDE, WIDE), lambda i: (0, 0)),
         ] + [ANY] * len(held),
-        out_specs=[pl.BlockSpec((s_dev, WIDE), lambda i: (0, i + skip))] * group,
+        out_specs=[pl.BlockSpec((s_dev, rows), lambda i: (0, side))] * group,
         out_shape=[jax.ShapeDtypeStruct((s_dev, 2 * rows), jnp.bfloat16)] * group,
-        scratch_shapes=[pltpu.VMEM((group * s_dev, chans), source.dtype)],
         input_output_aliases={5 + k: k for k in range(len(held))},
         compiler_params=PARAMS,
         cost_estimate=cost_of(group * s_dev, rows, chans),
     )(source, target, *wide, *held)
 
 
-def place_kernel(direct_ref, *refs):
-    parts, out_ref, sems = refs[:-2], refs[-2], refs[-1]
-    group = len(parts)
+def place_direct_kernel(direct_ref, out_ref, sems):
     n, _, tail = direct_ref.shape
-    first = parts[0].shape[1] // 2
-    stride = first + tail
-    me = lax.axis_index("src")
+    stride = out_ref.shape[1] // n
     copies = [
         pltpu.make_async_copy(
-            direct_ref.at[i], out_ref.at[:, i * stride + first:(i + 1) * stride], sems.at[i]
+            direct_ref.at[i], out_ref.at[:, (i + 1) * stride - tail:(i + 1) * stride], sems.at[i]
         )
         for i in range(n)
     ]
+    for copy in copies:
+        copy.start()
+    for copy in copies:
+        copy.wait()
+
+
+def place_direct(direct, width):
+    n, s_dev, tail = direct.shape
+    return pl.pallas_call(
+        place_direct_kernel,
+        in_specs=[ANY],
+        out_specs=ANY,
+        out_shape=jax.ShapeDtypeStruct((s_dev, width), direct.dtype),
+        scratch_shapes=[pltpu.SemaphoreType.DMA((n,))],
+        compiler_params=SMALL,
+        cost_estimate=pl.CostEstimate(flops=0, bytes_accessed=4 * n * s_dev * tail, transcendentals=0),
+    )(direct)
+
+
+def place_near_kernel(*refs):
+    parts, out_ref, sems = refs[:-3], refs[-2], refs[-1]
+    group = len(parts)
+    first = parts[0].shape[1] // 2
+    stride = out_ref.shape[1] // (2 * group)
+    me = lax.axis_index("src")
+    copies = []
     for k, part in enumerate(parts):
-        near = me ^ k
+        near = me ^ partners(group)[k]
         for side, frm in ((0, near), (1, near ^ group)):
             at = pl.multiple_of(frm * stride, 128)
             copies.append(pltpu.make_async_copy(
                 part.at[:, side * first:(side + 1) * first],
                 out_ref.at[:, pl.ds(at, first)],
-                sems.at[n + 2 * k + side],
+                sems.at[2 * k + side],
             ))
     for copy in copies:
         copy.start()
@@ -195,18 +227,17 @@
         copy.wait()
 
 
-def place(direct, parts):
-    n, s_dev, tail = direct.shape
-    width = n * (tail + parts[0].shape[1] // 2)
-    return pl.pallas_call(
-        place_kernel,
+def place_near(parts, held):
+    return pl.pallas_call(
+        place_near_kernel,
         in_specs=[ANY] * (1 + len(parts)),
         out_specs=ANY,
-        out_shape=jax.ShapeDtypeStruct((s_dev, width), jnp.bfloat16),
-        scratch_shapes=[pltpu.SemaphoreType.DMA((n + 2 * len(parts),))],
+        out_shape=jax.ShapeDtypeStruct(held.shape, held.dtype),
+        scratch_shapes=[pltpu.SemaphoreType.DMA((2 * len(parts),))],
+        input_output_aliases={len(parts): 0},
         compiler_params=SMALL,
-        cost_estimate=pl.CostEstimate(flops=0, bytes_accessed=4 * s_dev * width, transcendentals=0),
-    )(direct, *parts)
+        cost_estimate=pl.CostEstimate(flops=0, bytes_accessed=2 * held.size, transcendentals=0),
+    )(*parts, held)
 
 
 def per_device(source_feat, target_feat, conv_weight, conv_bias, proj_weight):
@@ -217,11 +248,13 @@
     group, outer = n // 2, n // INNER
     swapped = patches * SWAP_NUM // SWAP_DEN * cells
 
+    patched = target_feat.reshape(-1, chans)
+
     def exchange(x, bits):
         return lax.ppermute(x, "src", [(i, i ^ bits) for i in range(n)])
 
     crossed, rest, *wide = prepare(
-        target_feat.reshape(-1, chans), swapped, conv_weight, conv_bias, proj_weight
+        patched, swapped, conv_weight, conv_bias, proj_weight
     )
     got = exchange(crossed, group)
     column = jnp.stack([source_feat] + [exchange(source_feat, k * INNER) for k in range(1, outer)])
@@ -233,8 +266,8 @@
 
     near = near_tokens(source, crossed, [], group, wide, scale)
     near = near_tokens(source, got, near, group, wide, scale)
-    parts = [near[0]] + [exchange(near[k], k) for k in range(1, group)]
-    return place(direct, parts)
+    parts = [exchange(x, k) if k else x for x, k in zip(near, partners(group))]
+    return place_near(parts, place_direct(direct, patched.shape[0] // cells * conv_weight.shape[1] * n))
 
 
 def solution(mesh):

time: 60 us -> 57.9 us (0.965)
  Pallas kernels: 10.2 us -> 7.12 us
  waiting for transfers between devices: 24.4 us -> 25.8 us
    pallas_call x2, Pallas kernels: 3.38 us -> 1.28 us  [near_tokens(): pl.pallas_call(functools.partial(near_kernel, scale=scale, group=group),...]
    ppermute x11, waiting for transfers between devices: 24.4 us -> 25.8 us  [exchange(): return lax.ppermute(x, 'src', [(i, i ^ bits) for i in range(n)])]
    pallas_call x2 -> x3, Pallas kernels: 5.5 us -> 4.55 us  [the longest x1 2.35 us: direct_tokens(): pl.pallas_call(functools.partial(direct_kernel, scale=scale), grid=(px //...]
  transfers between devices with their start and end apart: 12 -> 12, of which waited for: 8 -> 5; matrix products, arithmetic and copies ran while one was open for 1% -> 1% of each run, Pallas kernels for 15% -> 11%
where the time goes in v3:
time: 57.9 us; the launch traced here: 57.5 us
  waiting for transfers between devices  25.8 us (45%)
  starting transfers between devices  18 us (31%)
  Pallas kernels  7.12 us (12%)
  blocking collectives  5.79 us (10%)
  other arithmetic  0.73 us (1%)
    ppermute x11, waiting for transfers between devices, exchange(): return lax.ppermute(x, 'src', [(i, i ^ bits) for i in range(n)])  25.8 us
    ppermute x11, starting transfers between devices, exchange(): return lax.ppermute(x, 'src', [(i, i ^ bits) for i in range(n)])  14.3 us
    all_gather x1, blocking collectives, per_device(): source = lax.all_gather(column, 'src', axis=0, axis_index_groups=rows)  5.79 us
    all_to_all x1, starting transfers between devices, per_device(): direct = lax.all_to_all(direct, 'src', 0, 0, tiled=True)  3.7 us
    pallas_call x1, Pallas kernels, direct_tokens(): pl.pallas_call(functools.partial(direct_kernel, scale=scale), grid=(px //...  2.35 us
    pallas_call x1, Pallas kernels, prepare(): pl.pallas_call(prepare_kernel, in_specs=[HBM] * 4, out_specs=[VMEM] * 5,...  1.3 us
    pallas_call x2, Pallas kernels, near_tokens(): pl.pallas_call(functools.partial(near_kernel, scale=scale, group=group),...  1.28 us
    pallas_call x1, Pallas kernels, place_direct(): pl.pallas_call(place_direct_kernel, in_specs=[ANY], out_specs=ANY, out_sh...  1.18 us
  transfers between devices with their start and end apart: 12, of which 5 were waited for; matrix products, arithmetic and copies ran while one was open for 1% of the time, Pallas kernels for 11%

profile of v3, /device:TPU:0, one launch (start us, length us, event | category | flops | bytes accessed | tf_op | source)
XLA Modules:
  0.0 57.5 jit_solution(9102064109019164202)
XLA Ops:
  0.0 3.0 %collective-permute-start = (bf16[32,256]{1,0:T(8,128)(2,1)}, bf16[32,256]{1,0:T(8,128)(2,1)S(1)}, u32[]{:S(2)}, u32[]{:S(2)}) collective-permute-start(bf16[32,256]{1,0:T(8,128)(2,1)} %param.5), channel_id=1, source_target_pairs={{0,4},{1,5},{2,6},{3,7},{4,0},{5,1},{6,2},{7,3},{8,12},{9,13},{10,... | collective-permute-start | bytes 49160 | tf_op jit(solution)/shard_map/ppermute | solution.py:254
  3.0 2.5 %collective-permute-start.2 = (bf16[32,256]{1,0:T(8,128)(2,1)}, bf16[32,256]{1,0:T(8,128)(2,1)S(1)}, u32[]{:S(2)}, u32[]{:S(2)}) collective-permute-start(bf16[32,256]{1,0:T(8,128)(2,1)} %param.5), channel_id=1, source_target_pairs={{0,12},{1,13},{2,14},{3,15},{4,8},{5,9},{6,10},{7,11},{8,4},{9,5},... | collective-permute-start | bytes 49160 | tf_op jit(solution)/shard_map/ppermute | solution.py:254
  5.5 0.1 collective-permute-start.1
  5.6 1.3 %shard_map.55 = (bf16[768,256]{1,0:T(8,128)(2,1)S(1)}, bf16[1280,256]{1,0:T(8,128)(2,1)S(1)}, bf16[256,256]{1,0:T(8,128)(2,1)S(1)}, f32[1,256]{1,0:T(1,128)S(1)}, bf16[256,256]{1,0:T(8,128)(2,1)S(1)}) custom-call(bf16[2048,256]{1,0:T(8,128)(2,1)} %bitcast.11, bf16[64,64]{1,0:T(8,128)(2,1)} %w_in.1, f32[1,64]{1,0:T(1,128)} %bitcast.16, bf16[64,64]{1,0:T(8,128)(2,1)} %p_in.1), custom_call_target="tpu_custom_call" | custom-call | tf_op jit(solution)/shard_map/pallas_call | solution.py:78
  6.9 2.9 %collective-permute-start.3 = (bf16[768,256]{1,0:T(8,128)(2,1)S(1)}, bf16[768,256]{1,0:T(8,128)(2,1)S(1)}, u32[]{:S(2)}, u32[]{:S(2)}) collective-permute-start(bf16[768,256]{1,0:T(8,128)(2,1)S(1)} %get-tuple-element.26.tgt_ref), channel_id=1, source_target_pairs={{0,8},{1,9},{2,10},{3,11},{4,12},{5,13},{6,14},{7,15},{8,0},{9,1},... | collective-permute-start | bytes 1179656 | tf_op jit(solution)/shard_map/ppermute | solution.py:254
  9.8 0.0 collective-permute-done
  9.8 0.0 collective-permute-done.2
  9.8 0.8 %collective-permute-done.1 = bf16[32,256]{1,0:T(8,128)(2,1)S(1)} collective-permute-done((bf16[32,256]{1,0:T(8,128)(2,1)}, bf16[32,256]{1,0:T(8,128)(2,1)S(1)}, u32[]{:S(2)}, u32[]{:S(2)}) %collective-permute-start.1) | collective-permute-done | bytes 16416 | tf_op jit(solution)/shard_map/ppermute | solution.py:254
  10.6 0.7 %pad_maximum_fusion = bf16[4,32,256]{2,1,0:T(8,128)(2,1)S(1)} fusion(bf16[1,32,256]{2,1,0:T(8,128)(2,1)S(1)} %bitcast.14, bf16[1,32,256]{2,1,0:T(8,128)(2,1)S(1)} %bitcast.15, bf16[1,32,256]{2,1,0:T(8,128)(2,1)S(1)} %bitcast.13, bf16[1,32,256]{2,1,0:T(8,128)(2,1)} %bitcast.12), kind=kLoop, calls=%fused_computation | loop fusion | flops 98304 | bytes 131072 | tf_op jit(solution)/shard_map/stack | solution.py:260
  11.3 5.8 %all-gather = bf16[16,32,256]{2,1,0:T(8,128)(2,1)S(1)} all-gather(bf16[4,32,256]{2,1,0:T(8,128)(2,1)S(1)} %pad_maximum_fusion), channel_id=2, replica_groups={{0,1,2,3},{4,5,6,7},{8,9,10,11},{12,13,14,15},{16,17,18,19},{20,21,22,2..., dimensions={0}, use_global_device_ids=true | all-gather | bytes 327680 | tf_op jit(solution)/shard_map/all_gather | solution.py:262
  17.1 2.4 %shard_map.58 = bf16[512,1280]{1,0:T(8,128)(2,1)} custom-call(bf16[4,4,32,256]{3,2,1,0:T(8,128)(2,1)S(1)} %bitcast.8, bf16[1280,256]{1,0:T(8,128)(2,1)S(1)} %get-tuple-element.46.tgt_ref, bf16[256,256]{1,0:T(8,128)(2,1)S(1)} %get-tuple-element.27.w_ref, f32[1,256]{1,0:T(1,128)S(1)} %get-tuple-element.28.b_ref, bf16[256,256]{1,0:T(8,128)(2,1)S(1)} %get-tuple-element.29.p_ref), custom_call_target="tpu_custom_call" | custom-call | flops 40265318400 | bytes 1966080 | tf_op jit(solution)/shard_map/pallas_call | solution.py:128
  19.5 3.7 %all-to-all-start = ((bf16[16,32,1280]{2,1,0:T(8,128)(2,1)}), bf16[16,32,1280]{2,1,0:T(8,128)(2,1)S(1)}, u32[]{:S(2)}, u32[]{:S(2)}) async-start(bf16[16,32,1280]{2,1,0:T(8,128)(2,1)} %bitcast.7), calls=%async_computation | async-start | bytes 2621440 | tf_op jit(solution)/shard_map/all_to_all | solution.py:265
  23.2 0.6 %shard_map.56 = (bf16[32,1536]{1,0:T(8,128)(2,1)S(1)}, bf16[32,1536]{1,0:T(8,128)(2,1)S(1)}, bf16[32,1536]{1,0:T(8,128)(2,1)S(1)}, bf16[32,1536]{1,0:T(8,128)(2,...) custom-call(bf16[4,4,32,256]{3,2,1,0:T(8,128)(2,1)S(1)} %bitcast.9, ...), custom_call_target="tpu_custom_call" | custom-call | flops 12079595520 | bytes 786432 | tf_op jit(solution)/shard_map/pallas_call | solution.py:162
  23.8 3.2 %collective-permute-done.3.tgt_ref = bf16[768,256]{1,0:T(8,128)(2,1)S(1)} collective-permute-done((bf16[768,256]{1,0:T(8,128)(2,1)S(1)}, bf16[768,256]{1,0:T(8,128)(2,1)S(1)}, u32[]{:S(2)}, u32[]{:S(2)}) %collective-permute-start.3) | collective-permute-done | bytes 393248 | tf_op jit(solution)/shard_map/ppermute | solution.py:254
  27.0 0.6 %shard_map.57 = (bf16[32,1536]{1,0:T(8,128)(2,1)S(1)}, bf16[32,1536]{1,0:T(8,128)(2,1)S(1)}, bf16[32,1536]{1,0:T(8,128)(2,1)S(1)}, bf16[32,1536]{1,0:T(8,128)(2,...) custom-call(bf16[4,4,32,256]{3,2,1,0:T(8,128)(2,1)S(1)} %bitcast.10,, ...), custom_call_target="tpu_custom_call", output_to_operand_aliasing={{0}: (5, {}), {1}: (6, {}), {2}: (7, {}), {3}: (8, {}), {4}... | custom-call | flops 12079595520 | bytes 786432 | tf_op jit(solution)/shard_map/pallas_call | solution.py:162
  27.7 0.1 collective-permute-start.4
  27.8 1.9 %collective-permute-start.5 = (bf16[32,1536]{1,0:T(8,128)(2,1)S(1)}, bf16[32,1536]{1,0:T(8,128)(2,1)S(1)}, u32[]{:S(2)}, u32[]{:S(2)}) collective-permute-start(bf16[32,1536]{1,0:T(8,128)(2,1)S(1)} %get-tuple-element.39), channel_id=1, source_target_pairs={{0,6},{1,7},{2,4},{3,5},{4,2},{5,3},{6,0},{7,1},{8,14},{9,15},{10,... | collective-permute-start | bytes 294920 | tf_op jit(solution)/shard_map/ppermute | solution.py:254
  29.6 0.8 %collective-permute-start.6 = (bf16[32,1536]{1,0:T(8,128)(2,1)S(1)}, bf16[32,1536]{1,0:T(8,128)(2,1)S(1)}, u32[]{:S(2)}, u32[]{:S(2)}) collective-permute-start(bf16[32,1536]{1,0:T(8,128)(2,1)S(1)} %get-tuple-element.40), channel_id=1, source_target_pairs={{0,5},{1,4},{2,7},{3,6},{4,1},{5,0},{6,3},{7,2},{8,13},{9,12},{10,... | collective-permute-start | bytes 294920 | tf_op jit(solution)/shard_map/ppermute | solution.py:254
  30.5 1.7 %collective-permute-start.7 = (bf16[32,1536]{1,0:T(8,128)(2,1)S(1)}, bf16[32,1536]{1,0:T(8,128)(2,1)S(1)}, u32[]{:S(2)}, u32[]{:S(2)}) collective-permute-start(bf16[32,1536]{1,0:T(8,128)(2,1)S(1)} %get-tuple-element.41), channel_id=1, source_target_pairs={{0,4},{1,5},{2,6},{3,7},{4,0},{5,1},{6,2},{7,3},{8,12},{9,13},{10,... | collective-permute-start | bytes 294920 | tf_op jit(solution)/shard_map/ppermute | solution.py:254
  32.1 0.5 collective-permute-start.8
  32.6 16.1 %collective-permute-done.4.refs_0_ = bf16[32,1536]{1,0:T(8,128)(2,1)S(1)} collective-permute-done((bf16[32,1536]{1,0:T(8,128)(2,1)S(1)}, bf16[32,1536]{1,0:T(8,128)(2,1)S(1)}, u32[]{:S(2)}, u32[]{:S(2)}) %collective-permute-start.4) | collective-permute-done | bytes 98336 | tf_op jit(solution)/shard_map/ppermute | solution.py:254
  48.7 0.9 %collective-permute-start.9 = (bf16[32,1536]{1,0:T(8,128)(2,1)S(1)}, bf16[32,1536]{1,0:T(8,128)(2,1)S(1)}, u32[]{:S(2)}, u32[]{:S(2)}) collective-permute-start(bf16[32,1536]{1,0:T(8,128)(2,1)S(1)} %get-tuple-element.43), channel_id=1, source_target_pairs={{0,2},{1,3},{2,0},{3,1},{4,6},{5,7},{6,4},{7,5},{8,10},{9,11},{10,... | collective-permute-start | bytes 294920 | tf_op jit(solution)/shard_map/ppermute | solution.py:254
  49.6 3.8 %collective-permute-done.5.refs_1_ = bf16[32,1536]{1,0:T(8,128)(2,1)S(1)} collective-permute-done((bf16[32,1536]{1,0:T(8,128)(2,1)S(1)}, bf16[32,1536]{1,0:T(8,128)(2,1)S(1)}, u32[]{:S(2)}, u32[]{:S(2)}) %collective-permute-start.5) | collective-permute-done | bytes 98336 | tf_op jit(solution)/shard_map/ppermute | solution.py:254
  53.4 0.0 collective-permute-start.10
  53.4 0.0 all-to-all-done.direct_ref
  53.4 1.2 %shard_map.59.refs_8_ = bf16[32,32768]{1,0:T(8,128)(2,1)} custom-call(bf16[16,32,1280]{2,1,0:T(8,128)(2,1)S(1)} %all-to-all-done.direct_ref), custom_call_target="tpu_custom_call" | custom-call | bytes 2621440 | tf_op jit(solution)/shard_map/pallas_call | solution.py:197
  54.6 0.0 collective-permute-done.6.refs_2_
  54.6 1.9 %collective-permute-done.7.refs_3_ = bf16[32,1536]{1,0:T(8,128)(2,1)S(1)} collective-permute-done((bf16[32,1536]{1,0:T(8,128)(2,1)S(1)}, bf16[32,1536]{1,0:T(8,128)(2,1)S(1)}, u32[]{:S(2)}, u32[]{:S(2)}) %collective-permute-start.7) | collective-permute-done | bytes 98336 | tf_op jit(solution)/shard_map/ppermute | solution.py:254
  56.5 0.0 collective-permute-done.8.refs_4_
  56.5 0.0 collective-permute-done.9.refs_5_
  56.5 0.0 collective-permute-done.10.refs_6_
  56.5 1.0 %shard_map.60 = bf16[32,32768]{1,0:T(8,128)(2,1)} custom-call(bf16[32,1536]{1,0:T(8,128)(2,1)S(1)} %collective-permute-done.4.refs_0_, bf16[32,1536]{1,0:T(8,128)(2,1)S(1)} %collective-permute-done.5.refs_1_, bf16[32,1536]{1,0:T(8,128)(2,1)S(1)} %collective-permute-done.6.refs_2_, ...), custom_call_target="tpu_custom_call", output_to_operand_aliasing={{}: (8, {})} | custom-call | bytes 2097152 | tf_op jit(solution)/shard_map/pallas_call | solution.py:231
Async XLA Ops:
  0.0 9.8 %collective-permute-start = (bf16[32,256]{1,0:T(8,128)(2,1)}, bf16[32,256]{1,0:T(8,128)(2,1)S(1)}, u32[]{:S(2)}, u32[]{:S(2)}) collective-permute-start(bf16[32,256]{1,0:T(8,128)(2,1)} %param.5), channel_id=1, source_target_pairs={{0,4},{1,5},{2,6},{3,7},{4,0},{5,1},{6,2},{7,3},{8,12},{9,13},{10,... | collective-permute-start | bytes 49160 | tf_op jit(solution)/shard_map/ppermute | solution.py:254
  3.0 6.8 %collective-permute-start.2 = (bf16[32,256]{1,0:T(8,128)(2,1)}, bf16[32,256]{1,0:T(8,128)(2,1)S(1)}, u32[]{:S(2)}, u32[]{:S(2)}) collective-permute-start(bf16[32,256]{1,0:T(8,128)(2,1)} %param.5), channel_id=1, source_target_pairs={{0,12},{1,13},{2,14},{3,15},{4,8},{5,9},{6,10},{7,11},{8,4},{9,5},... | collective-permute-start | bytes 49160 | tf_op jit(solution)/shard_map/ppermute | solution.py:254
  5.5 5.1 %collective-permute-start.1 = (bf16[32,256]{1,0:T(8,128)(2,1)}, bf16[32,256]{1,0:T(8,128)(2,1)S(1)}, u32[]{:S(2)}, u32[]{:S(2)}) collective-permute-start(bf16[32,256]{1,0:T(8,128)(2,1)} %param.5), channel_id=1, source_target_pairs={{0,8},{1,9},{2,10},{3,11},{4,12},{5,13},{6,14},{7,15},{8,0},{9,1},... | collective-permute-start | bytes 49160 | tf_op jit(solution)/shard_map/ppermute | solution.py:254
  6.9 20.1 %collective-permute-start.3 = (bf16[768,256]{1,0:T(8,128)(2,1)S(1)}, bf16[768,256]{1,0:T(8,128)(2,1)S(1)}, u32[]{:S(2)}, u32[]{:S(2)}) collective-permute-start(bf16[768,256]{1,0:T(8,128)(2,1)S(1)} %get-tuple-element.26.tgt_ref), channel_id=1, source_target_pairs={{0,8},{1,9},{2,10},{3,11},{4,12},{5,13},{6,14},{7,15},{8,0},{9,1},... | collective-permute-start | bytes 1179656 | tf_op jit(solution)/shard_map/ppermute | solution.py:254
  19.5 33.9 %all-to-all-start = ((bf16[16,32,1280]{2,1,0:T(8,128)(2,1)}), bf16[16,32,1280]{2,1,0:T(8,128)(2,1)S(1)}, u32[]{:S(2)}, u32[]{:S(2)}) async-start(bf16[16,32,1280]{2,1,0:T(8,128)(2,1)} %bitcast.7), calls=%async_computation | async-start | bytes 2621440 | tf_op jit(solution)/shard_map/all_to_all | solution.py:265
  27.7 21.0 %collective-permute-start.4 = (bf16[32,1536]{1,0:T(8,128)(2,1)S(1)}, bf16[32,1536]{1,0:T(8,128)(2,1)S(1)}, u32[]{:S(2)}, u32[]{:S(2)}) collective-permute-start(bf16[32,1536]{1,0:T(8,128)(2,1)S(1)} %get-tuple-element.38), channel_id=1, source_target_pairs={{0,7},{1,6},{2,5},{3,4},{4,3},{5,2},{6,1},{7,0},{8,15},{9,14},{10,... | collective-permute-start | bytes 294920 | tf_op jit(solution)/shard_map/ppermute | solution.py:254
  27.8 25.6 %collective-permute-start.5 = (bf16[32,1536]{1,0:T(8,128)(2,1)S(1)}, bf16[32,1536]{1,0:T(8,128)(2,1)S(1)}, u32[]{:S(2)}, u32[]{:S(2)}) collective-permute-start(bf16[32,1536]{1,0:T(8,128)(2,1)S(1)} %get-tuple-element.39), channel_id=1, source_target_pairs={{0,6},{1,7},{2,4},{3,5},{4,2},{5,3},{6,0},{7,1},{8,14},{9,15},{10,... | collective-permute-start | bytes 294920 | tf_op jit(solution)/shard_map/ppermute | solution.py:254
  29.6 24.9 %collective-permute-start.6 = (bf16[32,1536]{1,0:T(8,128)(2,1)S(1)}, bf16[32,1536]{1,0:T(8,128)(2,1)S(1)}, u32[]{:S(2)}, u32[]{:S(2)}) collective-permute-start(bf16[32,1536]{1,0:T(8,128)(2,1)S(1)} %get-tuple-element.40), channel_id=1, source_target_pairs={{0,5},{1,4},{2,7},{3,6},{4,1},{5,0},{6,3},{7,2},{8,13},{9,12},{10,... | collective-permute-start | bytes 294920 | tf_op jit(solution)/shard_map/ppermute | solution.py:254
  30.5 26.0 %collective-permute-start.7 = (bf16[32,1536]{1,0:T(8,128)(2,1)S(1)}, bf16[32,1536]{1,0:T(8,128)(2,1)S(1)}, u32[]{:S(2)}, u32[]{:S(2)}) collective-permute-start(bf16[32,1536]{1,0:T(8,128)(2,1)S(1)} %get-tuple-element.41), channel_id=1, source_target_pairs={{0,4},{1,5},{2,6},{3,7},{4,0},{5,1},{6,2},{7,3},{8,12},{9,13},{10,... | collective-permute-start | bytes 294920 | tf_op jit(solution)/shard_map/ppermute | solution.py:254
  32.1 24.4 %collective-permute-start.8 = (bf16[32,1536]{1,0:T(8,128)(2,1)S(1)}, bf16[32,1536]{1,0:T(8,128)(2,1)S(1)}, u32[]{:S(2)}, u32[]{:S(2)}) collective-permute-start(bf16[32,1536]{1,0:T(8,128)(2,1)S(1)} %get-tuple-element.42), channel_id=1, source_target_pairs={{0,3},{1,2},{2,1},{3,0},{4,7},{5,6},{6,5},{7,4},{8,11},{9,10},{10,... | collective-permute-start | bytes 294920 | tf_op jit(solution)/shard_map/ppermute | solution.py:254
  48.7 7.8 %collective-permute-start.9 = (bf16[32,1536]{1,0:T(8,128)(2,1)S(1)}, bf16[32,1536]{1,0:T(8,128)(2,1)S(1)}, u32[]{:S(2)}, u32[]{:S(2)}) collective-permute-start(bf16[32,1536]{1,0:T(8,128)(2,1)S(1)} %get-tuple-element.43), channel_id=1, source_target_pairs={{0,2},{1,3},{2,0},{3,1},{4,6},{5,7},{6,4},{7,5},{8,10},{9,11},{10,... | collective-permute-start | bytes 294920 | tf_op jit(solution)/shard_map/ppermute | solution.py:254
  53.4 3.1 %collective-permute-start.10 = (bf16[32,1536]{1,0:T(8,128)(2,1)S(1)}, bf16[32,1536]{1,0:T(8,128)(2,1)S(1)}, u32[]{:S(2)}, u32[]{:S(2)}) collective-permute-start(bf16[32,1536]{1,0:T(8,128)(2,1)S(1)} %get-tuple-element.44), channel_id=1, source_target_pairs={{0,1},{1,0},{2,3},{3,2},{4,5},{5,4},{6,7},{7,6},{8,9},{9,8},{10,11... | collective-permute-start | bytes 294920 | tf_op jit(solution)/shard_map/ppermute | solution.py:254

commit v4 on v3

--- a/solution.py
+++ b/solution.py
@@ -10,7 +10,7 @@
 WIDE = 256
 INNER = 4
 SWAP_NUM, SWAP_DEN = 3, 8
-COVER = 40
+COVER = 50
 PARAMS = pltpu.CompilerParams(vmem_limit_bytes=20 << 20)
 SMALL = pltpu.CompilerParams(vmem_limit_bytes=4 << 20)
 ANY = pl.BlockSpec(memory_space=pl.ANY)
@@ -18,8 +18,12 @@
 VMEM = pl.BlockSpec(memory_space=pltpu.VMEM)
 
 
+def pieces(outer):
+    return [0, outer // 2] + [k for k in range(1, outer) if k != outer // 2]
+
+
 def partners(group):
-    return list(range(group))[::-1]
+    return [*range(1, INNER), *range(group - 1, INNER - 1, -1), 0]
 
 
 def gelu(x):
@@ -108,11 +112,13 @@
     inner, outer, s_dev, chans = src_ref.shape
     height = out_ref.shape[0] // s_dev
     mine = lax.axis_index("src") // inner
-    begin = pl.program_id(0) * height
+    begin = pl.program_id(0) * (height // inner)
     rows = []
     for r in range(height):
-        place = begin + r
-        rows.append(src_ref[lax.rem(place, inner), mine ^ (place // inner)])
+        bits = mine ^ (begin + r // inner)
+        at = jnp.where(bits < outer // 2, bits + 1, bits)
+        at = jnp.where(bits == outer // 2, 1, jnp.where(bits == 0, 0, at))
+        rows.append(src_ref[r % inner, at])
 
     def store(i, tok):
         out_ref[:, i * WIDE:(i + 1) * WIDE] = tok
@@ -144,9 +150,9 @@
 
 def near_kernel(src_ref, tgt_ref, w_ref, b_ref, p_ref, *rest, scale, group):
     outs = rest[-group:]
-    inner, _, s_dev, _ = src_ref.shape
+    inner, outer, s_dev, _ = src_ref.shape
     lane = lax.rem(lax.axis_index("src"), inner)
-    rows = [src_ref[lane ^ (k % inner), k // inner] for k in partners(group)]
+    rows = [src_ref[lane ^ (k % inner), pieces(outer).index(k // inner)] for k in partners(group)]
 
     def store(i, tok):
         for k in range(group):
@@ -214,7 +220,7 @@
     copies = []
     for k, part in enumerate(parts):
         near = me ^ partners(group)[k]
-        for side, frm in ((0, near), (1, near ^ group)):
+        for side, frm in ((0, near), (1, near ^ (2 * group - INNER))):
             at = pl.multiple_of(frm * stride, 128)
             copies.append(pltpu.make_async_copy(
                 part.at[:, side * first:(side + 1) * first],
@@ -256,8 +262,8 @@
     crossed, rest, *wide = prepare(
         patched, swapped, conv_weight, conv_bias, proj_weight
     )
-    got = exchange(crossed, group)
-    column = jnp.stack([source_feat] + [exchange(source_feat, k * INNER) for k in range(1, outer)])
+    got = exchange(crossed, n - INNER)
+    column = jnp.stack([exchange(source_feat, k * INNER) if k else source_feat for k in pieces(outer)])
     rows = [list(range(i, i + INNER)) for i in range(0, n, INNER)]
     source = lax.all_gather(column, "src", axis=0, axis_index_groups=rows)
 

time: 57.9 us -> 57 us (0.984)
  waiting for transfers between devices: 25.8 us -> 22.3 us
  starting transfers between devices: 18 us -> 20.7 us
    ppermute x11, waiting for transfers between devices: 25.8 us -> 8.69 us  [exchange(): return lax.ppermute(x, 'src', [(i, i ^ bits) for i in range(n)])]
    all_to_all x1, waiting for transfers between devices: 0.01 us -> 13.6 us  [per_device(): direct = lax.all_to_all(direct, 'src', 0, 0, tiled=True)]
    ppermute x11, starting transfers between devices: 14.3 us -> 16.5 us  [exchange(): return lax.ppermute(x, 'src', [(i, i ^ bits) for i in range(n)])]
where the time goes in v4:
time: 57 us; the launch traced here: 56.7 us
  waiting for transfers between devices  22.3 us (39%)
  starting transfers between devices  20.7 us (36%)
  Pallas kernels  7.12 us (12%)
  blocking collectives  5.79 us (10%)
  other arithmetic  0.73 us (1%)
    ppermute x11, starting transfers between devices, exchange(): return lax.ppermute(x, 'src', [(i, i ^ bits) for i in range(n)])  16.5 us
    all_to_all x1, waiting for transfers between devices, per_device(): direct = lax.all_to_all(direct, 'src', 0, 0, tiled=True)  13.6 us
    ppermute x11, waiting for transfers between devices, exchange(): return lax.ppermute(x, 'src', [(i, i ^ bits) for i in range(n)])  8.69 us
    all_gather x1, blocking collectives, per_device(): source = lax.all_gather(column, 'src', axis=0, axis_index_groups=rows)  5.79 us
    all_to_all x1, starting transfers between devices, per_device(): direct = lax.all_to_all(direct, 'src', 0, 0, tiled=True)  4.22 us
    pallas_call x1, Pallas kernels, direct_tokens(): pl.pallas_call(functools.partial(direct_kernel, scale=scale), grid=(px //...  2.36 us
    pallas_call x1, Pallas kernels, prepare(): pl.pallas_call(prepare_kernel, in_specs=[HBM] * 4, out_specs=[VMEM] * 5,...  1.3 us
    pallas_call x2, Pallas kernels, near_tokens(): pl.pallas_call(functools.partial(near_kernel, scale=scale, group=group),...  1.29 us
  transfers between devices with their start and end apart: 12, of which 5 were waited for; matrix products, arithmetic and copies ran while one was open for 1% of the time, Pallas kernels for 11%

profile of v4, /device:TPU:0, one launch (start us, length us, event | category | flops | bytes accessed | tf_op | source)
XLA Modules:
  0.0 56.7 jit_solution(16990620833651228618)
XLA Ops:
  0.0 4.0 %collective-permute-start = (bf16[32,256]{1,0:T(8,128)(2,1)}, bf16[32,256]{1,0:T(8,128)(2,1)S(1)}, u32[]{:S(2)}, u32[]{:S(2)}) collective-permute-start(bf16[32,256]{1,0:T(8,128)(2,1)} %param.5), channel_id=1, source_target_pairs={{0,8},{1,9},{2,10},{3,11},{4,12},{5,13},{6,14},{7,15},{8,0},{9,1},... | collective-permute-start | bytes 49160 | tf_op jit(solution)/shard_map/ppermute | solution.py:260
  4.0 1.3 %collective-permute-start.2 = (bf16[32,256]{1,0:T(8,128)(2,1)}, bf16[32,256]{1,0:T(8,128)(2,1)S(1)}, u32[]{:S(2)}, u32[]{:S(2)}) collective-permute-start(bf16[32,256]{1,0:T(8,128)(2,1)} %param.5), channel_id=1, source_target_pairs={{0,12},{1,13},{2,14},{3,15},{4,8},{5,9},{6,10},{7,11},{8,4},{9,5},... | collective-permute-start | bytes 49160 | tf_op jit(solution)/shard_map/ppermute | solution.py:260
  5.4 0.2 collective-permute-start.1
  5.6 1.3 %shard_map.55 = (bf16[768,256]{1,0:T(8,128)(2,1)S(1)}, bf16[1280,256]{1,0:T(8,128)(2,1)S(1)}, bf16[256,256]{1,0:T(8,128)(2,1)S(1)}, f32[1,256]{1,0:T(1,128)S(1)}, bf16[256,256]{1,0:T(8,128)(2,1)S(1)}) custom-call(bf16[2048,256]{1,0:T(8,128)(2,1)} %bitcast.11, bf16[64,64]{1,0:T(8,128)(2,1)} %w_in.1, f32[1,64]{1,0:T(1,128)} %bitcast.16, bf16[64,64]{1,0:T(8,128)(2,1)} %p_in.1), custom_call_target="tpu_custom_call" | custom-call | tf_op jit(solution)/shard_map/pallas_call | solution.py:82
  6.9 3.0 %collective-permute-start.3 = (bf16[768,256]{1,0:T(8,128)(2,1)S(1)}, bf16[768,256]{1,0:T(8,128)(2,1)S(1)}, u32[]{:S(2)}, u32[]{:S(2)}) collective-permute-start(bf16[768,256]{1,0:T(8,128)(2,1)S(1)} %get-tuple-element.26.tgt_ref), channel_id=1, source_target_pairs={{0,12},{1,13},{2,14},{3,15},{4,8},{5,9},{6,10},{7,11},{8,4},{9,5},... | collective-permute-start | bytes 1179656 | tf_op jit(solution)/shard_map/ppermute | solution.py:260
  9.9 0.0 collective-permute-done
  9.9 0.0 collective-permute-done.2
  9.9 0.0 collective-permute-done.1
  9.9 0.7 %pad_maximum_fusion = bf16[4,32,256]{2,1,0:T(8,128)(2,1)S(1)} fusion(bf16[1,32,256]{2,1,0:T(8,128)(2,1)S(1)} %bitcast.14, bf16[1,32,256]{2,1,0:T(8,128)(2,1)S(1)} %bitcast.15, bf16[1,32,256]{2,1,0:T(8,128)(2,1)S(1)} %bitcast.13, bf16[1,32,256]{2,1,0:T(8,128)(2,1)} %bitcast.12), kind=kLoop, calls=%fused_computation | loop fusion | flops 98304 | bytes 131072 | tf_op jit(solution)/shard_map/stack | solution.py:266
  10.7 5.8 %all-gather = bf16[16,32,256]{2,1,0:T(8,128)(2,1)S(1)} all-gather(bf16[4,32,256]{2,1,0:T(8,128)(2,1)S(1)} %pad_maximum_fusion), channel_id=2, replica_groups={{0,1,2,3},{4,5,6,7},{8,9,10,11},{12,13,14,15},{16,17,18,19},{20,21,22,2..., dimensions={0}, use_global_device_ids=true | all-gather | bytes 327680 | tf_op jit(solution)/shard_map/all_gather | solution.py:268
  16.4 2.4 %shard_map.58 = bf16[512,1280]{1,0:T(8,128)(2,1)} custom-call(bf16[4,4,32,256]{3,2,1,0:T(8,128)(2,1)S(1)} %bitcast.8, bf16[1280,256]{1,0:T(8,128)(2,1)S(1)} %get-tuple-element.46.tgt_ref, bf16[256,256]{1,0:T(8,128)(2,1)S(1)} %get-tuple-element.27.w_ref, f32[1,256]{1,0:T(1,128)S(1)} %get-tuple-element.28.b_ref, bf16[256,256]{1,0:T(8,128)(2,1)S(1)} %get-tuple-element.29.p_ref), custom_call_target="tpu_custom_call" | custom-call | flops 50331648000 | bytes 1966080 | tf_op jit(solution)/shard_map/pallas_call | solution.py:134
  18.8 4.2 %all-to-all-start = ((bf16[16,32,1280]{2,1,0:T(8,128)(2,1)}), bf16[16,32,1280]{2,1,0:T(8,128)(2,1)S(1)}, u32[]{:S(2)}, u32[]{:S(2)}) async-start(bf16[16,32,1280]{2,1,0:T(8,128)(2,1)} %bitcast.7), calls=%async_computation | async-start | bytes 2621440 | tf_op jit(solution)/shard_map/all_to_all | solution.py:271
  23.0 0.6 %shard_map.56 = (bf16[32,1536]{1,0:T(8,128)(2,1)S(1)}, bf16[32,1536]{1,0:T(8,128)(2,1)S(1)}, bf16[32,1536]{1,0:T(8,128)(2,1)S(1)}, bf16[32,1536]{1,0:T(8,128)(2,...) custom-call(bf16[4,4,32,256]{3,2,1,0:T(8,128)(2,1)S(1)} %bitcast.9, ...), custom_call_target="tpu_custom_call" | custom-call | flops 15099494400 | bytes 786432 | tf_op jit(solution)/shard_map/pallas_call | solution.py:168
  23.7 0.0 collective-permute-done.3.tgt_ref
  23.7 0.6 %shard_map.57 = (bf16[32,1536]{1,0:T(8,128)(2,1)S(1)}, bf16[32,1536]{1,0:T(8,128)(2,1)S(1)}, bf16[32,1536]{1,0:T(8,128)(2,1)S(1)}, bf16[32,1536]{1,0:T(8,128)(2,...) custom-call(bf16[4,4,32,256]{3,2,1,0:T(8,128)(2,1)S(1)} %bitcast.10,, ...), custom_call_target="tpu_custom_call", output_to_operand_aliasing={{0}: (5, {}), {1}: (6, {}), {2}: (7, {}), {3}: (8, {}), {4}... | custom-call | flops 15099494400 | bytes 786432 | tf_op jit(solution)/shard_map/pallas_call | solution.py:168
  24.3 0.5 collective-permute-start.4
  24.8 1.7 %collective-permute-start.5 = (bf16[32,1536]{1,0:T(8,128)(2,1)S(1)}, bf16[32,1536]{1,0:T(8,128)(2,1)S(1)}, u32[]{:S(2)}, u32[]{:S(2)}) collective-permute-start(bf16[32,1536]{1,0:T(8,128)(2,1)S(1)} %get-tuple-element.39), channel_id=1, source_target_pairs={{0,2},{1,3},{2,0},{3,1},{4,6},{5,7},{6,4},{7,5},{8,10},{9,11},{10,... | collective-permute-start | bytes 294920 | tf_op jit(solution)/shard_map/ppermute | solution.py:260
  26.5 0.0 collective-permute-start.6
  26.5 4.2 %collective-permute-start.7 = (bf16[32,1536]{1,0:T(8,128)(2,1)S(1)}, bf16[32,1536]{1,0:T(8,128)(2,1)S(1)}, u32[]{:S(2)}, u32[]{:S(2)}) collective-permute-start(bf16[32,1536]{1,0:T(8,128)(2,1)S(1)} %get-tuple-element.41), channel_id=1, source_target_pairs={{0,7},{1,6},{2,5},{3,4},{4,3},{5,2},{6,1},{7,0},{8,15},{9,14},{10,... | collective-permute-start | bytes 294920 | tf_op jit(solution)/shard_map/ppermute | solution.py:260
  30.7 0.1 collective-permute-start.8
  30.8 0.0 collective-permute-done.4.refs_0_
  30.8 1.4 %collective-permute-start.9 = (bf16[32,1536]{1,0:T(8,128)(2,1)S(1)}, bf16[32,1536]{1,0:T(8,128)(2,1)S(1)}, u32[]{:S(2)}, u32[]{:S(2)}) collective-permute-start(bf16[32,1536]{1,0:T(8,128)(2,1)S(1)} %get-tuple-element.43), channel_id=1, source_target_pairs={{0,5},{1,4},{2,7},{3,6},{4,1},{5,0},{6,3},{7,2},{8,13},{9,12},{10,... | collective-permute-start | bytes 294920 | tf_op jit(solution)/shard_map/ppermute | solution.py:260
  32.2 4.9 %collective-permute-done.5.refs_1_ = bf16[32,1536]{1,0:T(8,128)(2,1)S(1)} collective-permute-done((bf16[32,1536]{1,0:T(8,128)(2,1)S(1)}, bf16[32,1536]{1,0:T(8,128)(2,1)S(1)}, u32[]{:S(2)}, u32[]{:S(2)}) %collective-permute-start.5) | collective-permute-done | bytes 98336 | tf_op jit(solution)/shard_map/ppermute | solution.py:260
  37.1 0.0 collective-permute-start.10
  37.1 13.6 %all-to-all-done.direct_ref = bf16[16,32,1280]{2,1,0:T(8,128)(2,1)S(1)} async-done(((bf16[16,32,1280]{2,1,0:T(8,128)(2,1)}), bf16[16,32,1280]{2,1,0:T(8,128)(2,1)S(1)}, u32[]{:S(2)}, u32[]{:S(2)}) %all-to-all-start) | async-done | bytes 1310752 | tf_op jit(solution)/shard_map/all_to_all | solution.py:271
  50.6 1.2 %shard_map.59.refs_8_ = bf16[32,32768]{1,0:T(8,128)(2,1)} custom-call(bf16[16,32,1280]{2,1,0:T(8,128)(2,1)S(1)} %all-to-all-done.direct_ref), custom_call_target="tpu_custom_call" | custom-call | bytes 2621440 | tf_op jit(solution)/shard_map/pallas_call | solution.py:203
  51.8 0.0 collective-permute-done.6.refs_2_
  51.8 0.0 collective-permute-done.7.refs_3_
  51.9 0.7 %collective-permute-done.8.refs_4_ = bf16[32,1536]{1,0:T(8,128)(2,1)S(1)} collective-permute-done((bf16[32,1536]{1,0:T(8,128)(2,1)S(1)}, bf16[32,1536]{1,0:T(8,128)(2,1)S(1)}, u32[]{:S(2)}, u32[]{:S(2)}) %collective-permute-start.8) | collective-permute-done | bytes 98336 | tf_op jit(solution)/shard_map/ppermute | solution.py:260
  52.5 0.5 collective-permute-done.9.refs_5_
  53.1 2.6 %collective-permute-done.10.refs_6_ = bf16[32,1536]{1,0:T(8,128)(2,1)S(1)} collective-permute-done((bf16[32,1536]{1,0:T(8,128)(2,1)S(1)}, bf16[32,1536]{1,0:T(8,128)(2,1)S(1)}, u32[]{:S(2)}, u32[]{:S(2)}) %collective-permute-start.10) | collective-permute-done | bytes 98336 | tf_op jit(solution)/shard_map/ppermute | solution.py:260
  55.7 1.0 %shard_map.60 = bf16[32,32768]{1,0:T(8,128)(2,1)} custom-call(bf16[32,1536]{1,0:T(8,128)(2,1)S(1)} %collective-permute-done.4.refs_0_, bf16[32,1536]{1,0:T(8,128)(2,1)S(1)} %collective-permute-done.5.refs_1_, bf16[32,1536]{1,0:T(8,128)(2,1)S(1)} %collective-permute-done.6.refs_2_, ...), custom_call_target="tpu_custom_call", output_to_operand_aliasing={{}: (8, {})} | custom-call | bytes 2097152 | tf_op jit(solution)/shard_map/pallas_call | solution.py:237
Async XLA Ops:
  0.0 9.9 %collective-permute-start = (bf16[32,256]{1,0:T(8,128)(2,1)}, bf16[32,256]{1,0:T(8,128)(2,1)S(1)}, u32[]{:S(2)}, u32[]{:S(2)}) collective-permute-start(bf16[32,256]{1,0:T(8,128)(2,1)} %param.5), channel_id=1, source_target_pairs={{0,8},{1,9},{2,10},{3,11},{4,12},{5,13},{6,14},{7,15},{8,0},{9,1},... | collective-permute-start | bytes 49160 | tf_op jit(solution)/shard_map/ppermute | solution.py:260
  4.0 5.9 %collective-permute-start.2 = (bf16[32,256]{1,0:T(8,128)(2,1)}, bf16[32,256]{1,0:T(8,128)(2,1)S(1)}, u32[]{:S(2)}, u32[]{:S(2)}) collective-permute-start(bf16[32,256]{1,0:T(8,128)(2,1)} %param.5), channel_id=1, source_target_pairs={{0,12},{1,13},{2,14},{3,15},{4,8},{5,9},{6,10},{7,11},{8,4},{9,5},... | collective-permute-start | bytes 49160 | tf_op jit(solution)/shard_map/ppermute | solution.py:260
  5.4 4.5 %collective-permute-start.1 = (bf16[32,256]{1,0:T(8,128)(2,1)}, bf16[32,256]{1,0:T(8,128)(2,1)S(1)}, u32[]{:S(2)}, u32[]{:S(2)}) collective-permute-start(bf16[32,256]{1,0:T(8,128)(2,1)} %param.5), channel_id=1, source_target_pairs={{0,4},{1,5},{2,6},{3,7},{4,0},{5,1},{6,2},{7,3},{8,12},{9,13},{10,... | collective-permute-start | bytes 49160 | tf_op jit(solution)/shard_map/ppermute | solution.py:260
  6.9 16.8 %collective-permute-start.3 = (bf16[768,256]{1,0:T(8,128)(2,1)S(1)}, bf16[768,256]{1,0:T(8,128)(2,1)S(1)}, u32[]{:S(2)}, u32[]{:S(2)}) collective-permute-start(bf16[768,256]{1,0:T(8,128)(2,1)S(1)} %get-tuple-element.26.tgt_ref), channel_id=1, source_target_pairs={{0,12},{1,13},{2,14},{3,15},{4,8},{5,9},{6,10},{7,11},{8,4},{9,5},... | collective-permute-start | bytes 1179656 | tf_op jit(solution)/shard_map/ppermute | solution.py:260
  18.8 31.8 %all-to-all-start = ((bf16[16,32,1280]{2,1,0:T(8,128)(2,1)}), bf16[16,32,1280]{2,1,0:T(8,128)(2,1)S(1)}, u32[]{:S(2)}, u32[]{:S(2)}) async-start(bf16[16,32,1280]{2,1,0:T(8,128)(2,1)} %bitcast.7), calls=%async_computation | async-start | bytes 2621440 | tf_op jit(solution)/shard_map/all_to_all | solution.py:271
  24.3 6.5 %collective-permute-start.4 = (bf16[32,1536]{1,0:T(8,128)(2,1)S(1)}, bf16[32,1536]{1,0:T(8,128)(2,1)S(1)}, u32[]{:S(2)}, u32[]{:S(2)}) collective-permute-start(bf16[32,1536]{1,0:T(8,128)(2,1)S(1)} %get-tuple-element.38), channel_id=1, source_target_pairs={{0,1},{1,0},{2,3},{3,2},{4,5},{5,4},{6,7},{7,6},{8,9},{9,8},{10,11... | collective-permute-start | bytes 294920 | tf_op jit(solution)/shard_map/ppermute | solution.py:260
  24.8 12.2 %collective-permute-start.5 = (bf16[32,1536]{1,0:T(8,128)(2,1)S(1)}, bf16[32,1536]{1,0:T(8,128)(2,1)S(1)}, u32[]{:S(2)}, u32[]{:S(2)}) collective-permute-start(bf16[32,1536]{1,0:T(8,128)(2,1)S(1)} %get-tuple-element.39), channel_id=1, source_target_pairs={{0,2},{1,3},{2,0},{3,1},{4,6},{5,7},{6,4},{7,5},{8,10},{9,11},{10,... | collective-permute-start | bytes 294920 | tf_op jit(solution)/shard_map/ppermute | solution.py:260
  26.5 25.3 %collective-permute-start.6 = (bf16[32,1536]{1,0:T(8,128)(2,1)S(1)}, bf16[32,1536]{1,0:T(8,128)(2,1)S(1)}, u32[]{:S(2)}, u32[]{:S(2)}) collective-permute-start(bf16[32,1536]{1,0:T(8,128)(2,1)S(1)} %get-tuple-element.40), channel_id=1, source_target_pairs={{0,3},{1,2},{2,1},{3,0},{4,7},{5,6},{6,5},{7,4},{8,11},{9,10},{10,... | collective-permute-start | bytes 294920 | tf_op jit(solution)/shard_map/ppermute | solution.py:260
  26.5 25.3 %collective-permute-start.7 = (bf16[32,1536]{1,0:T(8,128)(2,1)S(1)}, bf16[32,1536]{1,0:T(8,128)(2,1)S(1)}, u32[]{:S(2)}, u32[]{:S(2)}) collective-permute-start(bf16[32,1536]{1,0:T(8,128)(2,1)S(1)} %get-tuple-element.41), channel_id=1, source_target_pairs={{0,7},{1,6},{2,5},{3,4},{4,3},{5,2},{6,1},{7,0},{8,15},{9,14},{10,... | collective-permute-start | bytes 294920 | tf_op jit(solution)/shard_map/ppermute | solution.py:260
  30.7 21.8 %collective-permute-start.8 = (bf16[32,1536]{1,0:T(8,128)(2,1)S(1)}, bf16[32,1536]{1,0:T(8,128)(2,1)S(1)}, u32[]{:S(2)}, u32[]{:S(2)}) collective-permute-start(bf16[32,1536]{1,0:T(8,128)(2,1)S(1)} %get-tuple-element.42), channel_id=1, source_target_pairs={{0,6},{1,7},{2,4},{3,5},{4,2},{5,3},{6,0},{7,1},{8,14},{9,15},{10,... | collective-permute-start | bytes 294920 | tf_op jit(solution)/shard_map/ppermute | solution.py:260
  30.8 22.3 %collective-permute-start.9 = (bf16[32,1536]{1,0:T(8,128)(2,1)S(1)}, bf16[32,1536]{1,0:T(8,128)(2,1)S(1)}, u32[]{:S(2)}, u32[]{:S(2)}) collective-permute-start(bf16[32,1536]{1,0:T(8,128)(2,1)S(1)} %get-tuple-element.43), channel_id=1, source_target_pairs={{0,5},{1,4},{2,7},{3,6},{4,1},{5,0},{6,3},{7,2},{8,13},{9,12},{10,... | collective-permute-start | bytes 294920 | tf_op jit(solution)/shard_map/ppermute | solution.py:260
  37.1 18.6 %collective-permute-start.10 = (bf16[32,1536]{1,0:T(8,128)(2,1)S(1)}, bf16[32,1536]{1,0:T(8,128)(2,1)S(1)}, u32[]{:S(2)}, u32[]{:S(2)}) collective-permute-start(bf16[32,1536]{1,0:T(8,128)(2,1)S(1)} %get-tuple-element.44), channel_id=1, source_target_pairs={{0,4},{1,5},{2,6},{3,7},{4,0},{5,1},{6,2},{7,3},{8,12},{9,13},{10,... | collective-permute-start | bytes 294920 | tf_op jit(solution)/shard_map/ppermute | solution.py:260

commit v5 on v4

--- a/solution.py
+++ b/solution.py
@@ -49,19 +49,39 @@
             store(i - 2, (embedded.pop(i - 2) + mixed).astype(jnp.bfloat16))
 
 
-def prepare_kernel(tgt_ref, w_in, b_in, p_in, cross_ref, rest_ref, ww_ref, wb_ref, wp_ref,
+def pin(*arrays):
+    return [pltpu.with_memory_space_constraint(x, pltpu.HBM) for x in arrays]
+
+
+def crossing_kernel(tgt_ref, out_ref, sem):
+    copy = pltpu.make_async_copy(tgt_ref.at[0:out_ref.shape[0], :], out_ref, sem)
+    copy.start()
+    copy.wait()
+
+
+def crossing(patched, rows):
+    return pl.pallas_call(
+        crossing_kernel,
+        in_specs=[HBM],
+        out_specs=VMEM,
+        out_shape=jax.ShapeDtypeStruct((rows, patched.shape[1]), patched.dtype),
+        scratch_shapes=[pltpu.SemaphoreType.DMA],
+        compiler_params=SMALL,
+    )(*pin(patched))
+
+
+def prepare_kernel(tgt_ref, w_in, b_in, p_in, rest_ref, ww_ref, wb_ref, wp_ref,
                    w_ref, b_ref, p_ref, sems):
-    swapped, total = cross_ref.shape[0], tgt_ref.shape[0]
+    total = tgt_ref.shape[0]
+    large = pltpu.make_async_copy(
+        tgt_ref.at[total - rest_ref.shape[0]:total, :], rest_ref, sems.at[3]
+    )
     small = [
         pltpu.make_async_copy(w_in, w_ref, sems.at[0]),
         pltpu.make_async_copy(b_in, b_ref, sems.at[1]),
         pltpu.make_async_copy(p_in, p_ref, sems.at[2]),
     ]
-    large = [
-        pltpu.make_async_copy(tgt_ref.at[0:swapped, :], cross_ref, sems.at[3]),
-        pltpu.make_async_copy(tgt_ref.at[swapped:total, :], rest_ref, sems.at[4]),
-    ]
-    for copy in small + large:
+    for copy in [*small, large]:
         copy.start()
     ww_ref[...] = jnp.zeros_like(ww_ref)
     wp_ref[...] = jnp.zeros_like(wp_ref)
@@ -72,8 +92,7 @@
         ww_ref[i * cells:(i + 1) * cells, i * emb:(i + 1) * emb] = w_ref[...]
         wp_ref[i * emb:(i + 1) * emb, i * emb:(i + 1) * emb] = p_ref[...]
         wb_ref[:, i * emb:(i + 1) * emb] = b_ref[...]
-    for copy in large:
-        copy.wait()
+    large.wait()
 
 
 def prepare(patched, swapped, conv_weight, conv_bias, proj_weight):
@@ -82,9 +101,8 @@
     return pl.pallas_call(
         prepare_kernel,
         in_specs=[HBM] * 4,
-        out_specs=[VMEM] * 5,
+        out_specs=[VMEM] * 4,
         out_shape=[
-            jax.ShapeDtypeStruct((swapped, chans), patched.dtype),
             jax.ShapeDtypeStruct((rows - swapped, chans), patched.dtype),
             jax.ShapeDtypeStruct((WIDE, WIDE), conv_weight.dtype),
             jax.ShapeDtypeStruct((1, WIDE), conv_bias.dtype),
@@ -94,10 +112,10 @@
             pltpu.VMEM(conv_weight.shape, conv_weight.dtype),
             pltpu.VMEM(bias.shape, bias.dtype),
             pltpu.VMEM(proj_weight.shape, proj_weight.dtype),
-            pltpu.SemaphoreType.DMA((5,)),
+            pltpu.SemaphoreType.DMA((4,)),
         ],
         compiler_params=SMALL,
-    )(*[pltpu.with_memory_space_constraint(x, pltpu.HBM) for x in (patched, conv_weight, bias, proj_weight)])
+    )(*pin(patched, conv_weight, bias, proj_weight))
 
 
 def cost_of(px, cols, chans):
@@ -259,9 +277,8 @@
     def exchange(x, bits):
         return lax.ppermute(x, "src", [(i, i ^ bits) for i in range(n)])
 
-    crossed, rest, *wide = prepare(
-        patched, swapped, conv_weight, conv_bias, proj_weight
-    )
+    crossed = crossing(patched, swapped)
+    rest, *wide = prepare(patched, swapped, conv_weight, conv_bias, proj_weight)
     got = exchange(crossed, n - INNER)
     column = jnp.stack([exchange(source_feat, k * INNER) if k else source_feat for k in pieces(outer)])
     rows = [list(range(i, i + INNER)) for i in range(0, n, INNER)]

time: 57 us -> 56.5 us (level)
  Pallas kernels: 7.12 us -> 7.99 us
  other arithmetic: 0.73 us -> 0.01 us
    pallas_call x1 -> x2, Pallas kernels: 1.3 us -> 2.18 us  [the longest x1 1.17 us: prepare(): pl.pallas_call(prepare_kernel, in_specs=[HBM] * 4, out_specs=[VMEM] * 4,...]
    another operation x1, other arithmetic: 0.73 us -> 0.01 us  [per_device(): jnp.stack([exchange(source_feat, k * INNER) if k else source_feat for k i...]
  transfers between devices with their start and end apart: 12 -> 12, of which waited for: 5 -> 5; matrix products, arithmetic and copies ran while one was open for 1% -> 0% of each run, Pallas kernels for 11% -> 12%
where the time goes in v5:
time: 56.5 us; the launch traced here: 56.2 us
  waiting for transfers between devices  22 us (39%)
  starting transfers between devices  20.4 us (36%)
  Pallas kernels  7.99 us (14%)
  blocking collectives  5.79 us (10%)
    ppermute x11, starting transfers between devices, exchange(): return lax.ppermute(x, 'src', [(i, i ^ bits) for i in range(n)])  16.7 us
    all_to_all x1, waiting for transfers between devices, per_device(): direct = lax.all_to_all(direct, 'src', 0, 0, tiled=True)  13.6 us
    ppermute x11, waiting for transfers between devices, exchange(): return lax.ppermute(x, 'src', [(i, i ^ bits) for i in range(n)])  8.31 us
    all_gather x1, blocking collectives, per_device(): source = lax.all_gather(column, 'src', axis=0, axis_index_groups=rows)  5.79 us
    all_to_all x1, starting transfers between devices, per_device(): direct = lax.all_to_all(direct, 'src', 0, 0, tiled=True)  3.7 us
    pallas_call x1, Pallas kernels, direct_tokens(): pl.pallas_call(functools.partial(direct_kernel, scale=scale), grid=(px //...  2.36 us
    pallas_call x2, Pallas kernels, near_tokens(): pl.pallas_call(functools.partial(near_kernel, scale=scale, group=group),...  1.29 us
    pallas_call x1, Pallas kernels, place_direct(): pl.pallas_call(place_direct_kernel, in_specs=[ANY], out_specs=ANY, out_sh...  1.18 us
  transfers between devices with their start and end apart: 12, of which 5 were waited for; matrix products, arithmetic and copies ran while one was open for 0% of the time, Pallas kernels for 12%

profile of v5, /device:TPU:0, one launch (start us, length us, event | category | flops | bytes accessed | tf_op | source)
XLA Modules:
  0.0 56.2 jit_solution(2964731665349737123)
XLA Ops:
  0.0 0.0 copy-start
  0.0 4.0 %collective-permute-start = (bf16[32,256]{1,0:T(8,128)(2,1)}, bf16[32,256]{1,0:T(8,128)(2,1)S(1)}, u32[]{:S(2)}, u32[]{:S(2)}) collective-permute-start(bf16[32,256]{1,0:T(8,128)(2,1)} %param.5), channel_id=1, source_target_pairs={{0,8},{1,9},{2,10},{3,11},{4,12},{5,13},{6,14},{7,15},{8,0},{9,1},... | collective-permute-start | bytes 49160 | tf_op jit(solution)/shard_map/ppermute | solution.py:278
  4.0 1.3 %collective-permute-start.2 = (bf16[32,256]{1,0:T(8,128)(2,1)}, bf16[32,256]{1,0:T(8,128)(2,1)S(1)}, u32[]{:S(2)}, u32[]{:S(2)}) collective-permute-start(bf16[32,256]{1,0:T(8,128)(2,1)} %param.5), channel_id=1, source_target_pairs={{0,12},{1,13},{2,14},{3,15},{4,8},{5,9},{6,10},{7,11},{8,4},{9,5},... | collective-permute-start | bytes 49160 | tf_op jit(solution)/shard_map/ppermute | solution.py:278
  5.4 0.2 collective-permute-start.1
  5.6 1.0 %shard_map.55.tgt_ref = bf16[768,256]{1,0:T(8,128)(2,1)S(1)} custom-call(bf16[2048,256]{1,0:T(8,128)(2,1)} %bitcast.11), custom_call_target="tpu_custom_call" | custom-call | tf_op jit(solution)/shard_map/pallas_call | solution.py:63
  6.6 3.0 %collective-permute-start.3 = (bf16[768,256]{1,0:T(8,128)(2,1)S(1)}, bf16[768,256]{1,0:T(8,128)(2,1)S(1)}, u32[]{:S(2)}, u32[]{:S(2)}) collective-permute-start(bf16[768,256]{1,0:T(8,128)(2,1)S(1)} %shard_map.55.tgt_ref), channel_id=1, source_target_pairs={{0,12},{1,13},{2,14},{3,15},{4,8},{5,9},{6,10},{7,11},{8,4},{9,5},... | collective-permute-start | bytes 1179656 | tf_op jit(solution)/shard_map/ppermute | solution.py:278
  9.6 1.2 %shard_map.56 = (bf16[1280,256]{1,0:T(8,128)(2,1)S(1)}, bf16[256,256]{1,0:T(8,128)(2,1)S(1)}, f32[1,256]{1,0:T(1,128)S(1)}, bf16[256,256]{1,0:T(8,128)(2,1)S(1)}) custom-call(bf16[2048,256]{1,0:T(8,128)(2,1)} %bitcast.12, bf16[64,64]{1,0:T(8,128)(2,1)} %w_in.1, f32[1,64]{1,0:T(1,128)} %bitcast.17, bf16[64,64]{1,0:T(8,128)(2,1)} %p_in.1), custom_call_target="tpu_custom_call" | custom-call | tf_op jit(solution)/shard_map/pallas_call | solution.py:101
  10.8 0.0 collective-permute-done
  10.8 0.0 collective-permute-done.2
  10.8 0.0 collective-permute-done.1
  10.8 0.0 copy-done
  10.9 5.8 %all-gather = bf16[16,32,256]{2,1,0:T(8,128)(2,1)S(1)} all-gather(bf16[4,32,256]{2,1,0:T(8,128)(2,1)S(1)} %pad_maximum_fusion), channel_id=2, replica_groups={{0,1,2,3},{4,5,6,7},{8,9,10,11},{12,13,14,15},{16,17,18,19},{20,21,22,2..., dimensions={0}, use_global_device_ids=true | all-gather | bytes 327680 | tf_op jit(solution)/shard_map/all_gather | solution.py:285
  16.6 2.4 %shard_map.59 = bf16[512,1280]{1,0:T(8,128)(2,1)} custom-call(bf16[4,4,32,256]{3,2,1,0:T(8,128)(2,1)S(1)} %bitcast.8, bf16[1280,256]{1,0:T(8,128)(2,1)S(1)} %get-tuple-element.44.tgt_ref, bf16[256,256]{1,0:T(8,128)(2,1)S(1)} %get-tuple-element.25.w_ref, f32[1,256]{1,0:T(1,128)S(1)} %get-tuple-element.26.b_ref, bf16[256,256]{1,0:T(8,128)(2,1)S(1)} %get-tuple-element.27.p_ref), custom_call_target="tpu_custom_call" | custom-call | flops 50331648000 | bytes 1966080 | tf_op jit(solution)/shard_map/pallas_call | solution.py:152
  19.0 3.7 %all-to-all-start = ((bf16[16,32,1280]{2,1,0:T(8,128)(2,1)}), bf16[16,32,1280]{2,1,0:T(8,128)(2,1)S(1)}, u32[]{:S(2)}, u32[]{:S(2)}) async-start(bf16[16,32,1280]{2,1,0:T(8,128)(2,1)} %bitcast.7), calls=%async_computation | async-start | bytes 2621440 | tf_op jit(solution)/shard_map/all_to_all | solution.py:288
  22.7 0.6 %shard_map.57 = (bf16[32,1536]{1,0:T(8,128)(2,1)S(1)}, bf16[32,1536]{1,0:T(8,128)(2,1)S(1)}, bf16[32,1536]{1,0:T(8,128)(2,1)S(1)}, bf16[32,1536]{1,0:T(8,128)(2,...) custom-call(bf16[4,4,32,256]{3,2,1,0:T(8,128)(2,1)S(1)} %bitcast.9, ...), custom_call_target="tpu_custom_call" | custom-call | flops 15099494400 | bytes 786432 | tf_op jit(solution)/shard_map/pallas_call | solution.py:186
  23.4 0.0 collective-permute-done.3.tgt_ref
  23.4 0.6 %shard_map.58 = (bf16[32,1536]{1,0:T(8,128)(2,1)S(1)}, bf16[32,1536]{1,0:T(8,128)(2,1)S(1)}, bf16[32,1536]{1,0:T(8,128)(2,1)S(1)}, bf16[32,1536]{1,0:T(8,128)(2,...) custom-call(bf16[4,4,32,256]{3,2,1,0:T(8,128)(2,1)S(1)} %bitcast.10,, ...), custom_call_target="tpu_custom_call", output_to_operand_aliasing={{0}: (5, {}), {1}: (6, {}), {2}: (7, {}), {3}: (8, {}), {4}... | custom-call | flops 15099494400 | bytes 786432 | tf_op jit(solution)/shard_map/pallas_call | solution.py:186
  24.0 0.4 collective-permute-start.4
  24.4 1.7 %collective-permute-start.5 = (bf16[32,1536]{1,0:T(8,128)(2,1)S(1)}, bf16[32,1536]{1,0:T(8,128)(2,1)S(1)}, u32[]{:S(2)}, u32[]{:S(2)}) collective-permute-start(bf16[32,1536]{1,0:T(8,128)(2,1)S(1)} %get-tuple-element.37), channel_id=1, source_target_pairs={{0,2},{1,3},{2,0},{3,1},{4,6},{5,7},{6,4},{7,5},{8,10},{9,11},{10,... | collective-permute-start | bytes 294920 | tf_op jit(solution)/shard_map/ppermute | solution.py:278
  26.1 0.0 collective-permute-start.6
  26.1 4.5 %collective-permute-start.7 = (bf16[32,1536]{1,0:T(8,128)(2,1)S(1)}, bf16[32,1536]{1,0:T(8,128)(2,1)S(1)}, u32[]{:S(2)}, u32[]{:S(2)}) collective-permute-start(bf16[32,1536]{1,0:T(8,128)(2,1)S(1)} %get-tuple-element.39), channel_id=1, source_target_pairs={{0,7},{1,6},{2,5},{3,4},{4,3},{5,2},{6,1},{7,0},{8,15},{9,14},{10,... | collective-permute-start | bytes 294920 | tf_op jit(solution)/shard_map/ppermute | solution.py:278
  30.6 0.1 collective-permute-start.8
  30.7 0.0 collective-permute-done.4.refs_0_
  30.7 1.4 %collective-permute-start.9 = (bf16[32,1536]{1,0:T(8,128)(2,1)S(1)}, bf16[32,1536]{1,0:T(8,128)(2,1)S(1)}, u32[]{:S(2)}, u32[]{:S(2)}) collective-permute-start(bf16[32,1536]{1,0:T(8,128)(2,1)S(1)} %get-tuple-element.41), channel_id=1, source_target_pairs={{0,5},{1,4},{2,7},{3,6},{4,1},{5,0},{6,3},{7,2},{8,13},{9,12},{10,... | collective-permute-start | bytes 294920 | tf_op jit(solution)/shard_map/ppermute | solution.py:278
  32.1 4.5 %collective-permute-done.5.refs_1_ = bf16[32,1536]{1,0:T(8,128)(2,1)S(1)} collective-permute-done((bf16[32,1536]{1,0:T(8,128)(2,1)S(1)}, bf16[32,1536]{1,0:T(8,128)(2,1)S(1)}, u32[]{:S(2)}, u32[]{:S(2)}) %collective-permute-start.5) | collective-permute-done | bytes 98336 | tf_op jit(solution)/shard_map/ppermute | solution.py:278
  36.6 0.0 collective-permute-start.10
  36.6 13.6 %all-to-all-done.direct_ref = bf16[16,32,1280]{2,1,0:T(8,128)(2,1)S(1)} async-done(((bf16[16,32,1280]{2,1,0:T(8,128)(2,1)}), bf16[16,32,1280]{2,1,0:T(8,128)(2,1)S(1)}, u32[]{:S(2)}, u32[]{:S(2)}) %all-to-all-start) | async-done | bytes 1310752 | tf_op jit(solution)/shard_map/all_to_all | solution.py:288
  50.3 1.2 %shard_map.60.refs_8_ = bf16[32,32768]{1,0:T(8,128)(2,1)} custom-call(bf16[16,32,1280]{2,1,0:T(8,128)(2,1)S(1)} %all-to-all-done.direct_ref), custom_call_target="tpu_custom_call" | custom-call | bytes 2621440 | tf_op jit(solution)/shard_map/pallas_call | solution.py:221
  51.5 0.0 collective-permute-done.6.refs_2_
  51.5 0.0 collective-permute-done.7.refs_3_
  51.5 0.6 %collective-permute-done.8.refs_4_ = bf16[32,1536]{1,0:T(8,128)(2,1)S(1)} collective-permute-done((bf16[32,1536]{1,0:T(8,128)(2,1)S(1)}, bf16[32,1536]{1,0:T(8,128)(2,1)S(1)}, u32[]{:S(2)}, u32[]{:S(2)}) %collective-permute-start.8) | collective-permute-done | bytes 98336 | tf_op jit(solution)/shard_map/ppermute | solution.py:278
  52.1 0.6 collective-permute-done.9.refs_5_
  52.7 2.6 %collective-permute-done.10.refs_6_ = bf16[32,1536]{1,0:T(8,128)(2,1)S(1)} collective-permute-done((bf16[32,1536]{1,0:T(8,128)(2,1)S(1)}, bf16[32,1536]{1,0:T(8,128)(2,1)S(1)}, u32[]{:S(2)}, u32[]{:S(2)}) %collective-permute-start.10) | collective-permute-done | bytes 98336 | tf_op jit(solution)/shard_map/ppermute | solution.py:278
  55.2 1.0 %shard_map.61 = bf16[32,32768]{1,0:T(8,128)(2,1)} custom-call(bf16[32,1536]{1,0:T(8,128)(2,1)S(1)} %collective-permute-done.4.refs_0_, bf16[32,1536]{1,0:T(8,128)(2,1)S(1)} %collective-permute-done.5.refs_1_, bf16[32,1536]{1,0:T(8,128)(2,1)S(1)} %collective-permute-done.6.refs_2_, ...), custom_call_target="tpu_custom_call", output_to_operand_aliasing={{}: (8, {})} | custom-call | bytes 2097152 | tf_op jit(solution)/shard_map/pallas_call | solution.py:255
  (1 shorter events, 0.0 us)
Async XLA Ops:
  0.0 10.8 %copy-start = (bf16[32,256]{1,0:T(8,128)(2,1)S(1)}, bf16[32,256]{1,0:T(8,128)(2,1)}, u32[]{:S(2)}) copy-start(bf16[32,256]{1,0:T(8,128)(2,1)} %param.5) | copy-start | bytes 49156
  0.0 10.8 %collective-permute-start = (bf16[32,256]{1,0:T(8,128)(2,1)}, bf16[32,256]{1,0:T(8,128)(2,1)S(1)}, u32[]{:S(2)}, u32[]{:S(2)}) collective-permute-start(bf16[32,256]{1,0:T(8,128)(2,1)} %param.5), channel_id=1, source_target_pairs={{0,8},{1,9},{2,10},{3,11},{4,12},{5,13},{6,14},{7,15},{8,0},{9,1},... | collective-permute-start | bytes 49160 | tf_op jit(solution)/shard_map/ppermute | solution.py:278
  4.0 6.8 %collective-permute-start.2 = (bf16[32,256]{1,0:T(8,128)(2,1)}, bf16[32,256]{1,0:T(8,128)(2,1)S(1)}, u32[]{:S(2)}, u32[]{:S(2)}) collective-permute-start(bf16[32,256]{1,0:T(8,128)(2,1)} %param.5), channel_id=1, source_target_pairs={{0,12},{1,13},{2,14},{3,15},{4,8},{5,9},{6,10},{7,11},{8,4},{9,5},... | collective-permute-start | bytes 49160 | tf_op jit(solution)/shard_map/ppermute | solution.py:278
  5.4 5.4 %collective-permute-start.1 = (bf16[32,256]{1,0:T(8,128)(2,1)}, bf16[32,256]{1,0:T(8,128)(2,1)S(1)}, u32[]{:S(2)}, u32[]{:S(2)}) collective-permute-start(bf16[32,256]{1,0:T(8,128)(2,1)} %param.5), channel_id=1, source_target_pairs={{0,4},{1,5},{2,6},{3,7},{4,0},{5,1},{6,2},{7,3},{8,12},{9,13},{10,... | collective-permute-start | bytes 49160 | tf_op jit(solution)/shard_map/ppermute | solution.py:278
  6.6 16.7 %collective-permute-start.3 = (bf16[768,256]{1,0:T(8,128)(2,1)S(1)}, bf16[768,256]{1,0:T(8,128)(2,1)S(1)}, u32[]{:S(2)}, u32[]{:S(2)}) collective-permute-start(bf16[768,256]{1,0:T(8,128)(2,1)S(1)} %shard_map.55.tgt_ref), channel_id=1, source_target_pairs={{0,12},{1,13},{2,14},{3,15},{4,8},{5,9},{6,10},{7,11},{8,4},{9,5},... | collective-permute-start | bytes 1179656 | tf_op jit(solution)/shard_map/ppermute | solution.py:278
  19.0 31.3 %all-to-all-start = ((bf16[16,32,1280]{2,1,0:T(8,128)(2,1)}), bf16[16,32,1280]{2,1,0:T(8,128)(2,1)S(1)}, u32[]{:S(2)}, u32[]{:S(2)}) async-start(bf16[16,32,1280]{2,1,0:T(8,128)(2,1)} %bitcast.7), calls=%async_computation | async-start | bytes 2621440 | tf_op jit(solution)/shard_map/all_to_all | solution.py:288
  24.0 6.7 %collective-permute-start.4 = (bf16[32,1536]{1,0:T(8,128)(2,1)S(1)}, bf16[32,1536]{1,0:T(8,128)(2,1)S(1)}, u32[]{:S(2)}, u32[]{:S(2)}) collective-permute-start(bf16[32,1536]{1,0:T(8,128)(2,1)S(1)} %get-tuple-element.36), channel_id=1, source_target_pairs={{0,1},{1,0},{2,3},{3,2},{4,5},{5,4},{6,7},{7,6},{8,9},{9,8},{10,11... | collective-permute-start | bytes 294920 | tf_op jit(solution)/shard_map/ppermute | solution.py:278
  24.4 12.3 %collective-permute-start.5 = (bf16[32,1536]{1,0:T(8,128)(2,1)S(1)}, bf16[32,1536]{1,0:T(8,128)(2,1)S(1)}, u32[]{:S(2)}, u32[]{:S(2)}) collective-permute-start(bf16[32,1536]{1,0:T(8,128)(2,1)S(1)} %get-tuple-element.37), channel_id=1, source_target_pairs={{0,2},{1,3},{2,0},{3,1},{4,6},{5,7},{6,4},{7,5},{8,10},{9,11},{10,... | collective-permute-start | bytes 294920 | tf_op jit(solution)/shard_map/ppermute | solution.py:278
  26.1 25.4 %collective-permute-start.6 = (bf16[32,1536]{1,0:T(8,128)(2,1)S(1)}, bf16[32,1536]{1,0:T(8,128)(2,1)S(1)}, u32[]{:S(2)}, u32[]{:S(2)}) collective-permute-start(bf16[32,1536]{1,0:T(8,128)(2,1)S(1)} %get-tuple-element.38), channel_id=1, source_target_pairs={{0,3},{1,2},{2,1},{3,0},{4,7},{5,6},{6,5},{7,4},{8,11},{9,10},{10,... | collective-permute-start | bytes 294920 | tf_op jit(solution)/shard_map/ppermute | solution.py:278
  26.1 25.4 %collective-permute-start.7 = (bf16[32,1536]{1,0:T(8,128)(2,1)S(1)}, bf16[32,1536]{1,0:T(8,128)(2,1)S(1)}, u32[]{:S(2)}, u32[]{:S(2)}) collective-permute-start(bf16[32,1536]{1,0:T(8,128)(2,1)S(1)} %get-tuple-element.39), channel_id=1, source_target_pairs={{0,7},{1,6},{2,5},{3,4},{4,3},{5,2},{6,1},{7,0},{8,15},{9,14},{10,... | collective-permute-start | bytes 294920 | tf_op jit(solution)/shard_map/ppermute | solution.py:278
  30.6 21.5 %collective-permute-start.8 = (bf16[32,1536]{1,0:T(8,128)(2,1)S(1)}, bf16[32,1536]{1,0:T(8,128)(2,1)S(1)}, u32[]{:S(2)}, u32[]{:S(2)}) collective-permute-start(bf16[32,1536]{1,0:T(8,128)(2,1)S(1)} %get-tuple-element.40), channel_id=1, source_target_pairs={{0,6},{1,7},{2,4},{3,5},{4,2},{5,3},{6,0},{7,1},{8,14},{9,15},{10,... | collective-permute-start | bytes 294920 | tf_op jit(solution)/shard_map/ppermute | solution.py:278
  30.7 22.0 %collective-permute-start.9 = (bf16[32,1536]{1,0:T(8,128)(2,1)S(1)}, bf16[32,1536]{1,0:T(8,128)(2,1)S(1)}, u32[]{:S(2)}, u32[]{:S(2)}) collective-permute-start(bf16[32,1536]{1,0:T(8,128)(2,1)S(1)} %get-tuple-element.41), channel_id=1, source_target_pairs={{0,5},{1,4},{2,7},{3,6},{4,1},{5,0},{6,3},{7,2},{8,13},{9,12},{10,... | collective-permute-start | bytes 294920 | tf_op jit(solution)/shard_map/ppermute | solution.py:278
  36.6 18.6 %collective-permute-start.10 = (bf16[32,1536]{1,0:T(8,128)(2,1)S(1)}, bf16[32,1536]{1,0:T(8,128)(2,1)S(1)}, u32[]{:S(2)}, u32[]{:S(2)}) collective-permute-start(bf16[32,1536]{1,0:T(8,128)(2,1)S(1)} %get-tuple-element.42), channel_id=1, source_target_pairs={{0,4},{1,5},{2,6},{3,7},{4,0},{5,1},{6,2},{7,3},{8,12},{9,13},{10,... | collective-permute-start | bytes 294920 | tf_op jit(solution)/shard_map/ppermute | solution.py:278

commit v6 on v5

--- a/solution.py
+++ b/solution.py
@@ -201,67 +201,69 @@
     )(source, target, *wide, *held)
 
 
-def place_direct_kernel(direct_ref, out_ref, sems):
+def run_all(copies):
+    for copy in copies:
+        copy.start()
+    for copy in copies:
+        copy.wait()
+
+
+def place_direct_kernel(direct_ref, held_ref, out_ref, sems):
     n, _, tail = direct_ref.shape
     stride = out_ref.shape[1] // n
-    copies = [
+    run_all([
         pltpu.make_async_copy(
             direct_ref.at[i], out_ref.at[:, (i + 1) * stride - tail:(i + 1) * stride], sems.at[i]
         )
         for i in range(n)
-    ]
-    for copy in copies:
-        copy.start()
-    for copy in copies:
-        copy.wait()
-
-
-def place_direct(direct, width):
+    ])
+
+
+def place_direct(direct, held):
     n, s_dev, tail = direct.shape
     return pl.pallas_call(
         place_direct_kernel,
-        in_specs=[ANY],
+        in_specs=[ANY] * 2,
         out_specs=ANY,
-        out_shape=jax.ShapeDtypeStruct((s_dev, width), direct.dtype),
+        out_shape=jax.ShapeDtypeStruct(held.shape, held.dtype),
         scratch_shapes=[pltpu.SemaphoreType.DMA((n,))],
+        input_output_aliases={1: 0},
         compiler_params=SMALL,
         cost_estimate=pl.CostEstimate(flops=0, bytes_accessed=4 * n * s_dev * tail, transcendentals=0),
-    )(direct)
-
-
-def place_near_kernel(*refs):
-    parts, out_ref, sems = refs[:-3], refs[-2], refs[-1]
-    group = len(parts)
+    )(direct, held)
+
+
+def place_near_kernel(*refs, bits, group):
+    parts, out_ref, sems = refs[:len(bits)], refs[-2], refs[-1]
     first = parts[0].shape[1] // 2
     stride = out_ref.shape[1] // (2 * group)
     me = lax.axis_index("src")
     copies = []
-    for k, part in enumerate(parts):
-        near = me ^ partners(group)[k]
+    for i, k in enumerate(bits):
+        near = me ^ k
         for side, frm in ((0, near), (1, near ^ (2 * group - INNER))):
             at = pl.multiple_of(frm * stride, 128)
             copies.append(pltpu.make_async_copy(
-                part.at[:, side * first:(side + 1) * first],
+                parts[i].at[:, side * first:(side + 1) * first],
                 out_ref.at[:, pl.ds(at, first)],
-                sems.at[2 * k + side],
+                sems.at[2 * i + side],
             ))
-    for copy in copies:
-        copy.start()
-    for copy in copies:
-        copy.wait()
-
-
-def place_near(parts, held):
-    return pl.pallas_call(
-        place_near_kernel,
-        in_specs=[ANY] * (1 + len(parts)),
+    run_all(copies)
+
+
+def place_near(parts, bits, group, shape, held=()):
+    return pl.pallas_call(
+        functools.partial(place_near_kernel, bits=bits, group=group),
+        in_specs=[ANY] * (len(parts) + len(held)),
         out_specs=ANY,
-        out_shape=jax.ShapeDtypeStruct(held.shape, held.dtype),
+        out_shape=jax.ShapeDtypeStruct(shape, parts[0].dtype),
         scratch_shapes=[pltpu.SemaphoreType.DMA((2 * len(parts),))],
-        input_output_aliases={len(parts): 0},
+        input_output_aliases={len(parts): 0} if held else {},
         compiler_params=SMALL,
-        cost_estimate=pl.CostEstimate(flops=0, bytes_accessed=2 * held.size, transcendentals=0),
-    )(*parts, held)
+        cost_estimate=pl.CostEstimate(
+            flops=0, bytes_accessed=4 * sum(part.size for part in parts), transcendentals=0
+        ),
+    )(*parts, *held)
 
 
 def per_device(source_feat, target_feat, conv_weight, conv_bias, proj_weight):
@@ -289,8 +291,13 @@
 
     near = near_tokens(source, crossed, [], group, wide, scale)
     near = near_tokens(source, got, near, group, wide, scale)
-    parts = [exchange(x, k) if k else x for x, k in zip(near, partners(group))]
-    return place_near(parts, place_direct(direct, patched.shape[0] // cells * conv_weight.shape[1] * n))
+    parts = {k: exchange(x, k) if k else x for x, k in zip(near, partners(group))}
+    soon = [1, 2, 0]
+    late = [k for k in partners(group) if k not in soon]
+    shape = (s_dev, n * patches * conv_weight.shape[1])
+    out = place_near([parts[k] for k in soon], soon, group, shape)
+    out = place_direct(direct, out)
+    return place_near([parts[k] for k in late], late, group, shape, [out])
 
 
 def solution(mesh):

time: 56.5 us -> 56.4 us (level)
  waiting for transfers between devices: 22 us -> 21.2 us
  Pallas kernels: 7.99 us -> 8.61 us
    all_to_all x1, waiting for transfers between devices: 13.6 us -> 12.9 us  [per_device(): direct = lax.all_to_all(direct, 'src', 0, 0, tiled=True)]
    pallas_call x2 -> x3, Pallas kernels: 2.18 us -> 2.78 us  [the longest x2 1.6 us: place_near(): pl.pallas_call(functools.partial(place_near_kernel, bits=bits, group=grou...]
  transfers between devices with their start and end apart: 12 -> 12, of which waited for: 5 -> 5; matrix products, arithmetic and copies ran while one was open for 0% -> 0% of each run, Pallas kernels for 12% -> 14%
where the time goes in v6:
time: 56.4 us; the launch traced here: 56.1 us
  waiting for transfers between devices  21.2 us (38%)
  starting transfers between devices  20.3 us (36%)
  Pallas kernels  8.61 us (15%)
  blocking collectives  5.79 us (10%)
    ppermute x11, starting transfers between devices, exchange(): return lax.ppermute(x, 'src', [(i, i ^ bits) for i in range(n)])  16.6 us
    all_to_all x1, waiting for transfers between devices, per_device(): direct = lax.all_to_all(direct, 'src', 0, 0, tiled=True)  12.9 us
    ppermute x11, waiting for transfers between devices, exchange(): return lax.ppermute(x, 'src', [(i, i ^ bits) for i in range(n)])  8.32 us
    all_gather x1, blocking collectives, per_device(): source = lax.all_gather(column, 'src', axis=0, axis_index_groups=rows)  5.79 us
    all_to_all x1, starting transfers between devices, per_device(): direct = lax.all_to_all(direct, 'src', 0, 0, tiled=True)  3.7 us
    pallas_call x1, Pallas kernels, direct_tokens(): pl.pallas_call(functools.partial(direct_kernel, scale=scale), grid=(px //...  2.37 us
    pallas_call x2, Pallas kernels, place_near(): pl.pallas_call(functools.partial(place_near_kernel, bits=bits, group=grou...  1.6 us
    pallas_call x2, Pallas kernels, near_tokens(): pl.pallas_call(functools.partial(near_kernel, scale=scale, group=group),...  1.29 us
  transfers between devices with their start and end apart: 12, of which 5 were waited for; matrix products, arithmetic and copies ran while one was open for 0% of the time, Pallas kernels for 14%

profile of v6, /device:TPU:0, one launch (start us, length us, event | category | flops | bytes accessed | tf_op | source)
XLA Modules:
  0.0 56.1 jit_solution(10150420067982404418)
XLA Ops:
  0.0 0.0 copy-start
  0.0 4.0 %collective-permute-start = (bf16[32,256]{1,0:T(8,128)(2,1)}, bf16[32,256]{1,0:T(8,128)(2,1)S(1)}, u32[]{:S(2)}, u32[]{:S(2)}) collective-permute-start(bf16[32,256]{1,0:T(8,128)(2,1)} %param.5), channel_id=1, source_target_pairs={{0,8},{1,9},{2,10},{3,11},{4,12},{5,13},{6,14},{7,15},{8,0},{9,1},... | collective-permute-start | bytes 49160 | tf_op jit(solution)/shard_map/ppermute | solution.py:280
  4.0 1.3 %collective-permute-start.2 = (bf16[32,256]{1,0:T(8,128)(2,1)}, bf16[32,256]{1,0:T(8,128)(2,1)S(1)}, u32[]{:S(2)}, u32[]{:S(2)}) collective-permute-start(bf16[32,256]{1,0:T(8,128)(2,1)} %param.5), channel_id=1, source_target_pairs={{0,12},{1,13},{2,14},{3,15},{4,8},{5,9},{6,10},{7,11},{8,4},{9,5},... | collective-permute-start | bytes 49160 | tf_op jit(solution)/shard_map/ppermute | solution.py:280
  5.4 0.2 collective-permute-start.1
  5.6 1.0 %shard_map.55.tgt_ref = bf16[768,256]{1,0:T(8,128)(2,1)S(1)} custom-call(bf16[2048,256]{1,0:T(8,128)(2,1)} %bitcast.11), custom_call_target="tpu_custom_call" | custom-call | tf_op jit(solution)/shard_map/pallas_call | solution.py:63
  6.6 3.0 %collective-permute-start.3 = (bf16[768,256]{1,0:T(8,128)(2,1)S(1)}, bf16[768,256]{1,0:T(8,128)(2,1)S(1)}, u32[]{:S(2)}, u32[]{:S(2)}) collective-permute-start(bf16[768,256]{1,0:T(8,128)(2,1)S(1)} %shard_map.55.tgt_ref), channel_id=1, source_target_pairs={{0,12},{1,13},{2,14},{3,15},{4,8},{5,9},{6,10},{7,11},{8,4},{9,5},... | collective-permute-start | bytes 1179656 | tf_op jit(solution)/shard_map/ppermute | solution.py:280
  9.6 1.2 %shard_map.56 = (bf16[1280,256]{1,0:T(8,128)(2,1)S(1)}, bf16[256,256]{1,0:T(8,128)(2,1)S(1)}, f32[1,256]{1,0:T(1,128)S(1)}, bf16[256,256]{1,0:T(8,128)(2,1)S(1)}) custom-call(bf16[2048,256]{1,0:T(8,128)(2,1)} %bitcast.12, bf16[64,64]{1,0:T(8,128)(2,1)} %w_in.1, f32[1,64]{1,0:T(1,128)} %bitcast.17, bf16[64,64]{1,0:T(8,128)(2,1)} %p_in.1), custom_call_target="tpu_custom_call" | custom-call | tf_op jit(solution)/shard_map/pallas_call | solution.py:101
  10.8 0.0 collective-permute-done
  10.8 0.0 collective-permute-done.2
  10.8 0.0 collective-permute-done.1
  10.8 0.0 copy-done
  10.9 5.8 %all-gather = bf16[16,32,256]{2,1,0:T(8,128)(2,1)S(1)} all-gather(bf16[4,32,256]{2,1,0:T(8,128)(2,1)S(1)} %pad_maximum_fusion), channel_id=2, replica_groups={{0,1,2,3},{4,5,6,7},{8,9,10,11},{12,13,14,15},{16,17,18,19},{20,21,22,2..., dimensions={0}, use_global_device_ids=true | all-gather | bytes 327680 | tf_op jit(solution)/shard_map/all_gather | solution.py:287
  16.6 2.4 %shard_map.59 = bf16[512,1280]{1,0:T(8,128)(2,1)} custom-call(bf16[4,4,32,256]{3,2,1,0:T(8,128)(2,1)S(1)} %bitcast.8, bf16[1280,256]{1,0:T(8,128)(2,1)S(1)} %get-tuple-element.41.tgt_ref, bf16[256,256]{1,0:T(8,128)(2,1)S(1)} %get-tuple-element.25.w_ref, f32[1,256]{1,0:T(1,128)S(1)} %get-tuple-element.26.b_ref, bf16[256,256]{1,0:T(8,128)(2,1)S(1)} %get-tuple-element.27.p_ref), custom_call_target="tpu_custom_call" | custom-call | flops 50331648000 | bytes 1966080 | tf_op jit(solution)/shard_map/pallas_call | solution.py:152
  19.0 3.7 %all-to-all-start = ((bf16[16,32,1280]{2,1,0:T(8,128)(2,1)}), bf16[16,32,1280]{2,1,0:T(8,128)(2,1)S(1)}, u32[]{:S(2)}, u32[]{:S(2)}) async-start(bf16[16,32,1280]{2,1,0:T(8,128)(2,1)} %bitcast.7), calls=%async_computation | async-start | bytes 2621440 | tf_op jit(solution)/shard_map/all_to_all | solution.py:290
  22.7 0.6 %shard_map.57 = (bf16[32,1536]{1,0:T(8,128)(2,1)S(1)}, bf16[32,1536]{1,0:T(8,128)(2,1)S(1)}, bf16[32,1536]{1,0:T(8,128)(2,1)S(1)}, bf16[32,1536]{1,0:T(8,128)(2,...) custom-call(bf16[4,4,32,256]{3,2,1,0:T(8,128)(2,1)S(1)} %bitcast.9, ...), custom_call_target="tpu_custom_call" | custom-call | flops 15099494400 | bytes 786432 | tf_op jit(solution)/shard_map/pallas_call | solution.py:186
  23.4 0.0 collective-permute-done.3.tgt_ref
  23.4 0.6 %shard_map.58 = (bf16[32,1536]{1,0:T(8,128)(2,1)S(1)}, bf16[32,1536]{1,0:T(8,128)(2,1)S(1)}, bf16[32,1536]{1,0:T(8,128)(2,1)S(1)}, bf16[32,1536]{1,0:T(8,128)(2,...) custom-call(bf16[4,4,32,256]{3,2,1,0:T(8,128)(2,1)S(1)} %bitcast.10,, ...), custom_call_target="tpu_custom_call", output_to_operand_aliasing={{0}: (5, {}), {1}: (6, {}), {2}: (7, {}), {3}: (8, {}), {4}... | custom-call | flops 15099494400 | bytes 786432 | tf_op jit(solution)/shard_map/pallas_call | solution.py:186
  24.0 0.3 collective-permute-start.9
  24.4 1.7 %collective-permute-start.10 = (bf16[32,1536]{1,0:T(8,128)(2,1)S(1)}, bf16[32,1536]{1,0:T(8,128)(2,1)S(1)}, u32[]{:S(2)}, u32[]{:S(2)}) collective-permute-start(bf16[32,1536]{1,0:T(8,128)(2,1)S(1)} %get-tuple-element.43), channel_id=1, source_target_pairs={{0,2},{1,3},{2,0},{3,1},{4,6},{5,7},{6,4},{7,5},{8,10},{9,11},{10,... | collective-permute-start | bytes 294920 | tf_op jit(solution)/shard_map/ppermute | solution.py:280
  26.1 0.0 collective-permute-start.4
  26.1 4.5 %collective-permute-start.5 = (bf16[32,1536]{1,0:T(8,128)(2,1)S(1)}, bf16[32,1536]{1,0:T(8,128)(2,1)S(1)}, u32[]{:S(2)}, u32[]{:S(2)}) collective-permute-start(bf16[32,1536]{1,0:T(8,128)(2,1)S(1)} %get-tuple-element.37), channel_id=1, source_target_pairs={{0,7},{1,6},{2,5},{3,4},{4,3},{5,2},{6,1},{7,0},{8,15},{9,14},{10,... | collective-permute-start | bytes 294920 | tf_op jit(solution)/shard_map/ppermute | solution.py:280
  30.6 0.1 collective-permute-start.6
  30.7 0.0 collective-permute-done.9.refs_0_
  30.7 1.4 %collective-permute-start.7 = (bf16[32,1536]{1,0:T(8,128)(2,1)S(1)}, bf16[32,1536]{1,0:T(8,128)(2,1)S(1)}, u32[]{:S(2)}, u32[]{:S(2)}) collective-permute-start(bf16[32,1536]{1,0:T(8,128)(2,1)S(1)} %get-tuple-element.39), channel_id=1, source_target_pairs={{0,5},{1,4},{2,7},{3,6},{4,1},{5,0},{6,3},{7,2},{8,13},{9,12},{10,... | collective-permute-start | bytes 294920 | tf_op jit(solution)/shard_map/ppermute | solution.py:280
  32.1 4.6 %collective-permute-done.10.refs_1_ = bf16[32,1536]{1,0:T(8,128)(2,1)S(1)} collective-permute-done((bf16[32,1536]{1,0:T(8,128)(2,1)S(1)}, bf16[32,1536]{1,0:T(8,128)(2,1)S(1)}, u32[]{:S(2)}, u32[]{:S(2)}) %collective-permute-start.10) | collective-permute-done | bytes 98336 | tf_op jit(solution)/shard_map/ppermute | solution.py:280
  36.6 0.0 collective-permute-start.8
  36.6 0.8 %shard_map.60.held_ref = bf16[32,32768]{1,0:T(8,128)(2,1)} custom-call(bf16[32,1536]{1,0:T(8,128)(2,1)S(1)} %collective-permute-done.9.refs_0_, bf16[32,1536]{1,0:T(8,128)(2,1)S(1)} %collective-permute-done.10.refs_1_, bf16[32,1536]{1,0:T(8,128)(2,1)S(1)} %get-tuple-element.44.refs_2_), custom_call_target="tpu_custom_call" | custom-call | bytes 589824 | tf_op jit(solution)/shard_map/pallas_call | solution.py:255
  37.4 12.9 %all-to-all-done.direct_ref = bf16[16,32,1280]{2,1,0:T(8,128)(2,1)S(1)} async-done(((bf16[16,32,1280]{2,1,0:T(8,128)(2,1)}), bf16[16,32,1280]{2,1,0:T(8,128)(2,1)S(1)}, u32[]{:S(2)}, u32[]{:S(2)}) %all-to-all-start) | async-done | bytes 1310752 | tf_op jit(solution)/shard_map/all_to_all | solution.py:290
  50.3 1.2 %shard_map.61.refs_5_ = bf16[32,32768]{1,0:T(8,128)(2,1)} custom-call(bf16[16,32,1280]{2,1,0:T(8,128)(2,1)S(1)} %all-to-all-done.direct_ref, bf16[32,32768]{1,0:T(8,128)(2,1)} %shard_map.60.held_ref), custom_call_target="tpu_custom_call", output_to_operand_aliasing={{}: (1, {})} | custom-call | bytes 2621440 | tf_op jit(solution)/shard_map/pallas_call | solution.py:224
  51.5 0.0 collective-permute-done.4.refs_0_
  51.5 0.0 collective-permute-done.5.refs_1_
  51.5 0.6 %collective-permute-done.6.refs_2_ = bf16[32,1536]{1,0:T(8,128)(2,1)S(1)} collective-permute-done((bf16[32,1536]{1,0:T(8,128)(2,1)S(1)}, bf16[32,1536]{1,0:T(8,128)(2,1)S(1)}, u32[]{:S(2)}, u32[]{:S(2)}) %collective-permute-start.6) | collective-permute-done | bytes 98336 | tf_op jit(solution)/shard_map/ppermute | solution.py:280
  52.1 0.6 %collective-permute-done.7.refs_3_ = bf16[32,1536]{1,0:T(8,128)(2,1)S(1)} collective-permute-done((bf16[32,1536]{1,0:T(8,128)(2,1)S(1)}, bf16[32,1536]{1,0:T(8,128)(2,1)S(1)}, u32[]{:S(2)}, u32[]{:S(2)}) %collective-permute-start.7) | collective-permute-done | bytes 98336 | tf_op jit(solution)/shard_map/ppermute | solution.py:280
  52.7 2.6 %collective-permute-done.8.refs_4_ = bf16[32,1536]{1,0:T(8,128)(2,1)S(1)} collective-permute-done((bf16[32,1536]{1,0:T(8,128)(2,1)S(1)}, bf16[32,1536]{1,0:T(8,128)(2,1)S(1)}, u32[]{:S(2)}, u32[]{:S(2)}) %collective-permute-start.8) | collective-permute-done | bytes 98336 | tf_op jit(solution)/shard_map/ppermute | solution.py:280
  55.2 0.8 %shard_map.62 = bf16[32,32768]{1,0:T(8,128)(2,1)} custom-call(bf16[32,1536]{1,0:T(8,128)(2,1)S(1)} %collective-permute-done.4.refs_0_, bf16[32,1536]{1,0:T(8,128)(2,1)S(1)} %collective-permute-done.5.refs_1_, bf16[32,1536]{1,0:T(8,128)(2,1)S(1)} %collective-permute-done.6.refs_2_, ...), custom_call_target="tpu_custom_call", output_to_operand_aliasing={{}: (5, {})} | custom-call | bytes 983040 | tf_op jit(solution)/shard_map/pallas_call | solution.py:255
  (1 shorter events, 0.0 us)
Async XLA Ops:
  0.0 10.8 %copy-start = (bf16[32,256]{1,0:T(8,128)(2,1)S(1)}, bf16[32,256]{1,0:T(8,128)(2,1)}, u32[]{:S(2)}) copy-start(bf16[32,256]{1,0:T(8,128)(2,1)} %param.5) | copy-start | bytes 49156
  0.0 10.8 %collective-permute-start = (bf16[32,256]{1,0:T(8,128)(2,1)}, bf16[32,256]{1,0:T(8,128)(2,1)S(1)}, u32[]{:S(2)}, u32[]{:S(2)}) collective-permute-start(bf16[32,256]{1,0:T(8,128)(2,1)} %param.5), channel_id=1, source_target_pairs={{0,8},{1,9},{2,10},{3,11},{4,12},{5,13},{6,14},{7,15},{8,0},{9,1},... | collective-permute-start | bytes 49160 | tf_op jit(solution)/shard_map/ppermute | solution.py:280
  4.0 6.8 %collective-permute-start.2 = (bf16[32,256]{1,0:T(8,128)(2,1)}, bf16[32,256]{1,0:T(8,128)(2,1)S(1)}, u32[]{:S(2)}, u32[]{:S(2)}) collective-permute-start(bf16[32,256]{1,0:T(8,128)(2,1)} %param.5), channel_id=1, source_target_pairs={{0,12},{1,13},{2,14},{3,15},{4,8},{5,9},{6,10},{7,11},{8,4},{9,5},... | collective-permute-start | bytes 49160 | tf_op jit(solution)/shard_map/ppermute | solution.py:280
  5.4 5.4 %collective-permute-start.1 = (bf16[32,256]{1,0:T(8,128)(2,1)}, bf16[32,256]{1,0:T(8,128)(2,1)S(1)}, u32[]{:S(2)}, u32[]{:S(2)}) collective-permute-start(bf16[32,256]{1,0:T(8,128)(2,1)} %param.5), channel_id=1, source_target_pairs={{0,4},{1,5},{2,6},{3,7},{4,0},{5,1},{6,2},{7,3},{8,12},{9,13},{10,... | collective-permute-start | bytes 49160 | tf_op jit(solution)/shard_map/ppermute | solution.py:280
  6.6 16.7 %collective-permute-start.3 = (bf16[768,256]{1,0:T(8,128)(2,1)S(1)}, bf16[768,256]{1,0:T(8,128)(2,1)S(1)}, u32[]{:S(2)}, u32[]{:S(2)}) collective-permute-start(bf16[768,256]{1,0:T(8,128)(2,1)S(1)} %shard_map.55.tgt_ref), channel_id=1, source_target_pairs={{0,12},{1,13},{2,14},{3,15},{4,8},{5,9},{6,10},{7,11},{8,4},{9,5},... | collective-permute-start | bytes 1179656 | tf_op jit(solution)/shard_map/ppermute | solution.py:280
  19.0 31.3 %all-to-all-start = ((bf16[16,32,1280]{2,1,0:T(8,128)(2,1)}), bf16[16,32,1280]{2,1,0:T(8,128)(2,1)S(1)}, u32[]{:S(2)}, u32[]{:S(2)}) async-start(bf16[16,32,1280]{2,1,0:T(8,128)(2,1)} %bitcast.7), calls=%async_computation | async-start | bytes 2621440 | tf_op jit(solution)/shard_map/all_to_all | solution.py:290
  24.0 6.7 %collective-permute-start.9 = (bf16[32,1536]{1,0:T(8,128)(2,1)S(1)}, bf16[32,1536]{1,0:T(8,128)(2,1)S(1)}, u32[]{:S(2)}, u32[]{:S(2)}) collective-permute-start(bf16[32,1536]{1,0:T(8,128)(2,1)S(1)} %get-tuple-element.42), channel_id=1, source_target_pairs={{0,1},{1,0},{2,3},{3,2},{4,5},{5,4},{6,7},{7,6},{8,9},{9,8},{10,11... | collective-permute-start | bytes 294920 | tf_op jit(solution)/shard_map/ppermute | solution.py:280
  24.4 12.3 %collective-permute-start.10 = (bf16[32,1536]{1,0:T(8,128)(2,1)S(1)}, bf16[32,1536]{1,0:T(8,128)(2,1)S(1)}, u32[]{:S(2)}, u32[]{:S(2)}) collective-permute-start(bf16[32,1536]{1,0:T(8,128)(2,1)S(1)} %get-tuple-element.43), channel_id=1, source_target_pairs={{0,2},{1,3},{2,0},{3,1},{4,6},{5,7},{6,4},{7,5},{8,10},{9,11},{10,... | collective-permute-start | bytes 294920 | tf_op jit(solution)/shard_map/ppermute | solution.py:280
  26.1 25.4 %collective-permute-start.4 = (bf16[32,1536]{1,0:T(8,128)(2,1)S(1)}, bf16[32,1536]{1,0:T(8,128)(2,1)S(1)}, u32[]{:S(2)}, u32[]{:S(2)}) collective-permute-start(bf16[32,1536]{1,0:T(8,128)(2,1)S(1)} %get-tuple-element.36), channel_id=1, source_target_pairs={{0,3},{1,2},{2,1},{3,0},{4,7},{5,6},{6,5},{7,4},{8,11},{9,10},{10,... | collective-permute-start | bytes 294920 | tf_op jit(solution)/shard_map/ppermute | solution.py:280
  26.1 25.4 %collective-permute-start.5 = (bf16[32,1536]{1,0:T(8,128)(2,1)S(1)}, bf16[32,1536]{1,0:T(8,128)(2,1)S(1)}, u32[]{:S(2)}, u32[]{:S(2)}) collective-permute-start(bf16[32,1536]{1,0:T(8,128)(2,1)S(1)} %get-tuple-element.37), channel_id=1, source_target_pairs={{0,7},{1,6},{2,5},{3,4},{4,3},{5,2},{6,1},{7,0},{8,15},{9,14},{10,... | collective-permute-start | bytes 294920 | tf_op jit(solution)/shard_map/ppermute | solution.py:280
  30.6 21.5 %collective-permute-start.6 = (bf16[32,1536]{1,0:T(8,128)(2,1)S(1)}, bf16[32,1536]{1,0:T(8,128)(2,1)S(1)}, u32[]{:S(2)}, u32[]{:S(2)}) collective-permute-start(bf16[32,1536]{1,0:T(8,128)(2,1)S(1)} %get-tuple-element.38), channel_id=1, source_target_pairs={{0,6},{1,7},{2,4},{3,5},{4,2},{5,3},{6,0},{7,1},{8,14},{9,15},{10,... | collective-permute-start | bytes 294920 | tf_op jit(solution)/shard_map/ppermute | solution.py:280
  30.7 22.0 %collective-permute-start.7 = (bf16[32,1536]{1,0:T(8,128)(2,1)S(1)}, bf16[32,1536]{1,0:T(8,128)(2,1)S(1)}, u32[]{:S(2)}, u32[]{:S(2)}) collective-permute-start(bf16[32,1536]{1,0:T(8,128)(2,1)S(1)} %get-tuple-element.39), channel_id=1, source_target_pairs={{0,5},{1,4},{2,7},{3,6},{4,1},{5,0},{6,3},{7,2},{8,13},{9,12},{10,... | collective-permute-start | bytes 294920 | tf_op jit(solution)/shard_map/ppermute | solution.py:280
  36.6 18.6 %collective-permute-start.8 = (bf16[32,1536]{1,0:T(8,128)(2,1)S(1)}, bf16[32,1536]{1,0:T(8,128)(2,1)S(1)}, u32[]{:S(2)}, u32[]{:S(2)}) collective-permute-start(bf16[32,1536]{1,0:T(8,128)(2,1)S(1)} %get-tuple-element.40), channel_id=1, source_target_pairs={{0,4},{1,5},{2,6},{3,7},{4,0},{5,1},{6,2},{7,3},{8,12},{9,13},{10,... | collective-permute-start | bytes 294920 | tf_op jit(solution)/shard_map/ppermute | solution.py:280

commit v7 on v6

--- a/solution.py
+++ b/solution.py
@@ -23,7 +23,7 @@
 
 
 def partners(group):
-    return [*range(1, INNER), *range(group - 1, INNER - 1, -1), 0]
+    return [1, 2, *range(group - 1, INNER - 1, -1), 3, 0]
 
 
 def gelu(x):

time: 56.4 us -> 56.4 us (level)
    ppermute x11, waiting for transfers between devices: 8.32 us -> 7.56 us  [exchange(): return lax.ppermute(x, 'src', [(i, i ^ bits) for i in range(n)])]
    all_to_all x1, waiting for transfers between devices: 12.9 us -> 13.6 us  [per_device(): direct = lax.all_to_all(direct, 'src', 0, 0, tiled=True)]
where the time goes in v7:
time: 56.4 us; the launch traced here: 56.1 us
  waiting for transfers between devices  21.2 us (38%)
  starting transfers between devices  20.4 us (36%)
  Pallas kernels  8.61 us (15%)
  blocking collectives  5.79 us (10%)
    ppermute x11, starting transfers between devices, exchange(): return lax.ppermute(x, 'src', [(i, i ^ bits) for i in range(n)])  16.7 us
    all_to_all x1, waiting for transfers between devices, per_device(): direct = lax.all_to_all(direct, 'src', 0, 0, tiled=True)  13.6 us
    ppermute x11, waiting for transfers between devices, exchange(): return lax.ppermute(x, 'src', [(i, i ^ bits) for i in range(n)])  7.56 us
    all_gather x1, blocking collectives, per_device(): source = lax.all_gather(column, 'src', axis=0, axis_index_groups=rows)  5.79 us
    all_to_all x1, starting transfers between devices, per_device(): direct = lax.all_to_all(direct, 'src', 0, 0, tiled=True)  3.7 us
    pallas_call x1, Pallas kernels, direct_tokens(): pl.pallas_call(functools.partial(direct_kernel, scale=scale), grid=(px //...  2.37 us
    pallas_call x2, Pallas kernels, place_near(): pl.pallas_call(functools.partial(place_near_kernel, bits=bits, group=grou...  1.6 us
    pallas_call x2, Pallas kernels, near_tokens(): pl.pallas_call(functools.partial(near_kernel, scale=scale, group=group),...  1.29 us
  transfers between devices with their start and end apart: 12, of which 5 were waited for; matrix products, arithmetic and copies ran while one was open for 0% of the time, Pallas kernels for 14%

profile of v7, /device:TPU:0, one launch (start us, length us, event | category | flops | bytes accessed | tf_op | source)
XLA Modules:
  0.0 56.1 jit_solution(12235548907187680243)
XLA Ops:
  0.0 0.0 copy-start
  0.0 4.0 %collective-permute-start = (bf16[32,256]{1,0:T(8,128)(2,1)}, bf16[32,256]{1,0:T(8,128)(2,1)S(1)}, u32[]{:S(2)}, u32[]{:S(2)}) collective-permute-start(bf16[32,256]{1,0:T(8,128)(2,1)} %param.5), channel_id=1, source_target_pairs={{0,8},{1,9},{2,10},{3,11},{4,12},{5,13},{6,14},{7,15},{8,0},{9,1},... | collective-permute-start | bytes 49160 | tf_op jit(solution)/shard_map/ppermute | solution.py:280
  4.0 1.3 %collective-permute-start.2 = (bf16[32,256]{1,0:T(8,128)(2,1)}, bf16[32,256]{1,0:T(8,128)(2,1)S(1)}, u32[]{:S(2)}, u32[]{:S(2)}) collective-permute-start(bf16[32,256]{1,0:T(8,128)(2,1)} %param.5), channel_id=1, source_target_pairs={{0,12},{1,13},{2,14},{3,15},{4,8},{5,9},{6,10},{7,11},{8,4},{9,5},... | collective-permute-start | bytes 49160 | tf_op jit(solution)/shard_map/ppermute | solution.py:280
  5.4 0.2 collective-permute-start.1
  5.6 1.0 %shard_map.55.tgt_ref = bf16[768,256]{1,0:T(8,128)(2,1)S(1)} custom-call(bf16[2048,256]{1,0:T(8,128)(2,1)} %bitcast.11), custom_call_target="tpu_custom_call" | custom-call | tf_op jit(solution)/shard_map/pallas_call | solution.py:63
  6.6 3.0 %collective-permute-start.3 = (bf16[768,256]{1,0:T(8,128)(2,1)S(1)}, bf16[768,256]{1,0:T(8,128)(2,1)S(1)}, u32[]{:S(2)}, u32[]{:S(2)}) collective-permute-start(bf16[768,256]{1,0:T(8,128)(2,1)S(1)} %shard_map.55.tgt_ref), channel_id=1, source_target_pairs={{0,12},{1,13},{2,14},{3,15},{4,8},{5,9},{6,10},{7,11},{8,4},{9,5},... | collective-permute-start | bytes 1179656 | tf_op jit(solution)/shard_map/ppermute | solution.py:280
  9.6 1.2 %shard_map.56 = (bf16[1280,256]{1,0:T(8,128)(2,1)S(1)}, bf16[256,256]{1,0:T(8,128)(2,1)S(1)}, f32[1,256]{1,0:T(1,128)S(1)}, bf16[256,256]{1,0:T(8,128)(2,1)S(1)}) custom-call(bf16[2048,256]{1,0:T(8,128)(2,1)} %bitcast.12, bf16[64,64]{1,0:T(8,128)(2,1)} %w_in.1, f32[1,64]{1,0:T(1,128)} %bitcast.17, bf16[64,64]{1,0:T(8,128)(2,1)} %p_in.1), custom_call_target="tpu_custom_call" | custom-call | tf_op jit(solution)/shard_map/pallas_call | solution.py:101
  10.8 0.0 collective-permute-done
  10.8 0.0 collective-permute-done.2
  10.8 0.0 collective-permute-done.1
  10.8 0.0 copy-done
  10.9 5.8 %all-gather = bf16[16,32,256]{2,1,0:T(8,128)(2,1)S(1)} all-gather(bf16[4,32,256]{2,1,0:T(8,128)(2,1)S(1)} %pad_maximum_fusion), channel_id=2, replica_groups={{0,1,2,3},{4,5,6,7},{8,9,10,11},{12,13,14,15},{16,17,18,19},{20,21,22,2..., dimensions={0}, use_global_device_ids=true | all-gather | bytes 327680 | tf_op jit(solution)/shard_map/all_gather | solution.py:287
  16.6 2.4 %shard_map.59 = bf16[512,1280]{1,0:T(8,128)(2,1)} custom-call(bf16[4,4,32,256]{3,2,1,0:T(8,128)(2,1)S(1)} %bitcast.8, bf16[1280,256]{1,0:T(8,128)(2,1)S(1)} %get-tuple-element.41.tgt_ref, bf16[256,256]{1,0:T(8,128)(2,1)S(1)} %get-tuple-element.25.w_ref, f32[1,256]{1,0:T(1,128)S(1)} %get-tuple-element.26.b_ref, bf16[256,256]{1,0:T(8,128)(2,1)S(1)} %get-tuple-element.27.p_ref), custom_call_target="tpu_custom_call" | custom-call | flops 50331648000 | bytes 1966080 | tf_op jit(solution)/shard_map/pallas_call | solution.py:152
  19.0 3.7 %all-to-all-start = ((bf16[16,32,1280]{2,1,0:T(8,128)(2,1)}), bf16[16,32,1280]{2,1,0:T(8,128)(2,1)S(1)}, u32[]{:S(2)}, u32[]{:S(2)}) async-start(bf16[16,32,1280]{2,1,0:T(8,128)(2,1)} %bitcast.7), calls=%async_computation | async-start | bytes 2621440 | tf_op jit(solution)/shard_map/all_to_all | solution.py:290
  22.7 0.6 %shard_map.57 = (bf16[32,1536]{1,0:T(8,128)(2,1)S(1)}, bf16[32,1536]{1,0:T(8,128)(2,1)S(1)}, bf16[32,1536]{1,0:T(8,128)(2,1)S(1)}, bf16[32,1536]{1,0:T(8,128)(2,...) custom-call(bf16[4,4,32,256]{3,2,1,0:T(8,128)(2,1)S(1)} %bitcast.9, ...), custom_call_target="tpu_custom_call" | custom-call | flops 15099494400 | bytes 786432 | tf_op jit(solution)/shard_map/pallas_call | solution.py:186
  23.4 0.0 collective-permute-done.3.tgt_ref
  23.4 0.6 %shard_map.58 = (bf16[32,1536]{1,0:T(8,128)(2,1)S(1)}, bf16[32,1536]{1,0:T(8,128)(2,1)S(1)}, bf16[32,1536]{1,0:T(8,128)(2,1)S(1)}, bf16[32,1536]{1,0:T(8,128)(2,...) custom-call(bf16[4,4,32,256]{3,2,1,0:T(8,128)(2,1)S(1)} %bitcast.10,, ...), custom_call_target="tpu_custom_call", output_to_operand_aliasing={{0}: (5, {}), {1}: (6, {}), {2}: (7, {}), {3}: (8, {}), {4}... | custom-call | flops 15099494400 | bytes 786432 | tf_op jit(solution)/shard_map/pallas_call | solution.py:186
  24.0 0.3 collective-permute-start.9
  24.4 1.7 %collective-permute-start.10 = (bf16[32,1536]{1,0:T(8,128)(2,1)S(1)}, bf16[32,1536]{1,0:T(8,128)(2,1)S(1)}, u32[]{:S(2)}, u32[]{:S(2)}) collective-permute-start(bf16[32,1536]{1,0:T(8,128)(2,1)S(1)} %get-tuple-element.43), channel_id=1, source_target_pairs={{0,2},{1,3},{2,0},{3,1},{4,6},{5,7},{6,4},{7,5},{8,10},{9,11},{10,... | collective-permute-start | bytes 294920 | tf_op jit(solution)/shard_map/ppermute | solution.py:280
  26.1 3.1 %collective-permute-start.4 = (bf16[32,1536]{1,0:T(8,128)(2,1)S(1)}, bf16[32,1536]{1,0:T(8,128)(2,1)S(1)}, u32[]{:S(2)}, u32[]{:S(2)}) collective-permute-start(bf16[32,1536]{1,0:T(8,128)(2,1)S(1)} %get-tuple-element.36), channel_id=1, source_target_pairs={{0,7},{1,6},{2,5},{3,4},{4,3},{5,2},{6,1},{7,0},{8,15},{9,14},{10,... | collective-permute-start | bytes 294920 | tf_op jit(solution)/shard_map/ppermute | solution.py:280
  29.1 0.3 collective-permute-start.5
  29.4 2.4 %collective-permute-start.6 = (bf16[32,1536]{1,0:T(8,128)(2,1)S(1)}, bf16[32,1536]{1,0:T(8,128)(2,1)S(1)}, u32[]{:S(2)}, u32[]{:S(2)}) collective-permute-start(bf16[32,1536]{1,0:T(8,128)(2,1)S(1)} %get-tuple-element.38), channel_id=1, source_target_pairs={{0,5},{1,4},{2,7},{3,6},{4,1},{5,0},{6,3},{7,2},{8,13},{9,12},{10,... | collective-permute-start | bytes 294920 | tf_op jit(solution)/shard_map/ppermute | solution.py:280
  31.8 0.0 collective-permute-done.9.refs_0_
  31.8 0.4 collective-permute-start.7
  32.2 3.8 %collective-permute-done.10.refs_1_ = bf16[32,1536]{1,0:T(8,128)(2,1)S(1)} collective-permute-done((bf16[32,1536]{1,0:T(8,128)(2,1)S(1)}, bf16[32,1536]{1,0:T(8,128)(2,1)S(1)}, u32[]{:S(2)}, u32[]{:S(2)}) %collective-permute-start.10) | collective-permute-done | bytes 98336 | tf_op jit(solution)/shard_map/ppermute | solution.py:280
  35.9 0.0 collective-permute-start.8
  35.9 0.8 %shard_map.60.held_ref = bf16[32,32768]{1,0:T(8,128)(2,1)} custom-call(bf16[32,1536]{1,0:T(8,128)(2,1)S(1)} %collective-permute-done.9.refs_0_, bf16[32,1536]{1,0:T(8,128)(2,1)S(1)} %collective-permute-done.10.refs_1_, bf16[32,1536]{1,0:T(8,128)(2,1)S(1)} %get-tuple-element.44.refs_2_), custom_call_target="tpu_custom_call" | custom-call | bytes 589824 | tf_op jit(solution)/shard_map/pallas_call | solution.py:255
  36.7 13.6 %all-to-all-done.direct_ref = bf16[16,32,1280]{2,1,0:T(8,128)(2,1)S(1)} async-done(((bf16[16,32,1280]{2,1,0:T(8,128)(2,1)}), bf16[16,32,1280]{2,1,0:T(8,128)(2,1)S(1)}, u32[]{:S(2)}, u32[]{:S(2)}) %all-to-all-start) | async-done | bytes 1310752 | tf_op jit(solution)/shard_map/all_to_all | solution.py:290
  50.3 1.2 %shard_map.61.refs_5_ = bf16[32,32768]{1,0:T(8,128)(2,1)} custom-call(bf16[16,32,1280]{2,1,0:T(8,128)(2,1)S(1)} %all-to-all-done.direct_ref, bf16[32,32768]{1,0:T(8,128)(2,1)} %shard_map.60.held_ref), custom_call_target="tpu_custom_call", output_to_operand_aliasing={{}: (1, {})} | custom-call | bytes 2621440 | tf_op jit(solution)/shard_map/pallas_call | solution.py:224
  51.5 0.0 collective-permute-done.4.refs_0_
  51.5 0.6 %collective-permute-done.5.refs_1_ = bf16[32,1536]{1,0:T(8,128)(2,1)S(1)} collective-permute-done((bf16[32,1536]{1,0:T(8,128)(2,1)S(1)}, bf16[32,1536]{1,0:T(8,128)(2,1)S(1)}, u32[]{:S(2)}, u32[]{:S(2)}) %collective-permute-start.5) | collective-permute-done | bytes 98336 | tf_op jit(solution)/shard_map/ppermute | solution.py:280
  52.1 0.6 %collective-permute-done.6.refs_2_ = bf16[32,1536]{1,0:T(8,128)(2,1)S(1)} collective-permute-done((bf16[32,1536]{1,0:T(8,128)(2,1)S(1)}, bf16[32,1536]{1,0:T(8,128)(2,1)S(1)}, u32[]{:S(2)}, u32[]{:S(2)}) %collective-permute-start.6) | collective-permute-done | bytes 98336 | tf_op jit(solution)/shard_map/ppermute | solution.py:280
  52.7 2.6 %collective-permute-done.7.refs_3_ = bf16[32,1536]{1,0:T(8,128)(2,1)S(1)} collective-permute-done((bf16[32,1536]{1,0:T(8,128)(2,1)S(1)}, bf16[32,1536]{1,0:T(8,128)(2,1)S(1)}, u32[]{:S(2)}, u32[]{:S(2)}) %collective-permute-start.7) | collective-permute-done | bytes 98336 | tf_op jit(solution)/shard_map/ppermute | solution.py:280
  55.2 0.0 collective-permute-done.8.refs_4_
  55.2 0.9 %shard_map.62 = bf16[32,32768]{1,0:T(8,128)(2,1)} custom-call(bf16[32,1536]{1,0:T(8,128)(2,1)S(1)} %collective-permute-done.4.refs_0_, bf16[32,1536]{1,0:T(8,128)(2,1)S(1)} %collective-permute-done.5.refs_1_, bf16[32,1536]{1,0:T(8,128)(2,1)S(1)} %collective-permute-done.6.refs_2_, ...), custom_call_target="tpu_custom_call", output_to_operand_aliasing={{}: (5, {})} | custom-call | bytes 983040 | tf_op jit(solution)/shard_map/pallas_call | solution.py:255
  (1 shorter events, 0.0 us)
Async XLA Ops:
  0.0 10.8 %copy-start = (bf16[32,256]{1,0:T(8,128)(2,1)S(1)}, bf16[32,256]{1,0:T(8,128)(2,1)}, u32[]{:S(2)}) copy-start(bf16[32,256]{1,0:T(8,128)(2,1)} %param.5) | copy-start | bytes 49156
  0.0 10.8 %collective-permute-start = (bf16[32,256]{1,0:T(8,128)(2,1)}, bf16[32,256]{1,0:T(8,128)(2,1)S(1)}, u32[]{:S(2)}, u32[]{:S(2)}) collective-permute-start(bf16[32,256]{1,0:T(8,128)(2,1)} %param.5), channel_id=1, source_target_pairs={{0,8},{1,9},{2,10},{3,11},{4,12},{5,13},{6,14},{7,15},{8,0},{9,1},... | collective-permute-start | bytes 49160 | tf_op jit(solution)/shard_map/ppermute | solution.py:280
  4.0 6.8 %collective-permute-start.2 = (bf16[32,256]{1,0:T(8,128)(2,1)}, bf16[32,256]{1,0:T(8,128)(2,1)S(1)}, u32[]{:S(2)}, u32[]{:S(2)}) collective-permute-start(bf16[32,256]{1,0:T(8,128)(2,1)} %param.5), channel_id=1, source_target_pairs={{0,12},{1,13},{2,14},{3,15},{4,8},{5,9},{6,10},{7,11},{8,4},{9,5},... | collective-permute-start | bytes 49160 | tf_op jit(solution)/shard_map/ppermute | solution.py:280
  5.4 5.4 %collective-permute-start.1 = (bf16[32,256]{1,0:T(8,128)(2,1)}, bf16[32,256]{1,0:T(8,128)(2,1)S(1)}, u32[]{:S(2)}, u32[]{:S(2)}) collective-permute-start(bf16[32,256]{1,0:T(8,128)(2,1)} %param.5), channel_id=1, source_target_pairs={{0,4},{1,5},{2,6},{3,7},{4,0},{5,1},{6,2},{7,3},{8,12},{9,13},{10,... | collective-permute-start | bytes 49160 | tf_op jit(solution)/shard_map/ppermute | solution.py:280
  6.6 16.7 %collective-permute-start.3 = (bf16[768,256]{1,0:T(8,128)(2,1)S(1)}, bf16[768,256]{1,0:T(8,128)(2,1)S(1)}, u32[]{:S(2)}, u32[]{:S(2)}) collective-permute-start(bf16[768,256]{1,0:T(8,128)(2,1)S(1)} %shard_map.55.tgt_ref), channel_id=1, source_target_pairs={{0,12},{1,13},{2,14},{3,15},{4,8},{5,9},{6,10},{7,11},{8,4},{9,5},... | collective-permute-start | bytes 1179656 | tf_op jit(solution)/shard_map/ppermute | solution.py:280
  19.0 31.3 %all-to-all-start = ((bf16[16,32,1280]{2,1,0:T(8,128)(2,1)}), bf16[16,32,1280]{2,1,0:T(8,128)(2,1)S(1)}, u32[]{:S(2)}, u32[]{:S(2)}) async-start(bf16[16,32,1280]{2,1,0:T(8,128)(2,1)} %bitcast.7), calls=%async_computation | async-start | bytes 2621440 | tf_op jit(solution)/shard_map/all_to_all | solution.py:290
  24.0 7.8 %collective-permute-start.9 = (bf16[32,1536]{1,0:T(8,128)(2,1)S(1)}, bf16[32,1536]{1,0:T(8,128)(2,1)S(1)}, u32[]{:S(2)}, u32[]{:S(2)}) collective-permute-start(bf16[32,1536]{1,0:T(8,128)(2,1)S(1)} %get-tuple-element.42), channel_id=1, source_target_pairs={{0,1},{1,0},{2,3},{3,2},{4,5},{5,4},{6,7},{7,6},{8,9},{9,8},{10,11... | collective-permute-start | bytes 294920 | tf_op jit(solution)/shard_map/ppermute | solution.py:280
  24.4 11.6 %collective-permute-start.10 = (bf16[32,1536]{1,0:T(8,128)(2,1)S(1)}, bf16[32,1536]{1,0:T(8,128)(2,1)S(1)}, u32[]{:S(2)}, u32[]{:S(2)}) collective-permute-start(bf16[32,1536]{1,0:T(8,128)(2,1)S(1)} %get-tuple-element.43), channel_id=1, source_target_pairs={{0,2},{1,3},{2,0},{3,1},{4,6},{5,7},{6,4},{7,5},{8,10},{9,11},{10,... | collective-permute-start | bytes 294920 | tf_op jit(solution)/shard_map/ppermute | solution.py:280
  26.1 25.4 %collective-permute-start.4 = (bf16[32,1536]{1,0:T(8,128)(2,1)S(1)}, bf16[32,1536]{1,0:T(8,128)(2,1)S(1)}, u32[]{:S(2)}, u32[]{:S(2)}) collective-permute-start(bf16[32,1536]{1,0:T(8,128)(2,1)S(1)} %get-tuple-element.36), channel_id=1, source_target_pairs={{0,7},{1,6},{2,5},{3,4},{4,3},{5,2},{6,1},{7,0},{8,15},{9,14},{10,... | collective-permute-start | bytes 294920 | tf_op jit(solution)/shard_map/ppermute | solution.py:280
  29.1 23.0 %collective-permute-start.5 = (bf16[32,1536]{1,0:T(8,128)(2,1)S(1)}, bf16[32,1536]{1,0:T(8,128)(2,1)S(1)}, u32[]{:S(2)}, u32[]{:S(2)}) collective-permute-start(bf16[32,1536]{1,0:T(8,128)(2,1)S(1)} %get-tuple-element.37), channel_id=1, source_target_pairs={{0,6},{1,7},{2,4},{3,5},{4,2},{5,3},{6,0},{7,1},{8,14},{9,15},{10,... | collective-permute-start | bytes 294920 | tf_op jit(solution)/shard_map/ppermute | solution.py:280
  29.4 23.3 %collective-permute-start.6 = (bf16[32,1536]{1,0:T(8,128)(2,1)S(1)}, bf16[32,1536]{1,0:T(8,128)(2,1)S(1)}, u32[]{:S(2)}, u32[]{:S(2)}) collective-permute-start(bf16[32,1536]{1,0:T(8,128)(2,1)S(1)} %get-tuple-element.38), channel_id=1, source_target_pairs={{0,5},{1,4},{2,7},{3,6},{4,1},{5,0},{6,3},{7,2},{8,13},{9,12},{10,... | collective-permute-start | bytes 294920 | tf_op jit(solution)/shard_map/ppermute | solution.py:280
  31.8 23.5 %collective-permute-start.7 = (bf16[32,1536]{1,0:T(8,128)(2,1)S(1)}, bf16[32,1536]{1,0:T(8,128)(2,1)S(1)}, u32[]{:S(2)}, u32[]{:S(2)}) collective-permute-start(bf16[32,1536]{1,0:T(8,128)(2,1)S(1)} %get-tuple-element.39), channel_id=1, source_target_pairs={{0,4},{1,5},{2,6},{3,7},{4,0},{5,1},{6,2},{7,3},{8,12},{9,13},{10,... | collective-permute-start | bytes 294920 | tf_op jit(solution)/shard_map/ppermute | solution.py:280
  35.9 19.3 %collective-permute-start.8 = (bf16[32,1536]{1,0:T(8,128)(2,1)S(1)}, bf16[32,1536]{1,0:T(8,128)(2,1)S(1)}, u32[]{:S(2)}, u32[]{:S(2)}) collective-permute-start(bf16[32,1536]{1,0:T(8,128)(2,1)S(1)} %get-tuple-element.40), channel_id=1, source_target_pairs={{0,3},{1,2},{2,1},{3,0},{4,7},{5,6},{6,5},{7,4},{8,11},{9,10},{10,... | collective-permute-start | bytes 294920 | tf_op jit(solution)/shard_map/ppermute | solution.py:280
